TPU v7x, 128 devices: a whole 4x4x4 slice. The times are simulated.
128 devices in a mesh: ctx: 32 (over x, y, core), vocab: 4 (over z).
Axes of the slice: x: 4, y: 4, z: 4, core: 2. Of those that a mesh axis runs over, the one named last changes fastest.
Arguments:
- query_rows: bfloat16 [8192, 4096], P('ctx', 'vocab'), may hold values from -12 to 12
- key_rows: bfloat16 [8192, 2048], P('ctx', 'vocab'), may hold values from -6 to 6
- value_rows: bfloat16 [8192, 2048], P('ctx', 'vocab'), may hold values from -6 to 6
- residual: bfloat16 [8192, 4608], P('ctx', 'vocab'), may hold values from -6 to 6
- out_weight: bfloat16 [4096, 4608], P('vocab'), may hold values from -0.09375 to 0.09375
- post_gain: float32 [4608], P('vocab'), may hold values from 0.1 to 1.9
- final_gain: float32 [4608], P('vocab'), may hold values from 0.1 to 1.9
- embedding: bfloat16 [131072, 4608], P(('ctx', 'vocab')), may hold values from -0.25 to 0.25
- targets: int32 [256], P('ctx'), may hold values from 0 to 131071
- loss_mask: int32 [256], P('ctx'), may hold values 0 or 1
- pick_pos: int32 [256], P('ctx'), may hold values from 0 to 255, as said below
Outputs:
- final_hidden: bfloat16 [8192, 4608], P('ctx', 'vocab')
- mean_loss: float32 [], replicated
- grad_normed: float32 [256, 4608], P('ctx', 'vocab')
Inputs may be any that keep to these rules, and one draw needn't show every extreme that they name: `pick_pos`: entry k is a position inside the block of 256 tokens held by index k // 8 of ctx; entries may repeat.
All inputs are finite; a program needn't handle non-finite values. No bound on the sum of `loss_mask` on one device may be relied on, other than what follows from the above.
Results may differ from a plain program's by a relative error of at most 0.0049.
Values may be sent and summed in bfloat16 or wider, within the bound.
No kernel may reach another device: no remote copies, remote signals or barrier semaphores. Data moves between devices by JAX's collectives and lax.ppermute only.
A program may use at most 256 MiB of HBM per device.

v0:
```python
import functools

import jax
import jax.numpy as jnp
from jax import lax
from jax.sharding import Mesh
from jax.sharding import PartitionSpec as P

D = 4608
HEADS = 32
KV_HEADS = 16
HEAD_DIM = 128
WINDOW = 4096
CTX = ("ctx_0", "ctx_1", "ctx_2")
CTX_VOCAB = ("ctx_0", "ctx_1", "ctx_2", "vocab")


attn_cap = 50.0
logit_cap = 30.0
query_scalar = 144.0
epsilon = 1e-06


def in_blocks(shard, dim, peers):
    dims = shard.shape
    pieces = shard.reshape(*dims[:dim], peers, dims[dim] // peers, *dims[dim + 1 :])
    return jnp.moveaxis(pieces, dim, 0)


def sent_and_summed(shard, axis, dim):
    peers = lax.axis_size(axis)
    pieces = lax.all_to_all(in_blocks(shard, dim, peers), axis, 0, 0, tiled=True)
    return jnp.sum(pieces, axis=0)


def copy_for_each(shard, axis):
    peers = lax.axis_size(axis)
    return lax.all_to_all(
        jnp.broadcast_to(shard[None], (peers, *shard.shape)), axis, 0, 0, tiled=True
    )


def taken_together(shard, axis):
    return copy_for_each(shard, axis).sum(axis=0)


def laid_out(pieces, dim):
    dims = list(pieces.shape[1:])
    dims[dim] *= pieces.shape[0]
    return jnp.moveaxis(pieces, 0, dim).reshape(dims)


def collect(shard, axis, dim):
    pieces = copy_for_each(shard, axis)
    return laid_out(pieces, dim)


def rows_first(arrays, axis, dims):
    turned = [jnp.moveaxis(a, dim, 0) for a, dim in zip(arrays, dims)]
    widths = [t[0].size for t in turned]
    both = jnp.concatenate([t.reshape(-1, w) for t, w in zip(turned, widths)], axis=1)
    whole = lax.all_gather(both, axis, axis=0, tiled=True)
    pieces = jnp.split(whole, [sum(widths[:k]) for k in range(1, len(widths))], axis=1)
    return tuple(
        (
            jnp.moveaxis(b.reshape(-1, *t.shape[1:]), 0, dim)
            for b, t, dim in zip(pieces, turned, dims)
        )
    )


def by_axis(shard, axes):
    return functools.reduce(lax.psum, axes, shard)


def attend(key_value, query_grp, query_pos):
    piece_len = key_value.shape[1]
    kv_local = query_grp.shape[1]
    key_piece = key_value[0].reshape(piece_len, kv_local, HEAD_DIM)
    value_piece = key_value[1].reshape(piece_len, kv_local, HEAD_DIM)
    raw_scores = jnp.einsum(
        "tgcd,sgd->gcts", query_grp, key_piece, preferred_element_type=jnp.float32
    )
    capped = attn_cap * jnp.tanh(raw_scores * query_scalar ** (-0.5) / attn_cap)
    key_pos = jnp.arange(piece_len, dtype=jnp.int32)
    distance = query_pos[:, None] - key_pos[None, :]
    allowed = (distance >= 0) & (distance < WINDOW) & (key_pos[None, :] >= 0)
    weights = jnp.where(allowed, jnp.exp(capped), 0.0)
    acc_weights = jnp.sum(weights, axis=-1)
    acc_values = jnp.einsum(
        "gcts,sgd->gctd",
        weights.astype(jnp.bfloat16),
        value_piece,
        preferred_element_type=jnp.float32,
    )
    return (acc_values, acc_weights)


def shards(
    query_rows,
    key_rows,
    value_rows,
    residual,
    out_weight,
    post_gain,
    final_gain,
    embedding,
    targets,
    loss_mask,
    pick_pos,
):
    local_len = query_rows.shape[0]
    group_size = HEADS // KV_HEADS
    kv_local = key_rows.shape[1] // HEAD_DIM
    ctx_index = lax.axis_index(CTX)
    query_grp = query_rows.reshape(local_len, kv_local, group_size, HEAD_DIM)
    query_pos = ctx_index * local_len + jnp.arange(local_len, dtype=jnp.int32)
    key_value = jnp.stack((key_rows, value_rows))
    initial = (
        jnp.zeros((kv_local, group_size, local_len, HEAD_DIM), jnp.float32),
        jnp.zeros((kv_local, group_size, local_len), jnp.float32),
    )
    first_query = ctx_index * local_len
    last_query = first_query + local_len - 1
    piece = lax.all_gather(key_value, CTX, axis=1, tiled=True)
    offset = jnp.int32(0)
    piece_len = piece.shape[1]
    needed = (offset <= last_query) & (offset + piece_len - 1 > first_query - WINDOW)

    def work(state_now):
        return attend(piece, query_grp, query_pos)

    def skip(state_now):
        return state_now

    acc_values, acc_weights = lax.cond(needed, work, skip, initial)
    attended = acc_values / acc_weights[..., None]
    attended = jnp.transpose(attended, (2, 0, 1, 3)).reshape(
        local_len, kv_local * group_size * HEAD_DIM
    )
    attended = attended.astype(jnp.bfloat16)
    partial_proj = jnp.dot(attended, out_weight, preferred_element_type=jnp.float32)
    own_cols = sent_and_summed(partial_proj, "vocab", 1)
    square_sum = taken_together(jnp.sum(own_cols * own_cols, axis=1, keepdims=True), "vocab")
    inv_rms = lax.rsqrt(square_sum / D + epsilon)
    final_hidden = (residual.astype(jnp.float32) + own_cols * inv_rms * post_gain).astype(
        jnp.bfloat16
    )
    picked = jnp.take(final_hidden, pick_pos, axis=0).astype(jnp.float32)
    picked_sum = taken_together(jnp.sum(picked * picked, axis=1, keepdims=True), "vocab")
    normed = (picked * lax.rsqrt(picked_sum / D + epsilon) * final_gain).astype(jnp.bfloat16)
    normed_full = collect(normed, "vocab", 1)
    all_targets, all_mask = rows_first((targets, loss_mask), CTX, (0, 0))
    raw_logits = jnp.einsum(
        "td,vd->tv", collect(normed_full, CTX, 0), embedding, preferred_element_type=jnp.float32
    )
    logits = logit_cap * jnp.tanh(raw_logits / logit_cap)
    vocab_local = embedding.shape[0]
    vocab_base = (ctx_index * lax.axis_size("vocab") + lax.axis_index("vocab")) * vocab_local
    onehot = (vocab_base + jnp.arange(vocab_local, dtype=jnp.int32))[None, :] == all_targets[
        :, None
    ]
    exp_logits = jnp.exp(logits)
    local_total = jnp.sum(exp_logits, axis=1)
    local_target = jnp.sum(jnp.where(onehot, logits, 0.0), axis=1)
    totals, target_logit = (by_axis(local_total, CTX_VOCAB), by_axis(local_target, CTX_VOCAB))
    mask_float = all_mask.astype(jnp.float32)
    mean_loss = jnp.sum(mask_float * (jnp.log(totals) - target_logit)) / all_targets.shape[0]
    dlogits = mask_float[:, None] * (exp_logits / totals[:, None] - onehot.astype(jnp.float32))
    dlogits = (dlogits * (1.0 - (logits / logit_cap) ** 2)).astype(jnp.bfloat16)
    partial_grad = jnp.dot(dlogits, embedding, preferred_element_type=jnp.float32)
    by_features = sent_and_summed(partial_grad, "vocab", 1)
    grad_normed = sent_and_summed(by_features, CTX, 0)
    return (final_hidden, mean_loss, grad_normed)


def solution(mesh):
    split = Mesh(
        mesh.devices.reshape(4, 4, 2, mesh.shape["vocab"]), ("ctx_0", "ctx_1", "ctx_2", "vocab")
    )
    return jax.shard_map(
        shards,
        mesh=split,
        in_specs=(
            P(CTX, "vocab"),
            P(CTX, "vocab"),
            P(CTX, "vocab"),
            P(CTX, "vocab"),
            P("vocab", None),
            P("vocab"),
            P("vocab"),
            P(CTX_VOCAB, None),
            P(CTX),
            P(CTX),
            P(CTX),
        ),
        out_specs=(P(CTX, "vocab"), P(), P(CTX, "vocab")),
        check_vma=False,
    )
```

profile of v0, /device:TPU:1, one launch (start us, length us, event | category | flops | bytes accessed | tf_op | source)
XLA Modules:
  0.0 458.3 jit_solution(8563444499660979032)
XLA Ops:
  10.3 12.7 %copy.59 = bf16[4608,1024]{1,0:T(8,128)(2,1)} copy(bf16[4608,1024]{0,1:T(8,128)(2,1)} %bitcast.63) | data formatting | bytes 18874368 | tf_op jit(solution)/shard_map/dot_general | solution.py:142
  23.0 71.2 %all-gather.3.cloned.1.call-done = bf16[2,8192,512]{1,2,0:T(8,128)(2,1)} async-done(((bf16[2,256,512]{1,2,0:T(8,128)(2,1)}), bf16[2,8192,512]{1,2,0:T(8,128)(2,1)}) %all-gather.3.cloned.1.call-update) | async-done | bytes 16777232 | tf_op jit(solution)/shard_map/all_gather | solution.py:125
  94.2 74.6 %conditional.1 = (f32[4,2,256]{2,1,0:T(2,128)S(1)}, f32[4,2,256,128]{2,3,1,0:T(8,128)S(1)}) conditional(s32[]{:T(128)} %convert_element_type.49, () %tuple.16, (s32[]{:T(128)}, s32[256]{0:T(256)S(1)}, bf16[2,8192,512]{1,2,0:T(8,128)(2,1)}, bf16[256,1024]{1,0:T(8,128)(2,1)}) %tuple.17), branch_computations={%region_0.0_spmd, %region_1.3_spmd} | conditional | flops 8732538880 | bytes 195570736 | solution.py:136
  94.2 11.7 %fusion.39 = (bf16[1,8192,512]{1,2,0:T(8,128)(2,1)}, bf16[1,8192,512]{1,2,0:T(8,128)(2,1)}) fusion(bf16[2,8192,512]{1,2,0:T(8,128)(2,1)} %get-tuple-element.13), kind=kLoop, calls=%fused_computation.58 | loop fusion | bytes 33554432 | tf_op jit(solution)/shard_map/cond/branch_1_fun/slice | solution.py:80
  108.4 30.4 %fusion = (f32[4,2,256]{2,1,0:T(2,128)S(1)}, f32[4,8192,256,2]{2,1,3,0:T(8,128)}) fusion(pred[256,8192]{0,1:T(8,128)(4,1)S(1)} %fusion.7, bf16[8192,4,128,1]{0,2,3,1:T(8,128)(2,1)} %bitcast.66, bf16[256,4,2,128]{3,2,1,0:T(2,128)(2,1)S(1)} %reshape.107), kind=kOutput, calls=%fused_computation.2 | convolution fusion | flops 4362074112 | bytes 78127104 | tf_op jit(solution)/shard_map/cond/branch_1_fun/tgcd,sgd->gcts/dot_general | solution.py:81
  138.8 30.0 %fusion.2 = f32[4,2,256,128]{2,3,1,0:T(8,128)S(1)} fusion(bf16[8192,4,128,1]{0,2,3,1:T(8,128)(2,1)} %bitcast.65, f32[4,8192,256,2]{2,1,3,0:T(8,128)} %get-tuple-element.38, pred[256,8192]{0,1:T(8,128)(4,1)S(1)} %fusion.7), kind=kOutput, calls=%fused_computation.4 | convolution fusion | flops 4362076160 | bytes 78643200 | tf_op jit(solution)/shard_map/cond | solution.py:136
  168.9 11.6 %convolution_bitcast_fusion = f32[4,256,1152]{2,1,0:T(8,128)} fusion(bf16[256,1024,1]{0,1,2:T(8,128)(2,1)S(1)} %bitcast.70, bf16[4,1152,1024]{2,1,0:T(8,128)(2,1)} %bitcast.64), kind=kOutput, calls=%fused_computation.17 | convolution fusion | flops 2415919104 | bytes 14680064 | tf_op jit(solution)/shard_map/dot_general | solution.py:142
  180.5 5.1 %all-to-all-start = ((f32[4,256,1152]{2,1,0:T(8,128)}), f32[4,256,1152]{2,1,0:T(8,128)}, u32[]{:S(2)}, u32[]{:S(2)}) async-start(f32[4,256,1152]{2,1,0:T(8,128)} %convolution_bitcast_fusion), calls=%async_computation | async-start | bytes 9437184 | tf_op jit(solution)/shard_map/all_to_all | solution.py:32
  185.7 54.3 %all-to-all-done = f32[4,256,1152]{2,1,0:T(8,128)} async-done(((f32[4,256,1152]{2,1,0:T(8,128)}), f32[4,256,1152]{2,1,0:T(8,128)}, u32[]{:S(2)}, u32[]{:S(2)}) %all-to-all-start) | async-done | bytes 4718624 | tf_op jit(solution)/shard_map/all_to_all | solution.py:32
  246.7 4.1 all-to-all-done.1
  251.9 6.5 %all_to_all.35 = f32[4,8,1]{1,2,0:T(1,128)S(1)} all-to-all(f32[4,8,1]{1,2,0:T(1,128)S(1)} %broadcast_in_dim.66), channel_id=1, replica_groups=mesh['ctx_0'=4,'ctx_1'=4,'ctx_2'=2,'vocab'=4] {'vocab'}, dimensions={0} | all-to-all | bytes 256 | tf_op jit(solution)/shard_map/all_to_all | solution.py:38
  258.5 6.9 %all_to_all.36 = bf16[4,8,1152]{2,1,0:T(8,128)(2,1)S(1)} all-to-all(bf16[4,8,1152]{2,1,0:T(8,128)(2,1)S(1)} %broadcast_in_dim.67), channel_id=1, replica_groups=mesh['ctx_0'=4,'ctx_1'=4,'ctx_2'=2,'vocab'=4] {'vocab'}, dimensions={0} | all-to-all | bytes 147456 | tf_op jit(solution)/shard_map/all_to_all | solution.py:38
  266.9 10.4 %all-to-all-start.4 = ((bf16[32,8,4608]{2,1,0:T(8,128)(2,1)}), bf16[32,8,4608]{2,1,0:T(8,128)(2,1)S(1)}, u32[]{:S(2)}, u32[]{:S(2)}) async-start(bf16[32,8,4608]{2,1,0:T(8,128)(2,1)} %broadcast_in_dim.69), calls=%async_computation.4 | async-start | bytes 4718592 | tf_op jit(solution)/shard_map/all_to_all | solution.py:38
  277.4 46.1 %all-gather = s32[32,8,2]{1,2,0:T(2,128)S(1)} all-gather(s32[1,8,2]{1,2,0:T(2,128)S(1)} %add_bitcast_fusion), channel_id=1, replica_groups=mesh['ctx_0'=4,'ctx_1'=4,'ctx_2'=2,'vocab'=4] {'ctx_0','ctx_1','ctx_2'}, dimensions={0}, use_global_device_ids=true | all-gather | bytes 2112 | tf_op jit(solution)/shard_map/all_gather | solution.py:62
  323.6 7.4 %exponential_reduce_fusion = (f32[256]{0:T(256)S(1)}, f32[256]{0:T(256)S(1)}, f32[256,1024]{1,0:T(8,128)}) fusion(s32[256]{0:T(256)S(1)} %bitcast.74, s32[1024]{0:T(1024)S(1)} %iota_add_fusion, bf16[1024,4608]{1,0:T(8,128)(2,1)} %param.20, bf16[32,8,4608]{2,1,0:T(8,128)(2,1)S(1)} %all-to-all-done.4), kind=kOutput, calls=%fused_computation.32 | convolution fusion | flops 2417491456 | bytes 12852224 | tf_op jit(solution)/shard_map/td,vd->tv/dot_general | solution.py:154
  331.0 6.5 %all-reduce.2 = (f32[256]{0:T(256)S(1)}, f32[256]{0:T(256)S(1)}) all-reduce(f32[256]{0:T(256)S(1)} %get-tuple-element.26, f32[256]{0:T(256)S(1)} %get-tuple-element.25), channel_id=1, replica_groups=mesh['ctx_0'=4,'ctx_1'=4,'ctx_2'=2,'vocab'=4] {'ctx_0'}, use_global_device_ids=true, to_apply=%region_14.15 | all-reduce | flops 512 | bytes 4096 | tf_op jit(solution)/shard_map/psum | solution.py:73
  337.5 7.9 %all-reduce.1 = (f32[256]{0:T(256)S(1)}, f32[256]{0:T(256)S(1)}) all-reduce(f32[256]{0:T(256)S(1)} %get-tuple-element.31, f32[256]{0:T(256)S(1)} %get-tuple-element.32), channel_id=1, replica_groups=mesh['ctx_0'=4,'ctx_1'=4,'ctx_2'=2,'vocab'=4] {'ctx_1'}, use_global_device_ids=true, to_apply=%region_15.16 | all-reduce | flops 512 | bytes 4096 | tf_op jit(solution)/shard_map/psum | solution.py:73
  345.4 6.3 %all-reduce.3 = (f32[256]{0:T(256)S(1)}, f32[256]{0:T(256)S(1)}) all-reduce(f32[256]{0:T(256)S(1)} %get-tuple-element.29, f32[256]{0:T(256)S(1)} %get-tuple-element.30), channel_id=1, replica_groups=mesh['ctx_0'=4,'ctx_1'=4,'ctx_2'=2,'vocab'=4] {'ctx_2'}, use_global_device_ids=true, to_apply=%region_16.17 | all-reduce | flops 512 | bytes 4096 | tf_op jit(solution)/shard_map/psum | solution.py:73
  351.7 6.8 %all-reduce = (f32[256]{0:T(256)S(1)}, f32[256]{0:T(256)S(1)}) all-reduce(f32[256]{0:T(256)S(1)} %get-tuple-element.33, f32[256]{0:T(256)S(1)} %get-tuple-element.34), channel_id=1, replica_groups=mesh['ctx_0'=4,'ctx_1'=4,'ctx_2'=2,'vocab'=4] {'vocab'}, use_global_device_ids=true, to_apply=%region_17.18 | all-reduce | flops 512 | bytes 4096 | tf_op jit(solution)/shard_map/psum | solution.py:73
  358.6 6.2 %fusion.26 = f32[256,4608]{1,0:T(8,128)S(1)} fusion(bf16[1024,4608]{1,0:T(8,128)(2,1)} %param.20, f32[256,1024]{1,0:T(8,128)} %get-tuple-element.41, f32[256]{0:T(256)S(1)} %get-tuple-element.28, f32[256]{0:T(256)S(1)} %bitcast.72, s32[1024]{0:T(1024)S(1)} %iota_add_fusion, s32[256]{0:T(256)S(1)} %bitcast.75), kind=kOutput, calls=%fused_computation.33 | convolution fusion | flops 2418540544 | bytes 15211520 | tf_op jit(solution)/shard_map/dot_general | solution.py:171
  365.0 55.6 %all_to_all.37 = f32[4,256,1152]{2,1,0:T(8,128)} all-to-all(f32[4,256,1152]{2,1,0:T(8,128)S(1)} %bitcast.62), channel_id=1, replica_groups=mesh['ctx_0'=4,'ctx_1'=4,'ctx_2'=2,'vocab'=4] {'vocab'}, dimensions={0} | all-to-all | bytes 9437184 | tf_op jit(solution)/shard_map/all_to_all | solution.py:32
  420.6 3.8 reduce_sum.107
  424.4 6.8 %all-to-all-start.6 = ((f32[32,8,1152]{2,1,0:T(8,128)}), f32[32,8,1152]{2,1,0:T(8,128)S(1)}, u32[]{:S(2)}, u32[]{:S(2)}) async-start(f32[32,8,1152]{2,1,0:T(8,128)} %bitcast.22), calls=%async_computation.6 | async-start | bytes 2359296 | tf_op jit(solution)/shard_map/all_to_all | solution.py:32
  432.5 17.2 %all-to-all-done.6 = f32[32,8,1152]{2,1,0:T(8,128)S(1)} async-done(((f32[32,8,1152]{2,1,0:T(8,128)}), f32[32,8,1152]{2,1,0:T(8,128)S(1)}, u32[]{:S(2)}, u32[]{:S(2)}) %all-to-all-start.6) | async-done | bytes 1179680 | tf_op jit(solution)/shard_map/all_to_all | solution.py:32
  (53 shorter events, 17.0 us)
Async XLA Ops:
  7.2 87.0 %all-gather.3.cloned.1.call-start = ((), (), s32[]{:S(2)}) async-start(), calls=%async_computation.7 | async-start | bytes 17301504 | tf_op jit(solution)/shard_map/all_gather | solution.py:125
  94.2 13.9 %copy-start.2 = (bf16[256,1024]{1,0:T(8,128)(2,1)S(1)}, bf16[256,1024]{1,0:T(8,128)(2,1)}, u32[]{:S(2)}) copy-start(bf16[256,1024]{1,0:T(8,128)(2,1)} %get-tuple-element.23) | copy-start | bytes 1572868 | tf_op jit(solution)/shard_map/cond
  180.5 5.1 %copy-start.7 = (s32[8]{0:T(128)S(1)}, s32[8]{0:T(128)}, u32[]{:S(2)}) copy-start(s32[8]{0:T(128)} %param.23) | copy-start | bytes 100
  180.5 70.3 %copy-start.1 = (bf16[256,1152]{1,0:T(8,128)(2,1)S(1)}, bf16[256,1152]{1,0:T(8,128)(2,1)}, u32[]{:S(2)}) copy-start(bf16[256,1152]{1,0:T(8,128)(2,1)} %param.16) | copy-start | bytes 1769476
  180.5 70.3 %copy-start.3 = (f32[1152]{0:T(1024)S(1)}, f32[1152]{0:T(1024)}, u32[]{:S(2)}) copy-start(f32[1152]{0:T(1024)} %param.18) | copy-start | bytes 13828
  180.5 77.9 %copy-start.4 = (f32[1152]{0:T(1024)S(1)}, f32[1152]{0:T(1024)}, u32[]{:S(2)}) copy-start(f32[1152]{0:T(1024)} %param.19) | copy-start | bytes 13828
  180.5 59.4 %all-to-all-start = ((f32[4,256,1152]{2,1,0:T(8,128)}), f32[4,256,1152]{2,1,0:T(8,128)}, u32[]{:S(2)}, u32[]{:S(2)}) async-start(f32[4,256,1152]{2,1,0:T(8,128)} %convolution_bitcast_fusion), calls=%async_computation | async-start | bytes 9437184 | tf_op jit(solution)/shard_map/all_to_all | solution.py:32
  185.7 91.7 %copy-start.5 = (s32[8]{0:T(128)S(1)}, s32[8]{0:T(128)}, u32[]{:S(2)}) copy-start(s32[8]{0:T(128)} %param.22) | copy-start | bytes 100
  185.7 91.7 %copy-start.6 = (s32[8]{0:T(128)S(1)}, s32[8]{0:T(128)}, u32[]{:S(2)}) copy-start(s32[8]{0:T(128)} %param.21) | copy-start | bytes 100
  243.4 7.4 %all-to-all-start.1 = ((f32[4,256,1]{1,2,0:T(1,128)}), f32[4,256,1]{1,2,0:T(1,128)S(1)}, u32[]{:S(2)}, u32[]{:S(2)}) async-start(f32[4,256,1]{1,2,0:T(1,128)} %broadcast_in_dim.62), calls=%async_computation.1 | async-start | bytes 8192 | tf_op jit(solution)/shard_map/all_to_all | solution.py:38
  251.1 79.9 %copy-start = (bf16[256,1152]{1,0:T(8,128)(2,1)}, bf16[256,1152]{1,0:T(8,128)(2,1)S(1)}, u32[]{:S(2)}) copy-start(bf16[256,1152]{1,0:T(8,128)(2,1)S(1)} %add_convert_fusion) | copy-start | bytes 1769476
  266.9 56.6 %all-to-all-start.4 = ((bf16[32,8,4608]{2,1,0:T(8,128)(2,1)}), bf16[32,8,4608]{2,1,0:T(8,128)(2,1)S(1)}, u32[]{:S(2)}, u32[]{:S(2)}) async-start(bf16[32,8,4608]{2,1,0:T(8,128)(2,1)} %broadcast_in_dim.69), calls=%async_computation.4 | async-start | bytes 4718592 | tf_op jit(solution)/shard_map/all_to_all | solution.py:38
  424.4 25.3 %all-to-all-start.6 = ((f32[32,8,1152]{2,1,0:T(8,128)}), f32[32,8,1152]{2,1,0:T(8,128)S(1)}, u32[]{:S(2)}, u32[]{:S(2)}) async-start(f32[32,8,1152]{2,1,0:T(8,128)} %bitcast.22), calls=%async_computation.6 | async-start | bytes 2359296 | tf_op jit(solution)/shard_map/all_to_all | solution.py:32
Sparse Core Ops, SparseCore 0:
  10.7 83.3 all-gather.2
where the time goes:
time: 460 us; the launch traced here: 458 us
  waiting for transfers between devices  147 us (32%)
  blocking collectives  143 us (31%)
  matrix products  85.5 us (19%)
  local copies, waits for them, and re-layouts  30.1 us (7%)
  starting transfers between devices  25.6 us (6%)
  between operations  16.1 us (4%)
  other arithmetic  11.7 us (3%)
    all_to_all x2, waiting for transfers between devices, sent_and_summed(): lax.all_to_all(in_blocks(shard, dim, peers), axis, 0, 0, tiled=True)  71.4 us
    all_gather x1, waiting for transfers between devices, shards(): piece = lax.all_gather(key_value, CTX, axis=1, tiled=True)  71.2 us
    all_to_all x1, blocking collectives, sent_and_summed(): lax.all_to_all(in_blocks(shard, dim, peers), axis, 0, 0, tiled=True)  55.6 us
    all_gather x1, blocking collectives, rows_first(): whole = lax.all_gather(both, axis, axis=0, tiled=True)  46.1 us
    dot_general x1, matrix products, attend(): jnp.einsum('tgcd,sgd->gcts', query_grp, key_piece, preferred_element_type...  30.4 us
    cond x1, matrix products, shards(): acc_values, acc_weights = lax.cond(needed, work, skip, initial)  30 us
    psum x4, blocking collectives, by_axis(): return functools.reduce(lax.psum, axes, shard)  27.5 us
    all_to_all x2, starting transfers between devices, copy_for_each(): lax.all_to_all(jnp.broadcast_to(shard[None], (peers, *shard.shape)), axis...  13.7 us
  transfers between devices with their start and end apart: 5, of which 4 were waited for; matrix products, arithmetic and copies ran while one was open for 3% of the time, Pallas kernels for 0%

commit v1 on v0

v1 whole, which is shorter than its diff:
```python
import functools

import jax
import jax.numpy as jnp
from jax import lax
from jax.experimental import pallas as pl
from jax.experimental.pallas import tpu as pltpu
from jax.sharding import Mesh
from jax.sharding import PartitionSpec as P

D = 4608
HEAD_DIM = 128
TOKENS = 8192
PICK = 8
SPAN = 512
BLK = 256
COLS = 1152
EXT = 128
LOSS_TOKENS = 256
CTX = ("x", "y", "core")

attn_cap = 50.0
logit_cap = 30.0
query_scalar = 144.0
epsilon = 1e-06

f32 = jnp.float32
bf16 = jnp.bfloat16


def ring(k):
    return [(j, (j + k) % 4) for j in range(4)]


SWAP = [(0, 1), (1, 0)]


def exchange(pieces, axes):
    return lax.all_to_all(pieces, axes, 0, 0, tiled=True)


def scores(q, k):
    return lax.dot_general(q, k, (((1,), (1,)), ((), ())), preferred_element_type=f32)


def weigh(raw):
    return jnp.exp(attn_cap * jnp.tanh(raw * (query_scalar**-0.5 / attn_cap)))


def lane_sums(p):
    parts = [p[:, i : i + 128] for i in range(0, p.shape[1], 128)]
    return functools.reduce(jnp.add, parts)


def load_kv(sc_ref, a_ref, b_ref, buf, sem):
    core = sc_ref[0]
    one = pltpu.make_async_copy(a_ref, buf.at[core], sem.at[0])
    two = pltpu.make_async_copy(b_ref, buf.at[1 - core], sem.at[1])
    one.start()
    two.start()
    one.wait()
    two.wait()


def add_full(q_ref, buf, acc_ref, first, rows, span):
    q = q_ref[0, rows, :]
    k = buf[0, pl.ds(first, span), :]
    v = buf[1, pl.ds(first, span), :]
    p = weigh(scores(q, k))
    acc_ref[0, rows, HEAD_DIM:] += lane_sums(p)
    acc_ref[0, rows, :HEAD_DIM] += jnp.dot(p.astype(bf16), v, preferred_element_type=f32)


def attn_own_kernel(sc_ref, q_ref, a_ref, b_ref, acc_ref, buf, sem):
    i = pl.program_id(0)

    @pl.when(i == 0)
    def _():
        load_kv(sc_ref, a_ref, b_ref, buf, sem)

    has_edge = i >= 2
    edge0 = jnp.maximum(i - 2, 0) * SPAN
    diag0 = i * SPAN
    tq = lax.broadcasted_iota(jnp.int32, (BLK, BLK), 0)
    tk = lax.broadcasted_iota(jnp.int32, (BLK, BLK), 1)
    causal = tk <= tq
    beyond = jnp.logical_and(jnp.logical_not(causal), has_edge)
    for r in range(2):
        rows = pl.ds(r * BLK, BLK)
        q = q_ref[0, rows, :]
        kd = buf[0, pl.ds(diag0 + r * BLK, BLK), :]
        ke = buf[0, pl.ds(edge0 + r * BLK, BLK), :]
        vd = buf[1, pl.ds(diag0 + r * BLK, BLK), :]
        ve = buf[1, pl.ds(edge0 + r * BLK, BLK), :]
        p = weigh(jnp.where(causal, scores(q, kd), scores(q, ke)))
        pd = jnp.where(causal, p, 0.0)
        pe = jnp.where(beyond, p, 0.0)
        acc_ref[0, rows, HEAD_DIM:] = lane_sums(pd) + lane_sums(pe)
        acc_ref[0, rows, :HEAD_DIM] = jnp.dot(
            pd.astype(bf16), vd, preferred_element_type=f32
        ) + jnp.dot(pe.astype(bf16), ve, preferred_element_type=f32)
    add_full(q_ref, buf, acc_ref, diag0, pl.ds(BLK, BLK), BLK)

    @pl.when(has_edge)
    def _():
        add_full(q_ref, buf, acc_ref, edge0 + BLK, pl.ds(0, BLK), BLK)

    @pl.when(i >= 1)
    def _():
        for r in range(2):
            add_full(q_ref, buf, acc_ref, (i - 1) * SPAN, pl.ds(r * BLK, BLK), SPAN)


def attn_more_kernel(last, sc_ref, q_ref, a_ref, b_ref, in_ref, out_ref, buf, sem, *scr):
    i = pl.program_id(0)
    acc_ref = scr[0] if last else out_ref

    @pl.when(i == 0)
    def _():
        load_kv(sc_ref, a_ref, b_ref, buf, sem)

    acc_ref[...] = in_ref[...]
    for step in range(2):
        at = i - sc_ref[1] - step

        @pl.when(at >= 0)
        def _():
            for r in range(2):
                add_full(q_ref, buf, acc_ref, at * SPAN, pl.ds(r * BLK, BLK), SPAN)

    if last:
        whole = jnp.sum(acc_ref[0, :, HEAD_DIM:], axis=1, keepdims=True)
        done = (acc_ref[0, :, :HEAD_DIM] / whole).astype(bf16)
        for z in range(4):
            out_ref[z, 0] = done


def attn_call(scalars, q, a, b, acc=None, last=False):
    q_spec = pl.BlockSpec((1, SPAN, HEAD_DIM), lambda i, sc: (i, 0, 0))
    acc_spec = pl.BlockSpec((1, SPAN, 2 * HEAD_DIM), lambda i, sc: (i, 0, 0))
    hbm = pl.BlockSpec(memory_space=pl.ANY)
    scratch = [pltpu.VMEM((2, 4 * SPAN, HEAD_DIM), bf16), pltpu.SemaphoreType.DMA((2,))]
    out_spec, out_shape = acc_spec, jax.ShapeDtypeStruct((4, SPAN, 2 * HEAD_DIM), f32)
    in_specs, args = [q_spec, hbm, hbm], [q, a, b]
    kernel = attn_own_kernel
    if acc is not None:
        in_specs, args = in_specs + [acc_spec], args + [acc]
        kernel = functools.partial(attn_more_kernel, last)
    if last:
        out_spec = pl.BlockSpec((4, 1, SPAN, HEAD_DIM), lambda i, sc: (0, i, 0, 0))
        out_shape = jax.ShapeDtypeStruct((4, 4, SPAN, HEAD_DIM), bf16)
        scratch = scratch + [pltpu.VMEM((1, SPAN, 2 * HEAD_DIM), f32)]
    return pl.pallas_call(
        kernel,
        out_shape=out_shape,
        grid_spec=pltpu.PrefetchScalarGridSpec(
            num_scalar_prefetch=1,
            grid=(4,),
            in_specs=in_specs,
            out_specs=out_spec,
            scratch_shapes=scratch,
        ),
        compiler_params=pltpu.CompilerParams(dimension_semantics=("arbitrary",)),
    )(scalars, *args)


def proj_kernel(
    sc_ref, pick_ref, att_ref, w_ref, a1, a2, a3, b1, b2, b3, rp_ref, pg_ref, fg_ref,
    own_ref, zp_ref, abuf, wbuf, asem, wsem,
):
    zi, ci = sc_ref[0], sc_ref[1]
    heads = [zi * 2, zi * 2 + 1]
    heads += [((zi - s + 4) % 4) * 2 + ci for s in (1, 2, 3)]
    heads += [((zi - s + 4) % 4) * 2 + 1 - ci for s in (1, 2, 3)]
    col = pl.multiple_of(zi * COLS, 128)
    src = [w_ref.at[pl.ds(0, 512), pl.ds(col, COLS)], w_ref.at[pl.ds(512, 512), pl.ds(col, COLS)]]
    src += [a1, a2, a3, b1, b2, b3]
    acopies, wcopies = [], []
    for n in range(8):
        acopies.append(
            pltpu.make_async_copy(att_ref.at[pl.ds(heads[n] * 4, 4)], abuf.at[n], asem.at[n])
        )
        wcopies.append(pltpu.make_async_copy(src[n], wbuf.at[n], wsem.at[n]))
        acopies[n].start()
        wcopies[n].start()
    for n in range(8):
        acopies[n].wait()
        wcopies[n].wait()
        lhs = jnp.concatenate([abuf[n, h] for h in range(4)], axis=1)
        part = jnp.dot(lhs, wbuf[n], preferred_element_type=f32)
        if n == 0:
            own_ref[...] = part
        else:
            own_ref[...] += part
    own = own_ref[...]
    squares = lax.dot_general(
        jnp.ones((8, COLS), f32), own * own, (((1,), (1,)), ((), ())),
        preferred_element_type=f32, precision=lax.Precision.HIGHEST,
    )
    for z in range(4):
        for p in range(PICK):
            zp_ref[z, p : p + 1, :] = own_ref[pl.ds(pick_ref[p], 1), :]
        zp_ref[z, 8:16, :] = rp_ref[...]
        zp_ref[z, 16:17, :] = pg_ref[...]
        zp_ref[z, 17:18, :] = fg_ref[...]
        zp_ref[z, 18:24, :] = jnp.zeros((6, COLS), f32)
        zp_ref[z, 18:19, :LOSS_TOKENS] = squares[:1]


def project(scalars, pick, att, w, parts, res_pick, pg, fg):
    hbm = pl.BlockSpec(memory_space=pl.ANY)
    whole = lambda *dims: pl.BlockSpec(dims, lambda i, *sc: (0,) * len(dims))
    return pl.pallas_call(
        proj_kernel,
        out_shape=(
            jax.ShapeDtypeStruct((BLK, COLS), f32),
            jax.ShapeDtypeStruct((4, 24, COLS), f32),
        ),
        grid_spec=pltpu.PrefetchScalarGridSpec(
            num_scalar_prefetch=2,
            grid=(1,),
            in_specs=[hbm] * 8 + [whole(PICK, COLS), whole(1, COLS), whole(1, COLS)],
            out_specs=(whole(BLK, COLS), whole(4, 24, COLS)),
            scratch_shapes=[
                pltpu.VMEM((8, 4, BLK, HEAD_DIM), bf16),
                pltpu.VMEM((8, 512, COLS), bf16),
                pltpu.SemaphoreType.DMA((8,)),
                pltpu.SemaphoreType.DMA((8,)),
            ],
        ),
        compiler_params=pltpu.CompilerParams(dimension_semantics=("arbitrary",)),
    )(scalars, pick, att, w, *parts, res_pick, pg, fg)


def norm_kernel(zr_ref, ext_ref, out_ref):
    own = [zr_ref[z, :8, :] for z in range(4)]
    total = sum(jnp.sum(o * o, axis=1, keepdims=True) for o in own)
    inv = lax.rsqrt(total / D + epsilon)
    picked = [
        (zr_ref[z, 8:16, :] + own[z] * inv * zr_ref[z, 16:17, :]).astype(bf16).astype(f32)
        for z in range(4)
    ]
    total = sum(jnp.sum(o * o, axis=1, keepdims=True) for o in picked)
    inv = lax.rsqrt(total / D + epsilon)
    for z in range(4):
        normed = (picked[z] * inv * zr_ref[z, 17:18, :]).astype(bf16)
        for n in range(16):
            out_ref[n, :, z * COLS : (z + 1) * COLS] = normed
    for n in range(16):
        out_ref[n, :, D:] = ext_ref[...]


def normalise(zr, ext):
    return pl.pallas_call(
        norm_kernel, out_shape=jax.ShapeDtypeStruct((16, PICK, D + EXT), bf16)
    )(zr, ext)


def loss_kernel(sc_ref, g_ref, s_ref, e_ref, out_ref, row_ref, nbuf, acc):
    j = pl.program_id(0)

    @pl.when(j == 0)
    def _():
        nbuf[:128] = g_ref[...]
        nbuf[128:] = s_ref[...]

    emb = e_ref[...]
    raw = scores(nbuf[:, :D], emb)
    bent = jnp.tanh(raw / logit_cap)
    logits = logit_cap * bent
    big = jnp.exp(logits)
    code = nbuf[:, D:].astype(f32)
    target = code[:, 0:1] * 16384.0 + code[:, 1:2] * 128.0 + code[:, 2:3]
    at = lax.broadcasted_iota(jnp.int32, (LOSS_TOKENS, BLK), 1) + (sc_ref[0] + j * BLK)
    hit = at == target.astype(jnp.int32)
    left = jnp.concatenate(
        [(big * (1.0 - bent * bent)).astype(bf16), jnp.where(hit, 1.0, 0.0).astype(bf16)], axis=0
    )
    ones = jnp.ones((8, BLK), f32)
    row_sum = lambda m: lax.dot_general(
        ones, m, (((1,), (1,)), ((), ())),
        preferred_element_type=f32, precision=lax.Precision.HIGHEST,
    )
    totals = row_sum(big)
    hits = row_sum(jnp.where(hit, logits, 0.0))
    both = jnp.concatenate([totals[:1], hits[:1], jnp.zeros((6, LOSS_TOKENS), f32)], axis=0)

    @pl.when(j == 0)
    def _():
        acc[...] = jnp.dot(left, emb, preferred_element_type=f32)
        row_ref[...] = both

    @pl.when(j > 0)
    def _():
        acc[...] += jnp.dot(left, emb, preferred_element_type=f32)
        row_ref[...] += both

    @pl.when(j == 3)
    def _():
        for h in range(2):
            for z in range(4):
                for part in range(2):
                    out_ref[h, z, :, part * COLS : (part + 1) * COLS] = acc[
                        part * 256 + h * 128 : part * 256 + h * 128 + 128, z * COLS : (z + 1) * COLS
                    ].astype(bf16)


def loss_parts(scalars, g, s, emb):
    whole = lambda *dims: pl.BlockSpec(dims, lambda i, sc: (0,) * len(dims))
    return pl.pallas_call(
        loss_kernel,
        out_shape=(
            jax.ShapeDtypeStruct((2, 4, 128, 2 * COLS), bf16),
            jax.ShapeDtypeStruct((8, LOSS_TOKENS), f32),
        ),
        grid_spec=pltpu.PrefetchScalarGridSpec(
            num_scalar_prefetch=1,
            grid=(4,),
            in_specs=[
                whole(128, D + EXT),
                whole(128, D + EXT),
                pl.BlockSpec((BLK, D), lambda i, sc: (i, 0)),
            ],
            out_specs=(whole(2, 4, 128, 2 * COLS), whole(8, LOSS_TOKENS)),
            scratch_shapes=[
                pltpu.VMEM((LOSS_TOKENS, D + EXT), bf16),
                pltpu.VMEM((2 * LOSS_TOKENS, D), f32),
            ],
        ),
        compiler_params=pltpu.CompilerParams(dimension_semantics=("arbitrary",)),
    )(scalars, g, s, emb)


def shards(
    query_rows, key_rows, value_rows, residual, out_weight, post_gain, final_gain,
    embedding, targets, loss_mask, pick_pos,
):
    xi, yi, ci, zi = (lax.axis_index(a) for a in ("x", "y", "core", "vocab"))
    i32 = lambda *v: jnp.stack([jnp.asarray(e, jnp.int32) for e in v])

    q_heads = query_rows.reshape(BLK, 8, HEAD_DIM).transpose(1, 0, 2)
    k_heads = key_rows.reshape(BLK, 4, HEAD_DIM).transpose(1, 0, 2)
    v_heads = value_rows.reshape(BLK, 4, HEAD_DIM).transpose(1, 0, 2)
    kv = jnp.stack([k_heads, v_heads], axis=1).reshape(8, BLK, HEAD_DIM)
    got = exchange(jnp.concatenate([q_heads, kv], axis=1), ("x", "core"))
    q = got[:, :BLK].reshape(4, SPAN, HEAD_DIM)
    own = got[:, BLK:].reshape(4 * SPAN, HEAD_DIM)

    swap = lambda a: lax.ppermute(a, "core", SWAP)
    down, up, far = (lax.ppermute(own, "y", ring(k)) for k in (1, 3, 2))

    sent = [
        lax.dynamic_slice(out_weight, (ci * 512, ((zi + s) % 4) * COLS), (512, COLS))
        for s in (1, 2, 3)
    ]
    mine = [lax.ppermute(p, "vocab", ring(s)) for p, s in zip(sent, (1, 2, 3))]
    theirs = [swap(p) for p in mine]

    acc = attn_call(i32(ci, 0), q, own, swap(own))
    acc = attn_call(i32(ci, jnp.where(yi >= 1, 0, 1)), q, down, swap(down), acc)
    acc = attn_call(i32(ci, jnp.where(yi == 3, 0, 1)), q, up, swap(up), acc)
    out = attn_call(i32(ci, jnp.where(yi >= 2, 0, 1)), q, far, swap(far), acc, last=True)
    att = exchange(out.reshape(32, BLK, HEAD_DIM), ("vocab", "x", "core"))

    res_pick = jnp.take(residual, pick_pos, axis=0).astype(f32)
    own_cols, zp = project(
        i32(zi, ci), pick_pos, att, out_weight, mine + theirs,
        res_pick, post_gain[None], final_gain[None],
    )
    zr = exchange(zp, "vocab")
    square_sum = jnp.sum(zr[:, 18, :LOSS_TOKENS], axis=0)
    inv_rms = lax.rsqrt(square_sum / D + epsilon)[:, None]
    final_hidden = (residual.astype(f32) + own_cols * inv_rms * post_gain).astype(bf16)

    coded = jnp.stack([targets >> 14, (targets >> 7) & 127, targets & 127, loss_mask], axis=1)
    ext = jnp.pad(coded, ((0, 0), (0, EXT - 4))).astype(bf16)
    g = exchange(normalise(zr, ext), ("x", "y")).reshape(128, D + EXT)
    vocab_local = embedding.shape[0]
    base = (((xi * 4 + yi) * 2 + ci) * 4 + zi) * vocab_local
    parts, rows = loss_parts(i32(base), g, swap(g), embedding)

    summed = (parts[0].astype(f32) + swap(parts[1]).astype(f32)).astype(bf16)
    row = rows[:2, :128] + swap(rows[:2, 128:])
    high = lax.reduce_precision(row, 8, 7)
    low = row - high
    info = jnp.stack([high[0], low[0], high[1], low[1]] + [jnp.zeros((128,), f32)] * 4)
    info = jnp.broadcast_to(info.astype(bf16)[None], (64, 8, 128))
    back = exchange(
        jnp.concatenate([summed.reshape(64, 8, 2 * COLS), info], axis=2), ("vocab", "x", "y")
    ).astype(f32)
    facts = jnp.sum(back[:, :4, 2 * COLS :], axis=0)
    totals, target_logit = facts[0] + facts[1], facts[2] + facts[3]
    masks = g[:, D + 3].astype(f32)
    loss = jnp.sum(masks * (jnp.log(totals) - target_logit)) / LOSS_TOKENS
    loss = loss + lax.ppermute(loss[None], "core", SWAP)[0]

    sums = jnp.sum(back[:, :, : 2 * COLS], axis=0)
    at = (xi * 4 + yi) * PICK
    my_total = lax.dynamic_slice(totals, (at,), (PICK,))[:, None]
    my_logit = lax.dynamic_slice(target_logit, (at,), (PICK,))[:, None]
    slope = 1.0 - (my_logit / logit_cap) ** 2
    grad = loss_mask.astype(f32)[:, None] * (sums[:, :COLS] / my_total - slope * sums[:, COLS:])
    return (final_hidden, loss, grad)


def solution(mesh):
    split = Mesh(
        mesh.devices.reshape(4, 4, 2, mesh.shape["vocab"]), ("x", "y", "core", "vocab")
    )
    return jax.shard_map(
        shards,
        mesh=split,
        in_specs=(
            P(CTX, "vocab"),
            P(CTX, "vocab"),
            P(CTX, "vocab"),
            P(CTX, "vocab"),
            P("vocab", None),
            P("vocab"),
            P("vocab"),
            P((*CTX, "vocab"), None),
            P(CTX),
            P(CTX),
            P(CTX),
        ),
        out_specs=(P(CTX, "vocab"), P(), P(CTX, "vocab")),
        check_vma=False,
    )
```

time: 460 us -> 269 us (0.58)
  blocking collectives: 143 us -> 44.2 us
  matrix products: 85.5 us -> 0 us
  waiting for transfers between devices: 147 us -> 76.7 us
  Pallas kernels: 0 us -> 66.7 us
  starting transfers between devices: 25.6 us -> 42.9 us
  between operations: 16.1 us -> 3.34 us
  local copies, waits for them, and re-layouts: 30.1 us -> 18.5 us
    all_gather x1 -> x0, waiting for transfers between devices: 71.2 us -> none  [shards(): piece = lax.all_gather(key_value, CTX, axis=1, tiled=True)]
    pallas_call x0 -> x7, Pallas kernels: none -> 66.7 us  [the longest x4 34.6 us: attn_call(): pl.pallas_call(kernel, out_shape=out_shape, grid_spec=pltpu.PrefetchScala...]
    dot_general x4 -> x0, matrix products: 55.6 us -> none  [the longest x1 30.4 us: attend(): jnp.einsum('tgcd,sgd->gcts', query_grp, key_piece, preferred_element_type...]
    all_gather x1 -> x0, blocking collectives: 46.1 us -> none  [rows_first(): whole = lax.all_gather(both, axis, axis=0, tiled=True)]
    ppermute x0 -> x17, waiting for transfers between devices: none -> 37.7 us  [the longest x3 17.1 us: shards(): down, up, far = (lax.ppermute(own, 'y', ring(k)) for k in (1, 3, 2))]
    all_to_all x4 -> x3, waiting for transfers between devices: 75.5 us -> 39 us  [exchange(): return lax.all_to_all(pieces, axes, 0, 0, tiled=True)]
    cond x1 -> x0, matrix products: 30 us -> none  [shards(): acc_values, acc_weights = lax.cond(needed, work, skip, initial)]
    ppermute x0 -> x17, starting transfers between devices: none -> 29.5 us  [the longest x10 15.6 us: shards(): swap = lambda a: lax.ppermute(a, 'core', SWAP)]
  transfers between devices with their start and end apart: 5 -> 20, of which waited for: 4 -> 8; matrix products, arithmetic and copies ran while one was open for 3% -> 7% of each run, Pallas kernels for 0% -> 13%
where the time goes in v1:
time: 269 us; the launch traced here: 268 us
  waiting for transfers between devices  76.7 us (29%)
  Pallas kernels  66.7 us (25%)
  blocking collectives  44.2 us (16%)
  starting transfers between devices  42.9 us (16%)
  local copies, waits for them, and re-layouts  18.5 us (7%)
  other arithmetic  15.7 us (6%)
  between operations  3.34 us (1%)
    all_to_all x2, blocking collectives, exchange(): return lax.all_to_all(pieces, axes, 0, 0, tiled=True)  44.2 us
    all_to_all x3, waiting for transfers between devices, exchange(): return lax.all_to_all(pieces, axes, 0, 0, tiled=True)  39 us
    pallas_call x4, Pallas kernels, attn_call(): pl.pallas_call(kernel, out_shape=out_shape, grid_spec=pltpu.PrefetchScala...  34.6 us
    pallas_call x1, Pallas kernels, loss_parts(): pl.pallas_call(loss_kernel, out_shape=(jax.ShapeDtypeStruct((2, 4, 128, 2...  19.4 us
    ppermute x3, waiting for transfers between devices, shards(): down, up, far = (lax.ppermute(own, 'y', ring(k)) for k in (1, 3, 2))  17.1 us
    ppermute x10, starting transfers between devices, shards(): swap = lambda a: lax.ppermute(a, 'core', SWAP)  15.6 us
    ppermute x3, waiting for transfers between devices, shards(): mine = [lax.ppermute(p, 'vocab', ring(s)) for p, s in zip(sent, (1, 2, 3))]  14.5 us
    all_to_all x3, starting transfers between devices, exchange(): return lax.all_to_all(pieces, axes, 0, 0, tiled=True)  13.4 us
  transfers between devices with their start and end apart: 20, of which 8 were waited for; matrix products, arithmetic and copies ran while one was open for 7% of the time, Pallas kernels for 13%

profile of v1, /device:TPU:1, one launch (start us, length us, event | category | flops | bytes accessed | tf_op | source)
XLA Modules:
  0.0 268.0 jit_solution(8847625791322936826)
XLA Ops:
  3.4 20.5 %all_to_all.25 = bf16[8,512,128]{2,1,0:T(8,128)(2,1)S(1)} all-to-all(bf16[8,512,128]{2,1,0:T(8,128)(2,1)S(1)} %pad_maximum_fusion.1), channel_id=1, replica_groups=mesh['x'=4,'y'=4,'core'=2,'vocab'=4] {'x','core'}, dimensions={0} | all-to-all | bytes 2097152 | tf_op jit(solution)/shard_map/all_to_all | solution.py:39
  31.6 6.9 %collective-permute-done.4.a_ref = bf16[2048,128]{1,0:T(8,128)(2,1)S(1)} collective-permute-done((bf16[2048,128]{1,0:T(8,128)(2,1)S(1)}, bf16[2048,128]{1,0:T(8,128)(2,1)S(1)}, u32[]{:S(2)}, u32[]{:S(2)}) %collective-permute-start.4) | collective-permute-done | bytes 524320 | tf_op jit(solution)/shard_map/ppermute | solution.py:350
  40.7 10.2 %collective-permute-done.a_ref = bf16[2048,128]{1,0:T(8,128)(2,1)S(1)} collective-permute-done((bf16[2048,128]{1,0:T(8,128)(2,1)S(1)}, bf16[2048,128]{1,0:T(8,128)(2,1)S(1)}, u32[]{:S(2)}, u32[]{:S(2)}) %collective-permute-start) | collective-permute-done | bytes 524320 | tf_op jit(solution)/shard_map/ppermute | solution.py:350
  52.9 4.0 %fusion.12 = (bf16[512,1152]{1,0:T(8,128)(2,1)}, bf16[512,1152]{1,0:T(8,128)(2,1)}, bf16[512,1152]{1,0:T(8,128)(2,1)}) fusion(bf16[1024,4608]{1,0:T(8,128)(2,1)} %w_ref.1, s32[]{:T(128)S(6)} %select_n.55, s32[]{:T(128)S(6)} %select_n.61, s32[]{:T(128)S(6)} %select_n.59, s32[]{:T(128)S(6)} %select_n.57), kind=kLoop, calls=%fused_computation.49 | loop fusion | bytes 7077904 | tf_op jit(solution)/shard_map/dynamic_slice | solution.py:353
  58.7 3.3 %collective-permute-start.8 = (bf16[512,1152]{1,0:T(8,128)(2,1)}, bf16[512,1152]{1,0:T(8,128)(2,1)}, u32[]{:S(2)}, u32[]{:S(2)}) collective-permute-start(bf16[512,1152]{1,0:T(8,128)(2,1)} %get-tuple-element.15), channel_id=1, source_target_pairs={{0,2},{1,3},{2,0},{3,1},{4,6},{5,7},{6,4},{7,5},{8,10},{9,11},{10,... | collective-permute-start | bytes 3538952 | tf_op jit(solution)/shard_map/ppermute | solution.py:356
  65.1 9.8 %shard_map.130.in_ref = f32[4,512,256]{2,1,0:T(8,128)} custom-call(s32[2]{0:T(128)} %pad_add_fusion.4.sc_ref, bf16[4,512,128]{2,1,0:T(8,128)(2,1)} %bitcast.48, bf16[2048,128]{1,0:T(8,128)(2,1)} %bitcast.62, bf16[2048,128]{1,0:T(8,128)(2,1)} %collective-permute-done.6.b_ref), custom_call_target="tpu_custom_call" | custom-call | tf_op jit(solution)/shard_map/pallas_call | solution.py:153
  74.9 8.1 %shard_map.131.in_ref = f32[4,512,256]{2,1,0:T(8,128)} custom-call(s32[2]{0:T(128)} %pad_add_fusion.3.sc_ref, bf16[4,512,128]{2,1,0:T(8,128)(2,1)} %bitcast.49, bf16[2048,128]{1,0:T(8,128)(2,1)} %copy-done.8, bf16[2048,128]{1,0:T(8,128)(2,1)} %copy-done.10, f32[4,512,256]{2,1,0:T(8,128)} %shard_map.130.in_ref), custom_call_target="tpu_custom_call" | custom-call | tf_op jit(solution)/shard_map/pallas_call | solution.py:153
  83.1 8.1 %shard_map.132.in_ref = f32[4,512,256]{2,1,0:T(8,128)} custom-call(s32[2]{0:T(128)} %pad_add_fusion.2.sc_ref, bf16[4,512,128]{2,1,0:T(8,128)(2,1)} %bitcast.50, bf16[2048,128]{1,0:T(8,128)(2,1)} %copy-done.9, bf16[2048,128]{1,0:T(8,128)(2,1)} %collective-permute-done.3.b_ref, f32[4,512,256]{2,1,0:T(8,128)} %shard_map.131.in_ref), custom_call_target="tpu_custom_call" | custom-call | tf_op jit(solution)/shard_map/pallas_call | solution.py:153
  92.0 8.6 %shard_map.133 = bf16[4,4,512,128]{3,2,1,0:T(8,128)(2,1)} custom-call(s32[2]{0:T(128)} %pad_add_fusion.1.sc_ref, bf16[4,512,128]{2,1,0:T(8,128)(2,1)} %bitcast.51, bf16[2048,128]{1,0:T(8,128)(2,1)} %copy-done.7, bf16[2048,128]{1,0:T(8,128)(2,1)} %copy-done.11, f32[4,512,256]{2,1,0:T(8,128)} %shard_map.132.in_ref), custom_call_target="tpu_custom_call" | custom-call | tf_op jit(solution)/shard_map/pallas_call | solution.py:153
  100.7 5.0 %all-to-all-start.1 = ((bf16[32,256,128]{2,1,0:T(8,128)(2,1)}), bf16[32,256,128]{2,1,0:T(8,128)(2,1)S(1)}, u32[]{:S(2)}, u32[]{:S(2)}) async-start(bf16[32,256,128]{2,1,0:T(8,128)(2,1)} %bitcast.53), calls=%async_computation.1 | async-start | bytes 4194304 | tf_op jit(solution)/shard_map/all_to_all | solution.py:39
  106.1 14.5 %collective-permute-done.8.a2 = bf16[512,1152]{1,0:T(8,128)(2,1)} collective-permute-done((bf16[512,1152]{1,0:T(8,128)(2,1)}, bf16[512,1152]{1,0:T(8,128)(2,1)}, u32[]{:S(2)}, u32[]{:S(2)}) %collective-permute-start.8) | collective-permute-done | bytes 1179680 | tf_op jit(solution)/shard_map/ppermute | solution.py:356
  120.6 5.7 %collective-permute-start.11 = (bf16[512,1152]{1,0:T(8,128)(2,1)}, bf16[512,1152]{1,0:T(8,128)(2,1)}, u32[]{:S(2)}, u32[]{:S(2)}) collective-permute-start(bf16[512,1152]{1,0:T(8,128)(2,1)} %collective-permute-done.8.a2), channel_id=1, source_target_pairs={{0,4},{4,0},{1,5},{5,1},{2,6},{6,2},{3,7},{7,3},{8,12},{12,8},{9,1... | collective-permute-start | bytes 3538952 | tf_op jit(solution)/shard_map/ppermute | solution.py:349
  130.9 4.8 %all-to-all-done.1.att_ref = bf16[32,256,128]{2,1,0:T(8,128)(2,1)S(1)} async-done(((bf16[32,256,128]{2,1,0:T(8,128)(2,1)}), bf16[32,256,128]{2,1,0:T(8,128)(2,1)S(1)}, u32[]{:S(2)}, u32[]{:S(2)}) %all-to-all-start.1) | async-done | bytes 2097184 | tf_op jit(solution)/shard_map/all_to_all | solution.py:39
  137.1 10.4 %shard_map.134 = (f32[256,1152]{1,0:T(8,128)}, f32[4,24,1152]{2,1,0:T(8,128)}) custom-call(s32[2]{0:T(128)} %pad_add_fusion.sc_ref, s32[8]{0:T(128)} %pick_ref.1, bf16[32,256,128]{2,1,0:T(8,128)(2,1)} %copy-done.2, bf16[1024,4608]{1,0:T(8,128)(2,1)} %w_ref.1, bf16[512,1152]{1,0:T(8,128)(2,1)} %collective-permute-done.7.a1, ...), custom_call_target="tpu_custom_call" | custom-call | tf_op jit(solution)/shard_map/pallas_call | solution.py:213
  147.4 3.5 %all-to-all-start.2 = ((f32[4,24,1152]{2,1,0:T(8,128)}), f32[4,24,1152]{2,1,0:T(8,128)S(1)}, u32[]{:S(2)}, u32[]{:S(2)}) async-start(f32[4,24,1152]{2,1,0:T(8,128)} %get-tuple-element.8), calls=%async_computation.2 | async-start | bytes 884736 | tf_op jit(solution)/shard_map/all_to_all | solution.py:39
  151.9 6.1 %all-to-all-done.2.zr_ref = f32[4,24,1152]{2,1,0:T(8,128)S(1)} async-done(((f32[4,24,1152]{2,1,0:T(8,128)}), f32[4,24,1152]{2,1,0:T(8,128)S(1)}, u32[]{:S(2)}, u32[]{:S(2)}) %all-to-all-start.2) | async-done | bytes 442400 | tf_op jit(solution)/shard_map/all_to_all | solution.py:39
  161.1 23.6 %all_to_all.26 = bf16[16,8,4736]{2,1,0:T(8,128)(2,1)S(1)} all-to-all(bf16[16,8,4736]{2,1,0:T(8,128)(2,1)} %shard_map.135), channel_id=1, replica_groups=mesh['x'=4,'y'=4,'core'=2,'vocab'=4] {'x','y'}, dimensions={0} | all-to-all | bytes 2424832 | tf_op jit(solution)/shard_map/all_to_all | solution.py:39
  184.8 2.7 %collective-permute-start.13 = (bf16[128,4736]{1,0:T(8,128)(2,1)S(1)}, bf16[128,4736]{1,0:T(8,128)(2,1)S(1)}, u32[]{:S(2)}, u32[]{:S(2)}) collective-permute-start(bf16[128,4736]{1,0:T(8,128)(2,1)S(1)} %bitcast.54), channel_id=1, source_target_pairs={{0,4},{4,0},{1,5},{5,1},{2,6},{6,2},{3,7},{7,3},{8,12},{12,8},{9,1... | collective-permute-start | bytes 3637256 | tf_op jit(solution)/shard_map/ppermute | solution.py:349
  191.0 19.4 %shard_map.136 = (bf16[2,4,128,2304]{3,2,1,0:T(8,128)(2,1)}, f32[8,256]{1,0:T(8,128)}) custom-call(s32[1]{0:T(128)} %bitcast.19.sc_ref, bf16[128,4736]{1,0:T(8,128)(2,1)} %bitcast.55, bf16[128,4736]{1,0:T(8,128)(2,1)} %copy-done.6, bf16[1024,4608]{1,0:T(8,128)(2,1)} %e_ref.1), custom_call_target="tpu_custom_call" | custom-call | tf_op jit(solution)/shard_map/pallas_call | solution.py:310
  210.4 3.3 %slice_bitcast_fusion = bf16[4,128,2304]{2,1,0:T(8,128)(2,1)} fusion(bf16[2,4,128,2304]{3,2,1,0:T(8,128)(2,1)} %get-tuple-element.9), kind=kLoop, calls=%fused_computation.5 | loop fusion | bytes 4718592 | tf_op jit(solution)/shard_map/squeeze | solution.py:382
  214.9 3.5 %collective-permute-done.15 = f32[2,128]{1,0:T(2,128)S(1)} collective-permute-done((f32[2,128]{1,0:T(2,128)S(1)}, f32[2,128]{1,0:T(2,128)S(1)}, u32[]{:S(2)}, u32[]{:S(2)}) %collective-permute-start.15) | collective-permute-done | bytes 1056 | tf_op jit(solution)/shard_map/ppermute | solution.py:349
  223.0 4.9 %all-to-all-start.4 = ((bf16[64,8,2432]{2,1,0:T(8,128)(2,1)}), bf16[64,8,2432]{2,1,0:T(8,128)(2,1)S(1)}, u32[]{:S(2)}, u32[]{:S(2)}) async-start(bf16[64,8,2432]{2,1,0:T(8,128)(2,1)} %pad_maximum_fusion), calls=%async_computation.4 | async-start | bytes 4980736 | tf_op jit(solution)/shard_map/all_to_all | solution.py:39
  232.2 28.1 %all-to-all-done.4 = bf16[64,8,2432]{2,1,0:T(8,128)(2,1)S(1)} async-done(((bf16[64,8,2432]{2,1,0:T(8,128)(2,1)}), bf16[64,8,2432]{2,1,0:T(8,128)(2,1)S(1)}, u32[]{:S(2)}, u32[]{:S(2)}) %all-to-all-start.4) | async-done | bytes 2490400 | tf_op jit(solution)/shard_map/all_to_all | solution.py:39
  262.2 3.2 %collective-permute-start.16 = (f32[1]{0:T(128)}, f32[1]{0:T(128)}, u32[]{:S(2)}, u32[]{:S(2)}) collective-permute-start(f32[1]{0:T(128)} %bitcast.24), channel_id=1, source_target_pairs={{0,4},{4,0},{1,5},{5,1},{2,6},{6,2},{3,7},{7,3},{8,12},{12,8},{9,1... | collective-permute-start | bytes 20 | tf_op jit(solution)/shard_map/ppermute | solution.py:395
  (106 shorter events, 46.5 us)
Async XLA Ops:
  24.8 32.1 %copy-start.4 = (bf16[8,256,128]{2,1,0:T(8,128)(2,1)}, bf16[8,256,128]{2,1,0:T(8,128)(2,1)S(1)}, u32[]{:S(2)}) copy-start(bf16[8,256,128]{2,1,0:T(8,128)(2,1)S(1)} %get-tuple-element.17) | copy-start | bytes 1572868
  24.8 13.8 %collective-permute-start.4 = (bf16[2048,128]{1,0:T(8,128)(2,1)S(1)}, bf16[2048,128]{1,0:T(8,128)(2,1)S(1)}, u32[]{:S(2)}, u32[]{:S(2)}) collective-permute-start(bf16[2048,128]{1,0:T(8,128)(2,1)S(1)} %bitcast.58), channel_id=1, source_target_pairs={{0,8},{8,16},{16,24},{24,0},{1,9},{9,17},{17,25},{25,1},{2,10},{10... | collective-permute-start | bytes 1572872 | tf_op jit(solution)/shard_map/ppermute | solution.py:350
  26.1 24.8 %collective-permute-start = (bf16[2048,128]{1,0:T(8,128)(2,1)S(1)}, bf16[2048,128]{1,0:T(8,128)(2,1)S(1)}, u32[]{:S(2)}, u32[]{:S(2)}) collective-permute-start(bf16[2048,128]{1,0:T(8,128)(2,1)S(1)} %bitcast.59), channel_id=1, source_target_pairs={{0,16},{8,24},{16,0},{24,8},{1,17},{9,25},{17,1},{25,9},{2,18},{10... | collective-permute-start | bytes 1572872 | tf_op jit(solution)/shard_map/ppermute | solution.py:350
  28.7 24.1 %collective-permute-start.2 = (bf16[2048,128]{1,0:T(8,128)(2,1)S(1)}, bf16[2048,128]{1,0:T(8,128)(2,1)S(1)}, u32[]{:S(2)}, u32[]{:S(2)}) collective-permute-start(bf16[2048,128]{1,0:T(8,128)(2,1)S(1)} %bitcast.60), channel_id=1, source_target_pairs={{0,24},{8,0},{16,8},{24,16},{1,25},{9,1},{17,9},{25,17},{2,26},{10... | collective-permute-start | bytes 1572872 | tf_op jit(solution)/shard_map/ppermute | solution.py:350
  29.8 28.9 %collective-permute-start.6 = (bf16[2048,128]{1,0:T(8,128)(2,1)S(1)}, bf16[2048,128]{1,0:T(8,128)(2,1)}, u32[]{:S(2)}, u32[]{:S(2)}) collective-permute-start(bf16[2048,128]{1,0:T(8,128)(2,1)S(1)} %bitcast.61), channel_id=1, source_target_pairs={{0,4},{4,0},{1,5},{5,1},{2,6},{6,2},{3,7},{7,3},{8,12},{12,8},{9,1... | collective-permute-start | bytes 1572872 | tf_op jit(solution)/shard_map/ppermute | solution.py:349
  38.6 23.4 %collective-permute-start.5 = (bf16[2048,128]{1,0:T(8,128)(2,1)S(1)}, bf16[2048,128]{1,0:T(8,128)(2,1)S(1)}, u32[]{:S(2)}, u32[]{:S(2)}) collective-permute-start(bf16[2048,128]{1,0:T(8,128)(2,1)S(1)} %collective-permute-done.4.a_ref), channel_id=1, source_target_pairs={{0,4},{4,0},{1,5},{5,1},{2,6},{6,2},{3,7},{7,3},{8,12},{12,8},{9,1... | collective-permute-start | bytes 1572872 | tf_op jit(solution)/shard_map/ppermute | solution.py:349
  50.9 40.3 %collective-permute-start.1 = (bf16[2048,128]{1,0:T(8,128)(2,1)S(1)}, bf16[2048,128]{1,0:T(8,128)(2,1)S(1)}, u32[]{:S(2)}, u32[]{:S(2)}) collective-permute-start(bf16[2048,128]{1,0:T(8,128)(2,1)S(1)} %collective-permute-done.a_ref), channel_id=1, source_target_pairs={{0,4},{4,0},{1,5},{5,1},{2,6},{6,2},{3,7},{7,3},{8,12},{12,8},{9,1... | collective-permute-start | bytes 1572872 | tf_op jit(solution)/shard_map/ppermute | solution.py:349
  52.8 30.2 %collective-permute-start.3 = (bf16[2048,128]{1,0:T(8,128)(2,1)S(1)}, bf16[2048,128]{1,0:T(8,128)(2,1)}, u32[]{:S(2)}, u32[]{:S(2)}) collective-permute-start(bf16[2048,128]{1,0:T(8,128)(2,1)S(1)} %collective-permute-done.2.a_ref), channel_id=1, source_target_pairs={{0,4},{4,0},{1,5},{5,1},{2,6},{6,2},{3,7},{7,3},{8,12},{12,8},{9,1... | collective-permute-start | bytes 1572872 | tf_op jit(solution)/shard_map/ppermute | solution.py:349
  56.9 48.7 %collective-permute-start.7 = (bf16[512,1152]{1,0:T(8,128)(2,1)}, bf16[512,1152]{1,0:T(8,128)(2,1)}, u32[]{:S(2)}, u32[]{:S(2)}) collective-permute-start(bf16[512,1152]{1,0:T(8,128)(2,1)} %get-tuple-element.16), channel_id=1, source_target_pairs={{0,1},{1,2},{2,3},{3,0},{4,5},{5,6},{6,7},{7,4},{8,9},{9,10},{10,1... | collective-permute-start | bytes 3538952 | tf_op jit(solution)/shard_map/ppermute | solution.py:356
  58.7 61.9 %collective-permute-start.8 = (bf16[512,1152]{1,0:T(8,128)(2,1)}, bf16[512,1152]{1,0:T(8,128)(2,1)}, u32[]{:S(2)}, u32[]{:S(2)}) collective-permute-start(bf16[512,1152]{1,0:T(8,128)(2,1)} %get-tuple-element.15), channel_id=1, source_target_pairs={{0,2},{1,3},{2,0},{3,1},{4,6},{5,7},{6,4},{7,5},{8,10},{9,11},{10,... | collective-permute-start | bytes 3538952 | tf_op jit(solution)/shard_map/ppermute | solution.py:356
  62.0 64.3 %collective-permute-start.9 = (bf16[512,1152]{1,0:T(8,128)(2,1)}, bf16[512,1152]{1,0:T(8,128)(2,1)}, u32[]{:S(2)}, u32[]{:S(2)}) collective-permute-start(bf16[512,1152]{1,0:T(8,128)(2,1)} %get-tuple-element.14), channel_id=1, source_target_pairs={{0,3},{1,0},{2,1},{3,2},{4,7},{5,4},{6,5},{7,6},{8,11},{9,8},{10,9... | collective-permute-start | bytes 3538952 | tf_op jit(solution)/shard_map/ppermute | solution.py:356
  100.6 25.9 %copy-start.16 = (s32[8]{0:T(128)S(1)}, s32[8]{0:T(128)}, u32[]{:S(2)}) copy-start(s32[8]{0:T(128)} %param.20) | copy-start | bytes 100
  100.6 26.5 %copy-start.13 = (f32[1152]{0:T(1024)S(1)}, f32[1152]{0:T(1024)}, u32[]{:S(2)}) copy-start(f32[1152]{0:T(1024)} %param.17) | copy-start | bytes 13828
  100.7 27.2 %copy-start.14 = (s32[8]{0:T(128)S(1)}, s32[8]{0:T(128)}, u32[]{:S(2)}) copy-start(s32[8]{0:T(128)} %pick_ref.1) | copy-start | bytes 100
  100.7 35.0 %all-to-all-start.1 = ((bf16[32,256,128]{2,1,0:T(8,128)(2,1)}), bf16[32,256,128]{2,1,0:T(8,128)(2,1)S(1)}, u32[]{:S(2)}, u32[]{:S(2)}) async-start(bf16[32,256,128]{2,1,0:T(8,128)(2,1)} %bitcast.53), calls=%async_computation.1 | async-start | bytes 4194304 | tf_op jit(solution)/shard_map/all_to_all | solution.py:39
  105.6 25.3 %collective-permute-start.10 = (bf16[512,1152]{1,0:T(8,128)(2,1)}, bf16[512,1152]{1,0:T(8,128)(2,1)}, u32[]{:S(2)}, u32[]{:S(2)}) collective-permute-start(bf16[512,1152]{1,0:T(8,128)(2,1)} %collective-permute-done.7.a1), channel_id=1, source_target_pairs={{0,4},{4,0},{1,5},{5,1},{2,6},{6,2},{3,7},{7,3},{8,12},{12,8},{9,1... | collective-permute-start | bytes 3538952 | tf_op jit(solution)/shard_map/ppermute | solution.py:349
  120.6 10.4 %collective-permute-start.11 = (bf16[512,1152]{1,0:T(8,128)(2,1)}, bf16[512,1152]{1,0:T(8,128)(2,1)}, u32[]{:S(2)}, u32[]{:S(2)}) collective-permute-start(bf16[512,1152]{1,0:T(8,128)(2,1)} %collective-permute-done.8.a2), channel_id=1, source_target_pairs={{0,4},{4,0},{1,5},{5,1},{2,6},{6,2},{3,7},{7,3},{8,12},{12,8},{9,1... | collective-permute-start | bytes 3538952 | tf_op jit(solution)/shard_map/ppermute | solution.py:349
  126.2 4.7 %collective-permute-start.12 = (bf16[512,1152]{1,0:T(8,128)(2,1)}, bf16[512,1152]{1,0:T(8,128)(2,1)}, u32[]{:S(2)}, u32[]{:S(2)}) collective-permute-start(bf16[512,1152]{1,0:T(8,128)(2,1)} %collective-permute-done.9.a3), channel_id=1, source_target_pairs={{0,4},{4,0},{1,5},{5,1},{2,6},{6,2},{3,7},{7,3},{8,12},{12,8},{9,1... | collective-permute-start | bytes 3538952 | tf_op jit(solution)/shard_map/ppermute | solution.py:349
  147.4 10.6 %all-to-all-start.2 = ((f32[4,24,1152]{2,1,0:T(8,128)}), f32[4,24,1152]{2,1,0:T(8,128)S(1)}, u32[]{:S(2)}, u32[]{:S(2)}) async-start(f32[4,24,1152]{2,1,0:T(8,128)} %get-tuple-element.8), calls=%async_computation.2 | async-start | bytes 884736 | tf_op jit(solution)/shard_map/all_to_all | solution.py:39
  184.8 5.2 %collective-permute-start.13 = (bf16[128,4736]{1,0:T(8,128)(2,1)S(1)}, bf16[128,4736]{1,0:T(8,128)(2,1)S(1)}, u32[]{:S(2)}, u32[]{:S(2)}) collective-permute-start(bf16[128,4736]{1,0:T(8,128)(2,1)S(1)} %bitcast.54), channel_id=1, source_target_pairs={{0,4},{4,0},{1,5},{5,1},{2,6},{6,2},{3,7},{7,3},{8,12},{12,8},{9,1... | collective-permute-start | bytes 3637256 | tf_op jit(solution)/shard_map/ppermute | solution.py:349
  213.7 5.5 %collective-permute-start.14 = (bf16[4,128,2304]{2,1,0:T(8,128)(2,1)}, bf16[4,128,2304]{2,1,0:T(8,128)(2,1)S(1)}, u32[]{:S(2)}, u32[]{:S(2)}) collective-permute-start(bf16[4,128,2304]{2,1,0:T(8,128)(2,1)} %slice_bitcast_fusion), channel_id=1, source_target_pairs={{0,4},{4,0},{1,5},{5,1},{2,6},{6,2},{3,7},{7,3},{8,12},{12,8},{9,1... | collective-permute-start | bytes 7077896 | tf_op jit(solution)/shard_map/ppermute | solution.py:349
  214.7 3.7 %collective-permute-start.15 = (f32[2,128]{1,0:T(2,128)S(1)}, f32[2,128]{1,0:T(2,128)S(1)}, u32[]{:S(2)}, u32[]{:S(2)}) collective-permute-start(f32[2,128]{1,0:T(2,128)S(1)} %slice.71), channel_id=1, source_target_pairs={{0,4},{4,0},{1,5},{5,1},{2,6},{6,2},{3,7},{7,3},{8,12},{12,8},{9,1... | collective-permute-start | bytes 3080 | tf_op jit(solution)/shard_map/ppermute | solution.py:349
  223.0 37.3 %all-to-all-start.4 = ((bf16[64,8,2432]{2,1,0:T(8,128)(2,1)}), bf16[64,8,2432]{2,1,0:T(8,128)(2,1)S(1)}, u32[]{:S(2)}, u32[]{:S(2)}) async-start(bf16[64,8,2432]{2,1,0:T(8,128)(2,1)} %pad_maximum_fusion), calls=%async_computation.4 | async-start | bytes 4980736 | tf_op jit(solution)/shard_map/all_to_all | solution.py:39
  262.2 4.0 %collective-permute-start.16 = (f32[1]{0:T(128)}, f32[1]{0:T(128)}, u32[]{:S(2)}, u32[]{:S(2)}) collective-permute-start(f32[1]{0:T(128)} %bitcast.24), channel_id=1, source_target_pairs={{0,4},{4,0},{1,5},{5,1},{2,6},{6,2},{3,7},{7,3},{8,12},{12,8},{9,1... | collective-permute-start | bytes 20 | tf_op jit(solution)/shard_map/ppermute | solution.py:395
  (13 other events, 105.4 us)

commit v2 on v1

v2 whole, which is shorter than its diff:
```python
import functools

import jax
import jax.numpy as jnp
from jax import lax
from jax.experimental import pallas as pl
from jax.experimental.pallas import tpu as pltpu
from jax.sharding import Mesh
from jax.sharding import PartitionSpec as P


D = 4608
HEAD_DIM = 128
PICK = 8
SPAN = 512
BLK = 256
COLS = 1152
EXT = 128
LOSS_TOKENS = 256
CTX = ("x", "y", "core")

attn_cap = 50.0
logit_cap = 30.0
query_scalar = 144.0
epsilon = 1e-06

f32 = jnp.float32
bf16 = jnp.bfloat16


def ring(k):
    return [(j, (j + k) % 4) for j in range(4)]


SWAP = [(0, 1), (1, 0)]


def exchange(pieces, axes):
    return lax.all_to_all(pieces, axes, 0, 0, tiled=True)


def scores(q, k):
    return lax.dot_general(q, k, (((1,), (1,)), ((), ())), preferred_element_type=f32)


def weigh(raw):
    return jnp.exp(attn_cap * jnp.tanh(raw * (query_scalar**-0.5 / attn_cap)))


def lane_sums(p):
    parts = [p[:, i : i + 128] for i in range(0, p.shape[1], 128)]
    return functools.reduce(jnp.add, parts)


def load_kv(core, a_ref, b_ref, buf, sem):
    copies = [
        pltpu.make_async_copy(a_ref, buf.at[core], sem.at[0]),
        pltpu.make_async_copy(b_ref, buf.at[1 - core], sem.at[1]),
    ]
    for copy in copies:
        copy.start()
    return copies


def seen(q, buf, first, span, valid=None):
    p = weigh(scores(q, buf[0, pl.ds(first, span), :]))
    if valid is not None:
        half = span // 2
        p = jnp.concatenate([p[:, :half], jnp.where(valid, p[:, half:], 0.0)], axis=1)
    v = buf[1, pl.ds(first, span), :]
    return jnp.dot(p.astype(bf16), v, preferred_element_type=f32), lane_sums(p)


def attn_own_kernel(sc_ref, q_ref, a_ref, b_ref, acc_ref, buf, sem):
    i = pl.program_id(0)

    @pl.when(i == 0)
    def _():
        for copy in load_kv(sc_ref[1], a_ref, b_ref, buf, sem):
            copy.wait()

    def body(earlier):
        has_edge = i >= 2
        edge0 = jnp.maximum(i - 2, 0) * SPAN
        diag0 = i * SPAN
        tq = lax.broadcasted_iota(jnp.int32, (BLK, BLK), 0)
        tk = lax.broadcasted_iota(jnp.int32, (BLK, BLK), 1)
        causal = tk <= tq
        beyond = jnp.logical_and(jnp.logical_not(causal), has_edge)
        for r in range(2):
            q = q_ref[0, pl.ds(r * BLK, BLK), :]
            raw = scores(q, buf[0, pl.ds(diag0 + r * BLK, BLK), :])
            if earlier:
                raw = jnp.where(causal, raw, scores(q, buf[0, pl.ds(edge0 + r * BLK, BLK), :]))
            p = weigh(raw)
            pd = jnp.where(causal, p, 0.0)
            top = jnp.dot(
                pd.astype(bf16), buf[1, pl.ds(diag0 + r * BLK, BLK), :], preferred_element_type=f32
            )
            low = lane_sums(pd)
            if earlier:
                pe = jnp.where(beyond, p, 0.0)
                top += jnp.dot(
                    pe.astype(bf16), buf[1, pl.ds(edge0 + r * BLK, BLK), :],
                    preferred_element_type=f32,
                )
                low += lane_sums(pe)
                more = seen(q, buf, (i - 1) * SPAN, SPAN)
                top, low = top + more[0], low + more[1]
            if r == 1:
                more = seen(q, buf, diag0, BLK)
                top, low = top + more[0], low + more[1]
            elif earlier:
                p = jnp.where(has_edge, weigh(scores(q, buf[0, pl.ds(edge0 + BLK, BLK), :])), 0.0)
                top += jnp.dot(
                    p.astype(bf16), buf[1, pl.ds(edge0 + BLK, BLK), :], preferred_element_type=f32
                )
                low += lane_sums(p)
            acc_ref[0, pl.ds(r * BLK, BLK), :HEAD_DIM] = top
            acc_ref[0, pl.ds(r * BLK, BLK), HEAD_DIM:] = low

    pl.when(i == 0)(lambda: body(False))
    pl.when(i > 0)(lambda: body(True))


def attn_more_kernel(chunks, last, at, sc_ref, q_ref, *refs):
    keys, (in_ref, out_ref, buf, sem, *scr) = refs[: 2 * chunks], refs[2 * chunks :]
    i = pl.program_id(0)
    acc_ref = scr[0] if last else out_ref

    @pl.when(i == 0)
    def _():
        copies = []
        for n in range(chunks):
            copies += load_kv(sc_ref[1], keys[2 * n], keys[2 * n + 1], buf.at[n], sem.at[n])
        for copy in copies:
            copy.wait()
        acc_ref[...] = in_ref[...]

    for n in range(chunks):

        @pl.when(jnp.logical_and(i == 0, sc_ref[at + n] == 0))
        def _():
            for r in range(2):
                rows = pl.ds(r * BLK, BLK)
                top, low = seen(q_ref[0, rows, :], buf.at[n], 0, SPAN)
                acc_ref[0, rows, :HEAD_DIM] += top
                acc_ref[0, rows, HEAD_DIM:] += low

    @pl.when(i > 0)
    def _():
        for r in range(2):
            rows = pl.ds(r * BLK, BLK)
            q = q_ref[0, rows, :]
            top, low = in_ref[0, rows, :HEAD_DIM], in_ref[0, rows, HEAD_DIM:]
            for n in range(chunks):
                newest = i - sc_ref[at + n]
                first = jnp.maximum(newest - 1, 0) * SPAN
                more = seen(q, buf.at[n], first, 2 * SPAN, newest > 0)
                top, low = top + more[0], low + more[1]
            acc_ref[0, rows, :HEAD_DIM] = top
            acc_ref[0, rows, HEAD_DIM:] = low

    if last:
        whole = jnp.sum(acc_ref[0, :, HEAD_DIM:], axis=1, keepdims=True)
        done = (acc_ref[0, :, :HEAD_DIM] / whole).astype(bf16)
        for z in range(4):
            out_ref[z, 0] = done


def attn_call(scalars, q, keys, acc=None, at=0, last=False):
    q_spec = pl.BlockSpec((1, SPAN, HEAD_DIM), lambda i, sc: (i, 0, 0))
    acc_spec = pl.BlockSpec((1, SPAN, 2 * HEAD_DIM), lambda i, sc: (i, 0, 0))
    hbm = pl.BlockSpec(memory_space=pltpu.MemorySpace.HBM)
    chunks = len(keys) // 2
    out_spec, out_shape = acc_spec, jax.ShapeDtypeStruct((4, SPAN, 2 * HEAD_DIM), f32)
    in_specs, args = [q_spec] + [hbm] * len(keys), [q, *keys]
    if acc is None:
        kernel = attn_own_kernel
        scratch = [pltpu.VMEM((2, 4 * SPAN, HEAD_DIM), bf16), pltpu.SemaphoreType.DMA((2,))]
    else:
        in_specs, args = in_specs + [acc_spec], args + [acc]
        kernel = functools.partial(attn_more_kernel, chunks, last, at)
        scratch = [
            pltpu.VMEM((chunks, 2, 4 * SPAN, HEAD_DIM), bf16),
            pltpu.SemaphoreType.DMA((chunks, 2)),
        ]
    if last:
        out_spec = pl.BlockSpec((4, 1, SPAN, HEAD_DIM), lambda i, sc: (0, i, 0, 0))
        out_shape = jax.ShapeDtypeStruct((4, 4, SPAN, HEAD_DIM), bf16)
        scratch = scratch + [pltpu.VMEM((1, SPAN, 2 * HEAD_DIM), f32)]
    return pl.pallas_call(
        kernel,
        out_shape=out_shape,
        grid_spec=pltpu.PrefetchScalarGridSpec(
            num_scalar_prefetch=1,
            grid=(4,),
            in_specs=in_specs,
            out_specs=out_spec,
            scratch_shapes=scratch,
        ),
        cost_estimate=pl.CostEstimate(
            flops=5_000_000_000 * chunks, transcendentals=0, bytes_accessed=4_000_000
        ),
        compiler_params=pltpu.CompilerParams(dimension_semantics=("arbitrary",)),
    )(scalars, *args)


def row_of_sums(m):
    return lax.dot_general(
        jnp.ones((8, m.shape[1]), f32), m, (((1,), (1,)), ((), ())),
        preferred_element_type=f32, precision=lax.Precision.HIGHEST,
    )


def proj_kernel(
    sc_ref, pick_ref, att_ref, w_ref, a1, a2, a3, b1, b2, b3, rp_ref, pg_ref, fg_ref,
    own_ref, zp_ref, abuf, wbuf, asem, wsem,
):
    zi, ci = sc_ref[0], sc_ref[1]
    heads = [zi * 2, zi * 2 + 1]
    heads += [((zi - s + 4) % 4) * 2 + ci for s in (1, 2, 3)]
    heads += [((zi - s + 4) % 4) * 2 + 1 - ci for s in (1, 2, 3)]
    col = pl.multiple_of(zi * COLS, 128)
    src = [w_ref.at[pl.ds(0, 512), pl.ds(col, COLS)], w_ref.at[pl.ds(512, 512), pl.ds(col, COLS)]]
    src += [a1, a2, a3, b1, b2, b3]
    acopies, wcopies = [], []
    for n in range(8):
        acopies.append(
            pltpu.make_async_copy(att_ref.at[pl.ds(heads[n] * 4, 4)], abuf.at[n], asem.at[n])
        )
        wcopies.append(pltpu.make_async_copy(src[n], wbuf.at[n], wsem.at[n]))
        acopies[n].start()
        wcopies[n].start()
    for n in range(8):
        acopies[n].wait()
        wcopies[n].wait()
        lhs = jnp.concatenate([abuf[n, h] for h in range(4)], axis=1)
        part = jnp.dot(lhs, wbuf[n], preferred_element_type=f32)
        if n == 0:
            own_ref[...] = part
        else:
            own_ref[...] += part
    own = own_ref[...]
    squares = row_of_sums(lane_sums(own * own))
    for z in range(4):
        for p in range(PICK):
            zp_ref[z, p : p + 1, :] = own_ref[pl.ds(pick_ref[p], 1), :]
        zp_ref[z, 8:16, :] = rp_ref[...]
        zp_ref[z, 16:17, :] = pg_ref[...]
        zp_ref[z, 17:18, :] = fg_ref[...]
        zp_ref[z, 18:24, :] = jnp.zeros((6, COLS), f32)
        zp_ref[z, 18:19, :LOSS_TOKENS] = squares[:1]


def project(scalars, pick, att, w, parts, res_pick, pg, fg):
    hbm = pl.BlockSpec(memory_space=pltpu.MemorySpace.HBM)
    whole = lambda *dims: pl.BlockSpec(dims, lambda i, *sc: (0,) * len(dims))
    return pl.pallas_call(
        proj_kernel,
        out_shape=(
            jax.ShapeDtypeStruct((BLK, COLS), f32),
            jax.ShapeDtypeStruct((4, 24, COLS), f32),
        ),
        grid_spec=pltpu.PrefetchScalarGridSpec(
            num_scalar_prefetch=2,
            grid=(1,),
            in_specs=[hbm] * 8 + [whole(PICK, COLS), whole(1, COLS), whole(1, COLS)],
            out_specs=(whole(BLK, COLS), whole(4, 24, COLS)),
            scratch_shapes=[
                pltpu.VMEM((8, 4, BLK, HEAD_DIM), bf16),
                pltpu.VMEM((8, 512, COLS), bf16),
                pltpu.SemaphoreType.DMA((8,)),
                pltpu.SemaphoreType.DMA((8,)),
            ],
        ),
        compiler_params=pltpu.CompilerParams(dimension_semantics=("arbitrary",)),
    )(scalars, pick, att, w, *parts, res_pick, pg, fg)


def norm_kernel(zr_ref, ext_ref, out_ref):
    own = [zr_ref[z, :8, :] for z in range(4)]
    total = sum(jnp.sum(o * o, axis=1, keepdims=True) for o in own)
    inv = lax.rsqrt(total / D + epsilon)
    picked = [
        (zr_ref[z, 8:16, :] + own[z] * inv * zr_ref[z, 16:17, :]).astype(bf16).astype(f32)
        for z in range(4)
    ]
    total = sum(jnp.sum(o * o, axis=1, keepdims=True) for o in picked)
    inv = lax.rsqrt(total / D + epsilon)
    for z in range(4):
        normed = (picked[z] * inv * zr_ref[z, 17:18, :]).astype(bf16)
        for n in range(16):
            out_ref[n, :, z * COLS : (z + 1) * COLS] = normed
    for n in range(16):
        out_ref[n, :, D:] = ext_ref[...]


def normalise(zr, ext):
    return pl.pallas_call(
        norm_kernel, out_shape=jax.ShapeDtypeStruct((16, PICK, D + EXT), bf16)
    )(zr, ext)


def loss_kernel(sc_ref, g_ref, s_ref, e_ref, own_ref, sib_ref, row_ref, nbuf, acc, sums):
    j = pl.program_id(0)

    @pl.when(j == 0)
    def _():
        nbuf[:128] = g_ref[...]
        nbuf[128:] = s_ref[...]

    emb = e_ref[...]
    raw = scores(nbuf[:, :D], emb)
    bent = jnp.tanh(raw / logit_cap)
    logits = logit_cap * bent
    big = jnp.exp(logits)
    code = nbuf[:, D:].astype(f32)
    target = code[:, 0:1] * 16384.0 + code[:, 1:2] * 128.0 + code[:, 2:3]
    at = lax.broadcasted_iota(jnp.int32, (LOSS_TOKENS, BLK), 1) + (sc_ref[5] + j * BLK)
    hit = at == target.astype(jnp.int32)
    left = jnp.concatenate(
        [(big * (1.0 - bent * bent)).astype(bf16), jnp.where(hit, 1.0, 0.0).astype(bf16)], axis=0
    )
    both = [lane_sums(big), lane_sums(jnp.where(hit, logits, 0.0))]

    @pl.when(j == 0)
    def _():
        acc[...] = jnp.dot(left, emb, preferred_element_type=f32)
        sums[0], sums[1] = both

    @pl.when(jnp.logical_and(j > 0, j < 3))
    def _():
        acc[...] += jnp.dot(left, emb, preferred_element_type=f32)
        sums[0] += both[0]
        sums[1] += both[1]

    @pl.when(j == 3)
    def _():
        for part in range(2):
            row_ref[part : part + 1] = row_of_sums(sums[part] + both[part])[:1]
        row_ref[2:] = jnp.zeros((6, LOSS_TOKENS), f32)
        for part in range(2):
            for z in range(4):
                cols = slice(z * COLS, (z + 1) * COLS)
                rows = slice(part * 256, (part + 1) * 256)
                whole = acc[rows, cols] + jnp.dot(
                    left[rows], emb[:, cols], preferred_element_type=f32
                )
                lanes = slice(part * COLS, (part + 1) * COLS)
                own_ref[z, :, lanes] = whole[:128].astype(bf16)
                sib_ref[z, :, lanes] = whole[128:].astype(bf16)


def loss_parts(scalars, g, s, emb):
    whole = lambda *dims: pl.BlockSpec(dims, lambda i, sc: (0,) * len(dims))
    return pl.pallas_call(
        loss_kernel,
        out_shape=(
            jax.ShapeDtypeStruct((4, 128, 2 * COLS), bf16),
            jax.ShapeDtypeStruct((4, 128, 2 * COLS), bf16),
            jax.ShapeDtypeStruct((8, LOSS_TOKENS), f32),
        ),
        grid_spec=pltpu.PrefetchScalarGridSpec(
            num_scalar_prefetch=1,
            grid=(4,),
            in_specs=[
                whole(128, D + EXT),
                whole(128, D + EXT),
                pl.BlockSpec((BLK, D), lambda i, sc: (i, 0)),
            ],
            out_specs=(
                whole(4, 128, 2 * COLS), whole(4, 128, 2 * COLS), whole(8, LOSS_TOKENS),
            ),
            scratch_shapes=[
                pltpu.VMEM((LOSS_TOKENS, D + EXT), bf16),
                pltpu.VMEM((2 * LOSS_TOKENS, D), f32),
                pltpu.VMEM((2, LOSS_TOKENS, 128), f32),
            ],
        ),
        compiler_params=pltpu.CompilerParams(dimension_semantics=("arbitrary",)),
    )(scalars, g, s, emb)


def join_kernel(own_ref, sib_ref, info_ref, out_ref):
    out_ref[0, :, : 2 * COLS] = (own_ref[0].astype(f32) + sib_ref[0].astype(f32)).astype(bf16)
    for n in range(16):
        out_ref[0, n * 8 : (n + 1) * 8, 2 * COLS :] = info_ref[...].astype(bf16)


def join(own, sib, info):
    block = pl.BlockSpec((1, 128, 2 * COLS), lambda z: (z, 0, 0))
    return pl.pallas_call(
        join_kernel,
        out_shape=jax.ShapeDtypeStruct((4, 128, 2 * COLS + EXT), bf16),
        grid=(4,),
        in_specs=[block, block, pl.BlockSpec((8, EXT), lambda z: (0, 0))],
        out_specs=pl.BlockSpec((1, 128, 2 * COLS + EXT), lambda z: (z, 0, 0)),
    )(own, sib, info)


def shards(
    query_rows, key_rows, value_rows, residual, out_weight, post_gain, final_gain,
    embedding, targets, loss_mask, pick_pos,
):
    xi, yi, ci, zi = (lax.axis_index(a) for a in ("x", "y", "core", "vocab"))
    base = (((xi * 4 + yi) * 2 + ci) * 4 + zi) * embedding.shape[0]
    scalars = jnp.stack(
        [zi, ci, jnp.where(yi >= 1, 0, 1), jnp.where(yi == 3, 0, 1), jnp.where(yi >= 2, 0, 1), base]
    ).astype(jnp.int32)

    q_heads = query_rows.reshape(BLK, 8, HEAD_DIM).transpose(1, 0, 2)
    k_heads = key_rows.reshape(BLK, 4, HEAD_DIM).transpose(1, 0, 2)
    v_heads = value_rows.reshape(BLK, 4, HEAD_DIM).transpose(1, 0, 2)
    kv = jnp.stack([k_heads, v_heads], axis=1).reshape(8, BLK, HEAD_DIM)
    got = exchange(jnp.concatenate([q_heads, kv], axis=1), ("x", "core"))
    q = got[:, :BLK].reshape(4, SPAN, HEAD_DIM)
    own = got[:, BLK:].reshape(4 * SPAN, HEAD_DIM)

    swap = lambda a: lax.ppermute(a, "core", SWAP)
    own_pair = [own, swap(own)]
    got_y = []
    for k in (1, 3, 2):
        got_y.append(lax.ppermute(own, "y", ring(k)))
    down, up, far = got_y

    mine = []
    for s in (1, 2, 3):
        part = lax.dynamic_slice(out_weight, (ci * 512, ((zi + s) % 4) * COLS), (512, COLS))
        mine.append(lax.ppermute(part, "vocab", ring(s)))
    theirs = [swap(p) for p in mine]

    acc = attn_call(scalars, q, own_pair)
    acc = attn_call(scalars, q, [down, swap(down)], acc, at=2)
    out = attn_call(scalars, q, [up, swap(up), far, swap(far)], acc, at=3, last=True)
    att = exchange(out.reshape(32, BLK, HEAD_DIM), ("vocab", "x", "core"))

    res_pick = jnp.take(residual, pick_pos, axis=0).astype(f32)
    own_cols, zp = project(
        scalars, pick_pos, att, out_weight, mine + theirs,
        res_pick, post_gain[None], final_gain[None],
    )
    zr = exchange(zp, "vocab")
    square_sum = jnp.sum(zr[:, 18, :LOSS_TOKENS], axis=0)
    inv_rms = lax.rsqrt(square_sum / D + epsilon)[:, None]
    final_hidden = (residual.astype(f32) + own_cols * inv_rms * post_gain).astype(bf16)

    coded = jnp.stack([targets >> 14, (targets >> 7) & 127, targets & 127, loss_mask], axis=1)
    ext = jnp.pad(coded, ((0, 0), (0, EXT - 4))).astype(bf16)
    g = exchange(normalise(zr, ext), ("x", "y")).reshape(128, D + EXT)
    own_part, sib_part, rows = loss_parts(scalars, g, swap(g), embedding)

    row = rows[:2, :128] + swap(rows[:2, 128:])
    high = lax.reduce_precision(row, 8, 7)
    low = row - high
    info = jnp.stack([high[0], low[0], high[1], low[1]] + [jnp.zeros((128,), f32)] * 4)
    payload = join(own_part, swap(sib_part), info).reshape(64, 8, 2 * COLS + EXT)
    back = exchange(payload, ("vocab", "x", "y"))
    facts = jnp.sum(back[:, :4, 2 * COLS :].astype(f32), axis=0)
    totals, target_logit = facts[0] + facts[1], facts[2] + facts[3]
    masks = g[:, D + 3].astype(f32)
    loss = jnp.sum(masks * (jnp.log(totals) - target_logit)) / LOSS_TOKENS
    loss = loss + lax.ppermute(loss[None], "core", SWAP)[0]

    sums = jnp.sum(back[:, :, : 2 * COLS].astype(f32), axis=0)
    at = (xi * 4 + yi) * PICK
    my_total = lax.dynamic_slice(totals, (at,), (PICK,))[:, None]
    my_logit = lax.dynamic_slice(target_logit, (at,), (PICK,))[:, None]
    slope = 1.0 - (my_logit / logit_cap) ** 2
    grad = loss_mask.astype(f32)[:, None] * (sums[:, :COLS] / my_total - slope * sums[:, COLS:])
    return (final_hidden, loss, grad)


def solution(mesh):
    split = Mesh(
        mesh.devices.reshape(4, 4, 2, mesh.shape["vocab"]), ("x", "y", "core", "vocab")
    )

    return jax.shard_map(
        shards,
        mesh=split,
        in_specs=(
            P(CTX, "vocab"),
            P(CTX, "vocab"),
            P(CTX, "vocab"),
            P(CTX, "vocab"),
            P("vocab", None),
            P("vocab"),
            P("vocab"),
            P((*CTX, "vocab"), None),
            P(CTX),
            P(CTX),
            P(CTX),
        ),
        out_specs=(P(CTX, "vocab"), P(), P(CTX, "vocab")),
        check_vma=False,
    )
```

time: 269 us -> 260 us (0.967)
  Pallas kernels: 66.7 us -> 56.9 us
  blocking collectives: 44.2 us -> 52 us
  other arithmetic: 15.7 us -> 8.52 us
    all_to_all x2, blocking collectives: 44.2 us -> 52 us  [exchange(): return lax.all_to_all(pieces, axes, 0, 0, tiled=True)]
    pallas_call x4 -> x3, Pallas kernels: 34.6 us -> 26.9 us  [attn_call(): pl.pallas_call(kernel, out_shape=out_shape, grid_spec=pltpu.PrefetchScala...]
    another operation x6 -> x0, other arithmetic: 3.78 us -> none  [the longest x5 3.09 us: shards(): i32 = lambda *v: jnp.stack([jnp.asarray(e, jnp.int32) for e in v])]
    all_to_all x3, waiting for transfers between devices: 39 us -> 35.3 us  [exchange(): return lax.all_to_all(pieces, axes, 0, 0, tiled=True)]
    ppermute x10, starting transfers between devices: 15.6 us -> 12.1 us  [shards(): swap = lambda a: lax.ppermute(a, 'core', SWAP)]
    squeeze x1 -> x0, local copies, waits for them, and re-layouts: 3.27 us -> none  [shards(): summed = (parts[0].astype(f32) + swap(parts[1]).astype(f32)).astype(bf16)]
    ppermute x6, waiting for transfers between devices: 31.6 us -> 34.8 us  [the longest x3 26.7 us: shards(): mine.append(lax.ppermute(part, 'vocab', ring(s)))]
    pallas_call x1 -> x2, Pallas kernels: 19.4 us -> 19.4 us  [the longest x1 14.9 us: loss_parts(): pl.pallas_call(loss_kernel, out_shape=(jax.ShapeDtypeStruct((4, 128, 2 *...]
  transfers between devices with their start and end apart: 20 -> 20, of which waited for: 8 -> 9; matrix products, arithmetic and copies ran while one was open for 7% -> 6% of each run, Pallas kernels for 13% -> 10%
where the time goes in v2:
time: 260 us; the launch traced here: 258 us
  waiting for transfers between devices  78.2 us (30%)
  Pallas kernels  56.9 us (22%)
  blocking collectives  52 us (20%)
  starting transfers between devices  40.8 us (16%)
  local copies, waits for them, and re-layouts  18.6 us (7%)
  other arithmetic  8.52 us (3%)
  between operations  3.3 us (1%)
    all_to_all x2, blocking collectives, exchange(): return lax.all_to_all(pieces, axes, 0, 0, tiled=True)  52 us
    all_to_all x3, waiting for transfers between devices, exchange(): return lax.all_to_all(pieces, axes, 0, 0, tiled=True)  35.3 us
    pallas_call x3, Pallas kernels, attn_call(): pl.pallas_call(kernel, out_shape=out_shape, grid_spec=pltpu.PrefetchScala...  26.9 us
    ppermute x3, waiting for transfers between devices, shards(): mine.append(lax.ppermute(part, 'vocab', ring(s)))  26.7 us
    pallas_call x1, Pallas kernels, loss_parts(): pl.pallas_call(loss_kernel, out_shape=(jax.ShapeDtypeStruct((4, 128, 2 *...  14.9 us
    all_to_all x3, starting transfers between devices, exchange(): return lax.all_to_all(pieces, axes, 0, 0, tiled=True)  12.5 us
    ppermute x10, starting transfers between devices, shards(): swap = lambda a: lax.ppermute(a, 'core', SWAP)  12.1 us
    ppermute x3, starting transfers between devices, shards(): mine.append(lax.ppermute(part, 'vocab', ring(s)))  8.77 us
  transfers between devices with their start and end apart: 20, of which 9 were waited for; matrix products, arithmetic and copies ran while one was open for 6% of the time, Pallas kernels for 10%

profile of v2, /device:TPU:1, one launch (start us, length us, event | category | flops | bytes accessed | tf_op | source)
XLA Modules:
  0.0 258.3 jit_solution(12068389670809614187)
XLA Ops:
  3.4 20.5 %all_to_all.25 = bf16[8,512,128]{2,1,0:T(8,128)(2,1)S(1)} all-to-all(bf16[8,512,128]{2,1,0:T(8,128)(2,1)S(1)} %pad_maximum_fusion), channel_id=1, replica_groups=mesh['x'=4,'y'=4,'core'=2,'vocab'=4] {'x','core'}, dimensions={0} | all-to-all | bytes 2097152 | tf_op jit(solution)/shard_map/all_to_all | solution.py:39
  31.1 7.5 %collective-permute-done.4.refs_0_ = bf16[2048,128]{1,0:T(8,128)(2,1)S(1)} collective-permute-done((bf16[2048,128]{1,0:T(8,128)(2,1)S(1)}, bf16[2048,128]{1,0:T(8,128)(2,1)S(1)}, u32[]{:S(2)}, u32[]{:S(2)}) %collective-permute-start.4) | collective-permute-done | bytes 524320 | tf_op jit(solution)/shard_map/ppermute | solution.py:424
  40.7 4.0 %fusion.11 = (bf16[512,1152]{1,0:T(8,128)(2,1)}, bf16[512,1152]{1,0:T(8,128)(2,1)}, bf16[512,1152]{1,0:T(8,128)(2,1)}) fusion(bf16[1024,4608]{1,0:T(8,128)(2,1)} %w_ref.1, s32[]{:T(128)S(6)} %select_n.55, s32[]{:T(128)S(6)} %select_n.61, s32[]{:T(128)S(6)} %select_n.59, s32[]{:T(128)S(6)} %select_n.57), kind=kLoop, calls=%fused_computation.39 | loop fusion | bytes 7077904 | tf_op jit(solution)/shard_map/dynamic_slice | solution.py:429
  47.0 3.3 %collective-permute-start.8 = (bf16[512,1152]{1,0:T(8,128)(2,1)}, bf16[512,1152]{1,0:T(8,128)(2,1)}, u32[]{:S(2)}, u32[]{:S(2)}) collective-permute-start(bf16[512,1152]{1,0:T(8,128)(2,1)} %get-tuple-element.17), channel_id=1, source_target_pairs={{0,2},{1,3},{2,0},{3,1},{4,6},{5,7},{6,4},{7,5},{8,10},{9,11},{10,... | collective-permute-start | bytes 3538952 | tf_op jit(solution)/shard_map/ppermute | solution.py:430
  53.6 9.1 %shard_map.130.refs_2_ = f32[4,512,256]{2,1,0:T(8,128)} custom-call(s32[6]{0:T(128)} %stack.62.sc_ref, bf16[4,512,128]{2,1,0:T(8,128)(2,1)} %bitcast.51, bf16[2048,128]{1,0:T(8,128)(2,1)} %bitcast.58, bf16[2048,128]{1,0:T(8,128)(2,1)} %copy-done.14), custom_call_target="tpu_custom_call" | custom-call | flops 5000000000 | bytes 4000000 | tf_op jit(solution)/shard_map/pallas_call | solution.py:192
  62.7 3.8 %collective-permute-start.9 = (bf16[512,1152]{1,0:T(8,128)(2,1)}, bf16[512,1152]{1,0:T(8,128)(2,1)}, u32[]{:S(2)}, u32[]{:S(2)}) collective-permute-start(bf16[512,1152]{1,0:T(8,128)(2,1)} %get-tuple-element.16), channel_id=1, source_target_pairs={{0,3},{1,0},{2,1},{3,2},{4,7},{5,4},{6,5},{7,6},{8,11},{9,8},{10,9... | collective-permute-start | bytes 3538952 | tf_op jit(solution)/shard_map/ppermute | solution.py:430
  66.6 7.3 %shard_map.131.refs_4_ = f32[4,512,256]{2,1,0:T(8,128)} custom-call(s32[6]{0:T(128)} %stack.62.sc_ref, bf16[4,512,128]{2,1,0:T(8,128)(2,1)} %bitcast.52, bf16[2048,128]{1,0:T(8,128)(2,1)} %copy-done.13, bf16[2048,128]{1,0:T(8,128)(2,1)} %collective-permute-done.5.refs_1_, f32[4,512,256]{2,1,0:T(8,128)} %shard_map.130.refs_2_), custom_call_target="tpu_custom_call" | custom-call | flops 5000000000 | bytes 4000000 | tf_op jit(solution)/shard_map/pallas_call | solution.py:192
  74.7 10.6 %shard_map.132 = bf16[4,4,512,128]{3,2,1,0:T(8,128)(2,1)} custom-call(s32[6]{0:T(128)} %stack.62.sc_ref, bf16[4,512,128]{2,1,0:T(8,128)(2,1)} %bitcast.53, bf16[2048,128]{1,0:T(8,128)(2,1)} %copy-done.11, bf16[2048,128]{1,0:T(8,128)(2,1)} %collective-permute-done.1.refs_1_, bf16[2048,128]{1,0:T(8,128)(2,1)} %copy-done.12, bf16[2048,128]{1,0:T(8,128)(2,1)} %copy-done.15, ...), custom_call_target="tpu_custom_call" | custom-call | flops 10000000000 | bytes 4000000 | tf_op jit(solution)/shard_map/pallas_call | solution.py:192
  85.3 4.1 %all-to-all-start.1 = ((bf16[32,256,128]{2,1,0:T(8,128)(2,1)}), bf16[32,256,128]{2,1,0:T(8,128)(2,1)S(1)}, u32[]{:S(2)}, u32[]{:S(2)}) async-start(bf16[32,256,128]{2,1,0:T(8,128)(2,1)} %bitcast.47), calls=%async_computation.1 | async-start | bytes 4194304 | tf_op jit(solution)/shard_map/all_to_all | solution.py:39
  91.0 26.7 %collective-permute-done.8.a2 = bf16[512,1152]{1,0:T(8,128)(2,1)} collective-permute-done((bf16[512,1152]{1,0:T(8,128)(2,1)}, bf16[512,1152]{1,0:T(8,128)(2,1)}, u32[]{:S(2)}, u32[]{:S(2)}) %collective-permute-start.8) | collective-permute-done | bytes 1179680 | tf_op jit(solution)/shard_map/ppermute | solution.py:430
  117.7 2.4 collective-permute-start.11
  126.0 8.3 %shard_map.133 = (f32[256,1152]{1,0:T(8,128)}, f32[4,24,1152]{2,1,0:T(8,128)}) custom-call(s32[6]{0:T(128)} %stack.62.sc_ref, s32[8]{0:T(128)} %pick_ref.1, bf16[32,256,128]{2,1,0:T(8,128)(2,1)} %copy-done.1, bf16[1024,4608]{1,0:T(8,128)(2,1)} %w_ref.1, bf16[512,1152]{1,0:T(8,128)(2,1)} %collective-permute-done.7.a1, ...), custom_call_target="tpu_custom_call" | custom-call | tf_op jit(solution)/shard_map/pallas_call | solution.py:259
  134.2 3.5 %all-to-all-start.2 = ((f32[4,24,1152]{2,1,0:T(8,128)}), f32[4,24,1152]{2,1,0:T(8,128)S(1)}, u32[]{:S(2)}, u32[]{:S(2)}) async-start(f32[4,24,1152]{2,1,0:T(8,128)} %get-tuple-element.9), calls=%async_computation.2 | async-start | bytes 884736 | tf_op jit(solution)/shard_map/all_to_all | solution.py:39
  138.7 7.1 %all-to-all-done.2.zr_ref = f32[4,24,1152]{2,1,0:T(8,128)S(1)} async-done(((f32[4,24,1152]{2,1,0:T(8,128)}), f32[4,24,1152]{2,1,0:T(8,128)S(1)}, u32[]{:S(2)}, u32[]{:S(2)}) %all-to-all-start.2) | async-done | bytes 442400 | tf_op jit(solution)/shard_map/all_to_all | solution.py:39
  149.0 31.5 %all_to_all.26 = bf16[16,8,4736]{2,1,0:T(8,128)(2,1)S(1)} all-to-all(bf16[16,8,4736]{2,1,0:T(8,128)(2,1)} %shard_map.134), channel_id=1, replica_groups=mesh['x'=4,'y'=4,'core'=2,'vocab'=4] {'x','y'}, dimensions={0} | all-to-all | bytes 2424832 | tf_op jit(solution)/shard_map/all_to_all | solution.py:39
  180.5 2.8 %collective-permute-start.13 = (bf16[128,4736]{1,0:T(8,128)(2,1)S(1)}, bf16[128,4736]{1,0:T(8,128)(2,1)S(1)}, u32[]{:S(2)}, u32[]{:S(2)}) collective-permute-start(bf16[128,4736]{1,0:T(8,128)(2,1)S(1)} %bitcast.44), channel_id=1, source_target_pairs={{0,4},{4,0},{1,5},{5,1},{2,6},{6,2},{3,7},{7,3},{8,12},{12,8},{9,1... | collective-permute-start | bytes 3637256 | tf_op jit(solution)/shard_map/ppermute | solution.py:420
  183.3 2.5 collective-permute-done.13.s_ref
  186.8 14.9 %shard_map.135 = (bf16[4,128,2304]{2,1,0:T(8,128)(2,1)}, bf16[4,128,2304]{2,1,0:T(8,128)(2,1)}, f32[8,256]{1,0:T(8,128)}) custom-call(s32[6]{0:T(128)} %stack.62.sc_ref, bf16[128,4736]{1,0:T(8,128)(2,1)} %bitcast.45, bf16[128,4736]{1,0:T(8,128)(2,1)} %copy-done.5, bf16[1024,4608]{1,0:T(8,128)(2,1)} %e_ref.1), custom_call_target="tpu_custom_call" | custom-call | tf_op jit(solution)/shard_map/pallas_call | solution.py:357
  202.9 3.5 %collective-permute-done.15 = f32[2,128]{1,0:T(2,128)S(1)} collective-permute-done((f32[2,128]{1,0:T(2,128)S(1)}, f32[2,128]{1,0:T(2,128)S(1)}, u32[]{:S(2)}, u32[]{:S(2)}) %collective-permute-start.15) | collective-permute-done | bytes 1056 | tf_op jit(solution)/shard_map/ppermute | solution.py:420
  209.2 4.5 %shard_map.136 = bf16[4,128,2432]{2,1,0:T(8,128)(2,1)} custom-call(bf16[4,128,2304]{2,1,0:T(8,128)(2,1)} %get-tuple-element.10.own_ref, bf16[4,128,2304]{2,1,0:T(8,128)(2,1)} %copy-done.3, f32[8,128]{1,0:T(8,128)} %stack.72.info_ref), custom_call_target="tpu_custom_call" | custom-call | tf_op jit(solution)/shard_map/pallas_call | solution.py:393
  213.7 4.8 %all-to-all-start.4 = ((bf16[64,8,2432]{2,1,0:T(8,128)(2,1)}), bf16[64,8,2432]{2,1,0:T(8,128)(2,1)S(1)}, u32[]{:S(2)}, u32[]{:S(2)}) async-start(bf16[64,8,2432]{2,1,0:T(8,128)(2,1)} %bitcast.43), calls=%async_computation.4 | async-start | bytes 4980736 | tf_op jit(solution)/shard_map/all_to_all | solution.py:39
  219.3 2.5 add_convert_fusion
  222.7 28.2 %all-to-all-done.4 = bf16[64,8,2432]{2,1,0:T(8,128)(2,1)S(1)} async-done(((bf16[64,8,2432]{2,1,0:T(8,128)(2,1)}), bf16[64,8,2432]{2,1,0:T(8,128)(2,1)S(1)}, u32[]{:S(2)}, u32[]{:S(2)}) %all-to-all-start.4) | async-done | bytes 2490400 | tf_op jit(solution)/shard_map/all_to_all | solution.py:39
  252.3 3.2 %collective-permute-start.16 = (f32[1]{0:T(128)}, f32[1]{0:T(128)}, u32[]{:S(2)}, u32[]{:S(2)}) collective-permute-start(f32[1]{0:T(128)} %bitcast.22), channel_id=1, source_target_pairs={{0,4},{4,0},{1,5},{5,1},{2,6},{6,2},{3,7},{7,3},{8,12},{12,8},{9,1... | collective-permute-start | bytes 20 | tf_op jit(solution)/shard_map/ppermute | solution.py:463
  (97 shorter events, 38.5 us)
Async XLA Ops:
  24.8 19.9 %copy-start.6 = (bf16[8,256,128]{2,1,0:T(8,128)(2,1)}, bf16[8,256,128]{2,1,0:T(8,128)(2,1)S(1)}, u32[]{:S(2)}) copy-start(bf16[8,256,128]{2,1,0:T(8,128)(2,1)S(1)} %get-tuple-element.19) | copy-start | bytes 1572868
  24.8 13.8 %collective-permute-start.4 = (bf16[2048,128]{1,0:T(8,128)(2,1)S(1)}, bf16[2048,128]{1,0:T(8,128)(2,1)S(1)}, u32[]{:S(2)}, u32[]{:S(2)}) collective-permute-start(bf16[2048,128]{1,0:T(8,128)(2,1)S(1)} %bitcast.54), channel_id=1, source_target_pairs={{0,8},{8,16},{16,24},{24,0},{1,9},{9,17},{17,25},{25,1},{2,10},{10... | collective-permute-start | bytes 1572872 | tf_op jit(solution)/shard_map/ppermute | solution.py:424
  26.1 20.9 %collective-permute-start = (bf16[2048,128]{1,0:T(8,128)(2,1)S(1)}, bf16[2048,128]{1,0:T(8,128)(2,1)S(1)}, u32[]{:S(2)}, u32[]{:S(2)}) collective-permute-start(bf16[2048,128]{1,0:T(8,128)(2,1)S(1)} %bitcast.55), channel_id=1, source_target_pairs={{0,24},{8,0},{16,8},{24,16},{1,25},{9,1},{17,9},{25,17},{2,26},{10... | collective-permute-start | bytes 1572872 | tf_op jit(solution)/shard_map/ppermute | solution.py:424
  27.5 23.4 %collective-permute-start.2 = (bf16[2048,128]{1,0:T(8,128)(2,1)S(1)}, bf16[2048,128]{1,0:T(8,128)(2,1)S(1)}, u32[]{:S(2)}, u32[]{:S(2)}) collective-permute-start(bf16[2048,128]{1,0:T(8,128)(2,1)S(1)} %bitcast.56), channel_id=1, source_target_pairs={{0,16},{8,24},{16,0},{24,8},{1,17},{9,25},{17,1},{25,9},{2,18},{10... | collective-permute-start | bytes 1572872 | tf_op jit(solution)/shard_map/ppermute | solution.py:424
  29.2 23.6 %collective-permute-start.6 = (bf16[2048,128]{1,0:T(8,128)(2,1)S(1)}, bf16[2048,128]{1,0:T(8,128)(2,1)S(1)}, u32[]{:S(2)}, u32[]{:S(2)}) collective-permute-start(bf16[2048,128]{1,0:T(8,128)(2,1)S(1)} %bitcast.57), channel_id=1, source_target_pairs={{0,4},{4,0},{1,5},{5,1},{2,6},{6,2},{3,7},{7,3},{8,12},{12,8},{9,1... | collective-permute-start | bytes 1572872 | tf_op jit(solution)/shard_map/ppermute | solution.py:420
  38.6 24.2 %collective-permute-start.5 = (bf16[2048,128]{1,0:T(8,128)(2,1)S(1)}, bf16[2048,128]{1,0:T(8,128)(2,1)}, u32[]{:S(2)}, u32[]{:S(2)}) collective-permute-start(bf16[2048,128]{1,0:T(8,128)(2,1)S(1)} %collective-permute-done.4.refs_0_), channel_id=1, source_target_pairs={{0,4},{4,0},{1,5},{5,1},{2,6},{6,2},{3,7},{7,3},{8,12},{12,8},{9,1... | collective-permute-start | bytes 1572872 | tf_op jit(solution)/shard_map/ppermute | solution.py:420
  44.7 46.0 %collective-permute-start.7 = (bf16[512,1152]{1,0:T(8,128)(2,1)}, bf16[512,1152]{1,0:T(8,128)(2,1)}, u32[]{:S(2)}, u32[]{:S(2)}) collective-permute-start(bf16[512,1152]{1,0:T(8,128)(2,1)} %get-tuple-element.18), channel_id=1, source_target_pairs={{0,1},{1,2},{2,3},{3,0},{4,5},{5,6},{6,7},{7,4},{8,9},{9,10},{10,1... | collective-permute-start | bytes 3538952 | tf_op jit(solution)/shard_map/ppermute | solution.py:430
  47.0 15.7 %copy-start.11 = (bf16[2048,128]{1,0:T(8,128)(2,1)}, bf16[2048,128]{1,0:T(8,128)(2,1)S(1)}, u32[]{:S(2)}) copy-start(bf16[2048,128]{1,0:T(8,128)(2,1)S(1)} %collective-permute-done.refs_0_) | copy-start | bytes 1572868
  47.0 70.7 %collective-permute-start.8 = (bf16[512,1152]{1,0:T(8,128)(2,1)}, bf16[512,1152]{1,0:T(8,128)(2,1)}, u32[]{:S(2)}, u32[]{:S(2)}) collective-permute-start(bf16[512,1152]{1,0:T(8,128)(2,1)} %get-tuple-element.17), channel_id=1, source_target_pairs={{0,2},{1,3},{2,0},{3,1},{4,6},{5,7},{6,4},{7,5},{8,10},{9,11},{10,... | collective-permute-start | bytes 3538952 | tf_op jit(solution)/shard_map/ppermute | solution.py:430
  50.9 22.9 %collective-permute-start.1 = (bf16[2048,128]{1,0:T(8,128)(2,1)S(1)}, bf16[2048,128]{1,0:T(8,128)(2,1)}, u32[]{:S(2)}, u32[]{:S(2)}) collective-permute-start(bf16[2048,128]{1,0:T(8,128)(2,1)S(1)} %collective-permute-done.refs_0_), channel_id=1, source_target_pairs={{0,4},{4,0},{1,5},{5,1},{2,6},{6,2},{3,7},{7,3},{8,12},{12,8},{9,1... | collective-permute-start | bytes 1572872 | tf_op jit(solution)/shard_map/ppermute | solution.py:420
  52.8 21.0 %collective-permute-start.3 = (bf16[2048,128]{1,0:T(8,128)(2,1)S(1)}, bf16[2048,128]{1,0:T(8,128)(2,1)S(1)}, u32[]{:S(2)}, u32[]{:S(2)}) collective-permute-start(bf16[2048,128]{1,0:T(8,128)(2,1)S(1)} %collective-permute-done.2.refs_2_), channel_id=1, source_target_pairs={{0,4},{4,0},{1,5},{5,1},{2,6},{6,2},{3,7},{7,3},{8,12},{12,8},{9,1... | collective-permute-start | bytes 1572872 | tf_op jit(solution)/shard_map/ppermute | solution.py:420
  62.7 57.4 %collective-permute-start.9 = (bf16[512,1152]{1,0:T(8,128)(2,1)}, bf16[512,1152]{1,0:T(8,128)(2,1)}, u32[]{:S(2)}, u32[]{:S(2)}) collective-permute-start(bf16[512,1152]{1,0:T(8,128)(2,1)} %get-tuple-element.16), channel_id=1, source_target_pairs={{0,3},{1,0},{2,1},{3,2},{4,7},{5,4},{6,5},{7,6},{8,11},{9,8},{10,9... | collective-permute-start | bytes 3538952 | tf_op jit(solution)/shard_map/ppermute | solution.py:430
  85.3 34.8 %copy-start.16 = (s32[8]{0:T(128)S(1)}, s32[8]{0:T(128)}, u32[]{:S(2)}) copy-start(s32[8]{0:T(128)} %param.20) | copy-start | bytes 100
  85.3 34.9 %copy-start.9 = (s32[8]{0:T(128)S(1)}, s32[8]{0:T(128)}, u32[]{:S(2)}) copy-start(s32[8]{0:T(128)} %pick_ref.1) | copy-start | bytes 100
  85.3 39.3 %all-to-all-start.1 = ((bf16[32,256,128]{2,1,0:T(8,128)(2,1)}), bf16[32,256,128]{2,1,0:T(8,128)(2,1)S(1)}, u32[]{:S(2)}, u32[]{:S(2)}) async-start(bf16[32,256,128]{2,1,0:T(8,128)(2,1)} %bitcast.47), calls=%async_computation.1 | async-start | bytes 4194304 | tf_op jit(solution)/shard_map/all_to_all | solution.py:39
  90.7 32.0 %collective-permute-start.10 = (bf16[512,1152]{1,0:T(8,128)(2,1)}, bf16[512,1152]{1,0:T(8,128)(2,1)}, u32[]{:S(2)}, u32[]{:S(2)}) collective-permute-start(bf16[512,1152]{1,0:T(8,128)(2,1)} %collective-permute-done.7.a1), channel_id=1, source_target_pairs={{0,4},{4,0},{1,5},{5,1},{2,6},{6,2},{3,7},{7,3},{8,12},{12,8},{9,1... | collective-permute-start | bytes 3538952 | tf_op jit(solution)/shard_map/ppermute | solution.py:420
  117.7 5.2 %collective-permute-start.11 = (bf16[512,1152]{1,0:T(8,128)(2,1)}, bf16[512,1152]{1,0:T(8,128)(2,1)}, u32[]{:S(2)}, u32[]{:S(2)}) collective-permute-start(bf16[512,1152]{1,0:T(8,128)(2,1)} %collective-permute-done.8.a2), channel_id=1, source_target_pairs={{0,4},{4,0},{1,5},{5,1},{2,6},{6,2},{3,7},{7,3},{8,12},{12,8},{9,1... | collective-permute-start | bytes 3538952 | tf_op jit(solution)/shard_map/ppermute | solution.py:420
  120.1 4.5 %collective-permute-start.12 = (bf16[512,1152]{1,0:T(8,128)(2,1)}, bf16[512,1152]{1,0:T(8,128)(2,1)}, u32[]{:S(2)}, u32[]{:S(2)}) collective-permute-start(bf16[512,1152]{1,0:T(8,128)(2,1)} %collective-permute-done.9.a3), channel_id=1, source_target_pairs={{0,4},{4,0},{1,5},{5,1},{2,6},{6,2},{3,7},{7,3},{8,12},{12,8},{9,1... | collective-permute-start | bytes 3538952 | tf_op jit(solution)/shard_map/ppermute | solution.py:420
  134.2 11.6 %all-to-all-start.2 = ((f32[4,24,1152]{2,1,0:T(8,128)}), f32[4,24,1152]{2,1,0:T(8,128)S(1)}, u32[]{:S(2)}, u32[]{:S(2)}) async-start(f32[4,24,1152]{2,1,0:T(8,128)} %get-tuple-element.9), calls=%async_computation.2 | async-start | bytes 884736 | tf_op jit(solution)/shard_map/all_to_all | solution.py:39
  180.5 5.3 %collective-permute-start.13 = (bf16[128,4736]{1,0:T(8,128)(2,1)S(1)}, bf16[128,4736]{1,0:T(8,128)(2,1)S(1)}, u32[]{:S(2)}, u32[]{:S(2)}) collective-permute-start(bf16[128,4736]{1,0:T(8,128)(2,1)S(1)} %bitcast.44), channel_id=1, source_target_pairs={{0,4},{4,0},{1,5},{5,1},{2,6},{6,2},{3,7},{7,3},{8,12},{12,8},{9,1... | collective-permute-start | bytes 3637256 | tf_op jit(solution)/shard_map/ppermute | solution.py:420
  201.7 6.1 %collective-permute-start.14 = (bf16[4,128,2304]{2,1,0:T(8,128)(2,1)}, bf16[4,128,2304]{2,1,0:T(8,128)(2,1)S(1)}, u32[]{:S(2)}, u32[]{:S(2)}) collective-permute-start(bf16[4,128,2304]{2,1,0:T(8,128)(2,1)} %get-tuple-element.11), channel_id=1, source_target_pairs={{0,4},{4,0},{1,5},{5,1},{2,6},{6,2},{3,7},{7,3},{8,12},{12,8},{9,1... | collective-permute-start | bytes 7077896 | tf_op jit(solution)/shard_map/ppermute | solution.py:420
  202.7 3.7 %collective-permute-start.15 = (f32[2,128]{1,0:T(2,128)S(1)}, f32[2,128]{1,0:T(2,128)S(1)}, u32[]{:S(2)}, u32[]{:S(2)}) collective-permute-start(f32[2,128]{1,0:T(2,128)S(1)} %slice.59), channel_id=1, source_target_pairs={{0,4},{4,0},{1,5},{5,1},{2,6},{6,2},{3,7},{7,3},{8,12},{12,8},{9,1... | collective-permute-start | bytes 3080 | tf_op jit(solution)/shard_map/ppermute | solution.py:420
  213.7 37.2 %all-to-all-start.4 = ((bf16[64,8,2432]{2,1,0:T(8,128)(2,1)}), bf16[64,8,2432]{2,1,0:T(8,128)(2,1)S(1)}, u32[]{:S(2)}, u32[]{:S(2)}) async-start(bf16[64,8,2432]{2,1,0:T(8,128)(2,1)} %bitcast.43), calls=%async_computation.4 | async-start | bytes 4980736 | tf_op jit(solution)/shard_map/all_to_all | solution.py:39
  252.3 4.3 %collective-permute-start.16 = (f32[1]{0:T(128)}, f32[1]{0:T(128)}, u32[]{:S(2)}, u32[]{:S(2)}) collective-permute-start(f32[1]{0:T(128)} %bitcast.22), channel_id=1, source_target_pairs={{0,4},{4,0},{1,5},{5,1},{2,6},{6,2},{3,7},{7,3},{8,12},{12,8},{9,1... | collective-permute-start | bytes 20 | tf_op jit(solution)/shard_map/ppermute | solution.py:463
  (13 other events, 56.0 us)

commit v3 on v2

--- a/solution.py
+++ b/solution.py
@@ -35,6 +35,37 @@
 SWAP = [(0, 1), (1, 0)]
 
 
+def in_vmem(a):
+    return pltpu.with_memory_space_constraint(a, pltpu.MemorySpace.VMEM)
+
+
+def params(mib):
+    return pltpu.CompilerParams(
+        dimension_semantics=("arbitrary",), vmem_limit_bytes=mib * 1024 * 1024
+    )
+
+
+VMEM_SPEC = pl.BlockSpec(memory_space=pltpu.MemorySpace.VMEM)
+
+
+def pack_kernel(q_ref, k_ref, v_ref, out_ref):
+    for h, other in enumerate((k_ref, v_ref)):
+        out_ref[h, :BLK, :] = q_ref[:, h * HEAD_DIM : (h + 1) * HEAD_DIM]
+        out_ref[h, BLK:, :] = other[...]
+
+
+def pack(q, k, v):
+    one = pl.BlockSpec((BLK, HEAD_DIM), lambda i: (0, i))
+    return pl.pallas_call(
+        pack_kernel,
+        out_shape=jax.ShapeDtypeStruct((8, SPAN, HEAD_DIM), bf16),
+        grid=(4,),
+        in_specs=[pl.BlockSpec((BLK, 2 * HEAD_DIM), lambda i: (0, i)), one, one],
+        out_specs=pl.BlockSpec((2, SPAN, HEAD_DIM), lambda i: (i, 0, 0)),
+        compiler_params=params(16),
+    )(q, k, v)
+
+
 def exchange(pieces, axes):
     return lax.all_to_all(pieces, axes, 0, 0, tiled=True)
 
@@ -62,13 +93,30 @@
     return copies
 
 
+def in_turn(tasks):
+    results = []
+    raw = tasks[0][0]()
+    for n, (_, after) in enumerate(tasks):
+        ahead = tasks[n + 1][0]() if n + 1 < len(tasks) else None
+        results.append(after(weigh(raw)))
+        raw = ahead
+    return results
+
+
+def times_values(p, v):
+    return jnp.dot(p.astype(bf16), v, preferred_element_type=f32), lane_sums(p)
+
+
 def seen(q, buf, first, span, valid=None):
-    p = weigh(scores(q, buf[0, pl.ds(first, span), :]))
-    if valid is not None:
-        half = span // 2
-        p = jnp.concatenate([p[:, :half], jnp.where(valid, p[:, half:], 0.0)], axis=1)
-    v = buf[1, pl.ds(first, span), :]
-    return jnp.dot(p.astype(bf16), v, preferred_element_type=f32), lane_sums(p)
+    def before():
+        return scores(q, buf[0, pl.ds(first, span), :])
+
+    def after(p):
+        if valid is not None:
+            p = jnp.where(valid, p, 0.0)
+        return times_values(p, buf[1, pl.ds(first, span), :])
+
+    return before, after
 
 
 def attn_own_kernel(sc_ref, q_ref, a_ref, b_ref, acc_ref, buf, sem):
@@ -87,37 +135,42 @@
         tk = lax.broadcasted_iota(jnp.int32, (BLK, BLK), 1)
         causal = tk <= tq
         beyond = jnp.logical_and(jnp.logical_not(causal), has_edge)
+        q = [q_ref[0, pl.ds(r * BLK, BLK), :] for r in range(2)]
+
+        def corner(r):
+            def before():
+                raw = scores(q[r], buf[0, pl.ds(diag0 + r * BLK, BLK), :])
+                if earlier:
+                    edge = scores(q[r], buf[0, pl.ds(edge0 + r * BLK, BLK), :])
+                    raw = jnp.where(causal, raw, edge)
+                return raw
+
+            def after(p):
+                pd = jnp.where(causal, p, 0.0)
+                top, low = times_values(pd, buf[1, pl.ds(diag0 + r * BLK, BLK), :])
+                if earlier:
+                    pe = jnp.where(beyond, p, 0.0)
+                    more = times_values(pe, buf[1, pl.ds(edge0 + r * BLK, BLK), :])
+                    top, low = top + more[0], low + more[1]
+                return top, low
+
+            return before, after
+
+        tasks = [corner(0), corner(1), seen(q[1], buf, diag0, BLK)]
+        if earlier:
+            tasks.append(seen(q[0], buf, edge0 + BLK, BLK, has_edge))
+            tasks.append(seen(q_ref[0], buf, (i - 1) * SPAN, SPAN))
+        parts = in_turn(tasks)
         for r in range(2):
-            q = q_ref[0, pl.ds(r * BLK, BLK), :]
-            raw = scores(q, buf[0, pl.ds(diag0 + r * BLK, BLK), :])
-            if earlier:
-                raw = jnp.where(causal, raw, scores(q, buf[0, pl.ds(edge0 + r * BLK, BLK), :]))
-            p = weigh(raw)
-            pd = jnp.where(causal, p, 0.0)
-            top = jnp.dot(
-                pd.astype(bf16), buf[1, pl.ds(diag0 + r * BLK, BLK), :], preferred_element_type=f32
-            )
-            low = lane_sums(pd)
-            if earlier:
-                pe = jnp.where(beyond, p, 0.0)
-                top += jnp.dot(
-                    pe.astype(bf16), buf[1, pl.ds(edge0 + r * BLK, BLK), :],
-                    preferred_element_type=f32,
-                )
-                low += lane_sums(pe)
-                more = seen(q, buf, (i - 1) * SPAN, SPAN)
-                top, low = top + more[0], low + more[1]
-            if r == 1:
-                more = seen(q, buf, diag0, BLK)
-                top, low = top + more[0], low + more[1]
-            elif earlier:
-                p = jnp.where(has_edge, weigh(scores(q, buf[0, pl.ds(edge0 + BLK, BLK), :])), 0.0)
-                top += jnp.dot(
-                    p.astype(bf16), buf[1, pl.ds(edge0 + BLK, BLK), :], preferred_element_type=f32
-                )
-                low += lane_sums(p)
-            acc_ref[0, pl.ds(r * BLK, BLK), :HEAD_DIM] = top
-            acc_ref[0, pl.ds(r * BLK, BLK), HEAD_DIM:] = low
+            for lane in range(2):
+                total = parts[r][lane]
+                if r == 1:
+                    total += parts[2][lane]
+                if earlier and r == 0:
+                    total += parts[3][lane]
+                if earlier:
+                    total += parts[4][lane][r * BLK : (r + 1) * BLK]
+                acc_ref[0, pl.ds(r * BLK, BLK), lane * HEAD_DIM : (lane + 1) * HEAD_DIM] = total
 
     pl.when(i == 0)(lambda: body(False))
     pl.when(i > 0)(lambda: body(True))
@@ -137,29 +190,30 @@
             copy.wait()
         acc_ref[...] = in_ref[...]
 
+    def add(base, tasks):
+        for lane, lanes in enumerate((slice(0, HEAD_DIM), slice(HEAD_DIM, 2 * HEAD_DIM))):
+            if lane == 0:
+                parts = in_turn(tasks)
+            total = base[0, :, lanes]
+            for part in parts:
+                total += part[lane]
+            acc_ref[0, :, lanes] = total
+
     for n in range(chunks):
 
         @pl.when(jnp.logical_and(i == 0, sc_ref[at + n] == 0))
         def _():
-            for r in range(2):
-                rows = pl.ds(r * BLK, BLK)
-                top, low = seen(q_ref[0, rows, :], buf.at[n], 0, SPAN)
-                acc_ref[0, rows, :HEAD_DIM] += top
-                acc_ref[0, rows, HEAD_DIM:] += low
+            add(acc_ref, [seen(q_ref[0], buf.at[n], 0, SPAN)])
 
     @pl.when(i > 0)
     def _():
-        for r in range(2):
-            rows = pl.ds(r * BLK, BLK)
-            q = q_ref[0, rows, :]
-            top, low = in_ref[0, rows, :HEAD_DIM], in_ref[0, rows, HEAD_DIM:]
-            for n in range(chunks):
-                newest = i - sc_ref[at + n]
-                first = jnp.maximum(newest - 1, 0) * SPAN
-                more = seen(q, buf.at[n], first, 2 * SPAN, newest > 0)
-                top, low = top + more[0], low + more[1]
-            acc_ref[0, rows, :HEAD_DIM] = top
-            acc_ref[0, rows, HEAD_DIM:] = low
+        tasks = []
+        for n in range(chunks):
+            newest = i - sc_ref[at + n]
+            first = jnp.maximum(newest - 1, 0) * SPAN
+            tasks.append(seen(q_ref[0], buf.at[n], first, SPAN))
+            tasks.append(seen(q_ref[0], buf.at[n], first + SPAN, SPAN, newest > 0))
+        add(in_ref, tasks)
 
     if last:
         whole = jnp.sum(acc_ref[0, :, HEAD_DIM:], axis=1, keepdims=True)
@@ -187,7 +241,7 @@
         ]
     if last:
         out_spec = pl.BlockSpec((4, 1, SPAN, HEAD_DIM), lambda i, sc: (0, i, 0, 0))
-        out_shape = jax.ShapeDtypeStruct((4, 4, SPAN, HEAD_DIM), bf16)
+        out_shape = pltpu.MemorySpace.HBM((4, 4, SPAN, HEAD_DIM), bf16)
         scratch = scratch + [pltpu.VMEM((1, SPAN, 2 * HEAD_DIM), f32)]
     return pl.pallas_call(
         kernel,
@@ -202,7 +256,7 @@
         cost_estimate=pl.CostEstimate(
             flops=5_000_000_000 * chunks, transcendentals=0, bytes_accessed=4_000_000
         ),
-        compiler_params=pltpu.CompilerParams(dimension_semantics=("arbitrary",)),
+        compiler_params=params(20),
     )(scalars, *args)
 
 
@@ -215,32 +269,19 @@
 
 def proj_kernel(
     sc_ref, pick_ref, att_ref, w_ref, a1, a2, a3, b1, b2, b3, rp_ref, pg_ref, fg_ref,
-    own_ref, zp_ref, abuf, wbuf, asem, wsem,
+    own_ref, zp_ref,
 ):
     zi, ci = sc_ref[0], sc_ref[1]
     heads = [zi * 2, zi * 2 + 1]
     heads += [((zi - s + 4) % 4) * 2 + ci for s in (1, 2, 3)]
     heads += [((zi - s + 4) % 4) * 2 + 1 - ci for s in (1, 2, 3)]
-    col = pl.multiple_of(zi * COLS, 128)
-    src = [w_ref.at[pl.ds(0, 512), pl.ds(col, COLS)], w_ref.at[pl.ds(512, 512), pl.ds(col, COLS)]]
-    src += [a1, a2, a3, b1, b2, b3]
-    acopies, wcopies = [], []
+    weights = [w_ref.at[:512], w_ref.at[512:], a1, a2, a3, b1, b2, b3]
+    total = None
     for n in range(8):
-        acopies.append(
-            pltpu.make_async_copy(att_ref.at[pl.ds(heads[n] * 4, 4)], abuf.at[n], asem.at[n])
-        )
-        wcopies.append(pltpu.make_async_copy(src[n], wbuf.at[n], wsem.at[n]))
-        acopies[n].start()
-        wcopies[n].start()
-    for n in range(8):
-        acopies[n].wait()
-        wcopies[n].wait()
-        lhs = jnp.concatenate([abuf[n, h] for h in range(4)], axis=1)
-        part = jnp.dot(lhs, wbuf[n], preferred_element_type=f32)
-        if n == 0:
-            own_ref[...] = part
-        else:
-            own_ref[...] += part
+        lhs = jnp.concatenate([att_ref[heads[n] * 4 + h] for h in range(4)], axis=1)
+        part = jnp.dot(lhs, weights[n][...], preferred_element_type=f32)
+        total = part if total is None else total + part
+    own_ref[...] = total
     own = own_ref[...]
     squares = row_of_sums(lane_sums(own * own))
     for z in range(4):
@@ -254,28 +295,22 @@
 
 
 def project(scalars, pick, att, w, parts, res_pick, pg, fg):
-    hbm = pl.BlockSpec(memory_space=pltpu.MemorySpace.HBM)
     whole = lambda *dims: pl.BlockSpec(dims, lambda i, *sc: (0,) * len(dims))
     return pl.pallas_call(
         proj_kernel,
         out_shape=(
-            jax.ShapeDtypeStruct((BLK, COLS), f32),
-            jax.ShapeDtypeStruct((4, 24, COLS), f32),
+            pltpu.MemorySpace.HBM((BLK, COLS), f32),
+            pltpu.MemorySpace.HBM((4, 24, COLS), f32),
         ),
         grid_spec=pltpu.PrefetchScalarGridSpec(
             num_scalar_prefetch=2,
             grid=(1,),
-            in_specs=[hbm] * 8 + [whole(PICK, COLS), whole(1, COLS), whole(1, COLS)],
+            in_specs=[VMEM_SPEC] * 8
+            + [whole(PICK, COLS), whole(1, COLS), whole(1, COLS)],
             out_specs=(whole(BLK, COLS), whole(4, 24, COLS)),
-            scratch_shapes=[
-                pltpu.VMEM((8, 4, BLK, HEAD_DIM), bf16),
-                pltpu.VMEM((8, 512, COLS), bf16),
-                pltpu.SemaphoreType.DMA((8,)),
-                pltpu.SemaphoreType.DMA((8,)),
-            ],
-        ),
-        compiler_params=pltpu.CompilerParams(dimension_semantics=("arbitrary",)),
-    )(scalars, pick, att, w, *parts, res_pick, pg, fg)
+        ),
+        compiler_params=params(20),
+    )(scalars, pick, in_vmem(att), in_vmem(w), *[in_vmem(p) for p in parts], res_pick, pg, fg)
 
 
 def norm_kernel(zr_ref, ext_ref, out_ref):
@@ -298,11 +333,14 @@
 
 def normalise(zr, ext):
     return pl.pallas_call(
-        norm_kernel, out_shape=jax.ShapeDtypeStruct((16, PICK, D + EXT), bf16)
-    )(zr, ext)
-
-
-def loss_kernel(sc_ref, g_ref, s_ref, e_ref, own_ref, sib_ref, row_ref, nbuf, acc, sums):
+        norm_kernel,
+        out_shape=jax.ShapeDtypeStruct((16, PICK, D + EXT), bf16),
+        in_specs=[VMEM_SPEC, pl.BlockSpec((PICK, EXT), lambda: (0, 0))],
+        compiler_params=pltpu.CompilerParams(vmem_limit_bytes=16 * 1024 * 1024),
+    )(in_vmem(zr), ext)
+
+
+def loss_kernel(sc_ref, g_ref, s_ref, e_ref, own_ref, sib_ref, nbuf, acc, sums):
     j = pl.program_id(0)
 
     @pl.when(j == 0)
@@ -337,9 +375,18 @@
 
     @pl.when(j == 3)
     def _():
+        facts = []
         for part in range(2):
-            row_ref[part : part + 1] = row_of_sums(sums[part] + both[part])[:1]
-        row_ref[2:] = jnp.zeros((6, LOSS_TOKENS), f32)
+            row = row_of_sums(sums[part] + both[part])[:1]
+            high = row.astype(bf16).astype(f32)
+            facts += [high, row - high]
+        none = jnp.zeros((4, 128), f32)
+        mine = jnp.concatenate([r[:, :128] for r in facts] + [none], axis=0)
+        theirs = jnp.concatenate([none] + [r[:, 128:] for r in facts], axis=0)
+        for ref, info in ((own_ref, mine), (sib_ref, theirs)):
+            tall = jnp.concatenate([info] * 16, axis=0).astype(bf16)
+            for z in range(4):
+                ref[z, :, 2 * COLS :] = tall
         for part in range(2):
             for z in range(4):
                 cols = slice(z * COLS, (z + 1) * COLS)
@@ -357,46 +404,26 @@
     return pl.pallas_call(
         loss_kernel,
         out_shape=(
-            jax.ShapeDtypeStruct((4, 128, 2 * COLS), bf16),
-            jax.ShapeDtypeStruct((4, 128, 2 * COLS), bf16),
-            jax.ShapeDtypeStruct((8, LOSS_TOKENS), f32),
+            jax.ShapeDtypeStruct((4, 128, 2 * COLS + EXT), bf16),
+            jax.ShapeDtypeStruct((4, 128, 2 * COLS + EXT), bf16),
         ),
         grid_spec=pltpu.PrefetchScalarGridSpec(
             num_scalar_prefetch=1,
             grid=(4,),
             in_specs=[
-                whole(128, D + EXT),
-                whole(128, D + EXT),
+                VMEM_SPEC,
+                VMEM_SPEC,
                 pl.BlockSpec((BLK, D), lambda i, sc: (i, 0)),
             ],
-            out_specs=(
-                whole(4, 128, 2 * COLS), whole(4, 128, 2 * COLS), whole(8, LOSS_TOKENS),
-            ),
+            out_specs=(whole(4, 128, 2 * COLS + EXT), whole(4, 128, 2 * COLS + EXT)),
             scratch_shapes=[
                 pltpu.VMEM((LOSS_TOKENS, D + EXT), bf16),
                 pltpu.VMEM((2 * LOSS_TOKENS, D), f32),
                 pltpu.VMEM((2, LOSS_TOKENS, 128), f32),
             ],
         ),
-        compiler_params=pltpu.CompilerParams(dimension_semantics=("arbitrary",)),
-    )(scalars, g, s, emb)
-
-
-def join_kernel(own_ref, sib_ref, info_ref, out_ref):
-    out_ref[0, :, : 2 * COLS] = (own_ref[0].astype(f32) + sib_ref[0].astype(f32)).astype(bf16)
-    for n in range(16):
-        out_ref[0, n * 8 : (n + 1) * 8, 2 * COLS :] = info_ref[...].astype(bf16)
-
-
-def join(own, sib, info):
-    block = pl.BlockSpec((1, 128, 2 * COLS), lambda z: (z, 0, 0))
-    return pl.pallas_call(
-        join_kernel,
-        out_shape=jax.ShapeDtypeStruct((4, 128, 2 * COLS + EXT), bf16),
-        grid=(4,),
-        in_specs=[block, block, pl.BlockSpec((8, EXT), lambda z: (0, 0))],
-        out_specs=pl.BlockSpec((1, 128, 2 * COLS + EXT), lambda z: (z, 0, 0)),
-    )(own, sib, info)
+        compiler_params=params(44),
+    )(scalars, in_vmem(g), in_vmem(s), emb)
 
 
 def shards(
@@ -409,11 +436,8 @@
         [zi, ci, jnp.where(yi >= 1, 0, 1), jnp.where(yi == 3, 0, 1), jnp.where(yi >= 2, 0, 1), base]
     ).astype(jnp.int32)
 
-    q_heads = query_rows.reshape(BLK, 8, HEAD_DIM).transpose(1, 0, 2)
-    k_heads = key_rows.reshape(BLK, 4, HEAD_DIM).transpose(1, 0, 2)
-    v_heads = value_rows.reshape(BLK, 4, HEAD_DIM).transpose(1, 0, 2)
-    kv = jnp.stack([k_heads, v_heads], axis=1).reshape(8, BLK, HEAD_DIM)
-    got = exchange(jnp.concatenate([q_heads, kv], axis=1), ("x", "core"))
+    packed = pack(query_rows, key_rows, value_rows)
+    got = exchange(packed, ("x", "core"))
     q = got[:, :BLK].reshape(4, SPAN, HEAD_DIM)
     own = got[:, BLK:].reshape(4 * SPAN, HEAD_DIM)
 
@@ -434,10 +458,11 @@
     acc = attn_call(scalars, q, [down, swap(down)], acc, at=2)
     out = attn_call(scalars, q, [up, swap(up), far, swap(far)], acc, at=3, last=True)
     att = exchange(out.reshape(32, BLK, HEAD_DIM), ("vocab", "x", "core"))
+    kept = lax.dynamic_slice(out_weight, (0, zi * COLS), (1024, COLS))
 
     res_pick = jnp.take(residual, pick_pos, axis=0).astype(f32)
     own_cols, zp = project(
-        scalars, pick_pos, att, out_weight, mine + theirs,
+        scalars, pick_pos, att, kept, mine + theirs,
         res_pick, post_gain[None], final_gain[None],
     )
     zr = exchange(zp, "vocab")
@@ -447,17 +472,14 @@
 
     coded = jnp.stack([targets >> 14, (targets >> 7) & 127, targets & 127, loss_mask], axis=1)
     ext = jnp.pad(coded, ((0, 0), (0, EXT - 4))).astype(bf16)
-    g = exchange(normalise(zr, ext), ("x", "y")).reshape(128, D + EXT)
-    own_part, sib_part, rows = loss_parts(scalars, g, swap(g), embedding)
-
-    row = rows[:2, :128] + swap(rows[:2, 128:])
-    high = lax.reduce_precision(row, 8, 7)
-    low = row - high
-    info = jnp.stack([high[0], low[0], high[1], low[1]] + [jnp.zeros((128,), f32)] * 4)
-    payload = join(own_part, swap(sib_part), info).reshape(64, 8, 2 * COLS + EXT)
-    back = exchange(payload, ("vocab", "x", "y"))
-    facts = jnp.sum(back[:, :4, 2 * COLS :].astype(f32), axis=0)
-    totals, target_logit = facts[0] + facts[1], facts[2] + facts[3]
+    normed = normalise(zr, ext)
+    g = exchange(normed, ("x", "y")).reshape(128, D + EXT)
+    own_part, sib_part = loss_parts(scalars, g, swap(g), embedding)
+    payload = (own_part.astype(f32) + swap(sib_part).astype(f32)).astype(bf16)
+    back = exchange(payload.reshape(64, 8, 2 * COLS + EXT), ("vocab", "x", "y"))
+    facts = jnp.sum(back[:, :, 2 * COLS :].astype(f32), axis=0)
+    totals = facts[0] + facts[1] + facts[4] + facts[5]
+    target_logit = facts[2] + facts[3] + facts[6] + facts[7]
     masks = g[:, D + 3].astype(f32)
     loss = jnp.sum(masks * (jnp.log(totals) - target_logit)) / LOSS_TOKENS
     loss = loss + lax.ppermute(loss[None], "core", SWAP)[0]

time: 260 us -> 253 us (0.973)
  Pallas kernels: 56.9 us -> 37.4 us
  waiting for transfers between devices: 78.2 us -> 93.5 us
  local copies, waits for them, and re-layouts: 18.6 us -> 15.3 us
    ppermute x3, waiting for transfers between devices: 26.7 us -> 39.6 us  [shards(): mine.append(lax.ppermute(part, 'vocab', ring(s)))]
    pallas_call x3, Pallas kernels: 26.9 us -> 16.9 us  [attn_call(): pl.pallas_call(kernel, out_shape=out_shape, grid_spec=pltpu.PrefetchScala...]
    pallas_call x2, Pallas kernels: 12.8 us -> 8.4 us  [the longest x1 8.02 us: project(): pl.pallas_call(proj_kernel, out_shape=(pltpu.MemorySpace.HBM((BLK, COLS),...]
    pallas_call x1, Pallas kernels: 14.9 us -> 11.9 us  [loss_parts(): pl.pallas_call(loss_kernel, out_shape=(jax.ShapeDtypeStruct((4, 128, 2 *...]
    all_to_all x3, waiting for transfers between devices: 35.3 us -> 38.1 us  [exchange(): return lax.all_to_all(pieces, axes, 0, 0, tiled=True)]
    ppermute x10 -> x9, waiting for transfers between devices: 8.01 us -> 6.91 us  [shards(): swap = lambda a: lax.ppermute(a, 'core', SWAP)]
    ppermute x10 -> x9, starting transfers between devices: 12.1 us -> 11 us  [shards(): swap = lambda a: lax.ppermute(a, 'core', SWAP)]
    unnamed x34 -> x32, local copies, waits for them, and re-layouts: 6.16 us -> 5.08 us
  transfers between devices with their start and end apart: 20 -> 19, of which waited for: 9 -> 7; matrix products, arithmetic and copies ran while one was open for 6% -> 7% of each run, Pallas kernels for 10% -> 7%
where the time goes in v3:
time: 253 us; the launch traced here: 252 us
  waiting for transfers between devices  93.5 us (37%)
  blocking collectives  51.6 us (20%)
  starting transfers between devices  40.8 us (16%)
  Pallas kernels  37.4 us (15%)
  local copies, waits for them, and re-layouts  15.3 us (6%)
  other arithmetic  9.9 us (4%)
  between operations  3.42 us (1%)
    all_to_all x2, blocking collectives, exchange(): return lax.all_to_all(pieces, axes, 0, 0, tiled=True)  51.6 us
    ppermute x3, waiting for transfers between devices, shards(): mine.append(lax.ppermute(part, 'vocab', ring(s)))  39.6 us
    all_to_all x3, waiting for transfers between devices, exchange(): return lax.all_to_all(pieces, axes, 0, 0, tiled=True)  38.1 us
    pallas_call x3, Pallas kernels, attn_call(): pl.pallas_call(kernel, out_shape=out_shape, grid_spec=pltpu.PrefetchScala...  16.9 us
    all_to_all x3, starting transfers between devices, exchange(): return lax.all_to_all(pieces, axes, 0, 0, tiled=True)  13.9 us
    pallas_call x1, Pallas kernels, loss_parts(): pl.pallas_call(loss_kernel, out_shape=(jax.ShapeDtypeStruct((4, 128, 2 *...  11.9 us
    ppermute x9, starting transfers between devices, shards(): swap = lambda a: lax.ppermute(a, 'core', SWAP)  11 us
    ppermute x3, waiting for transfers between devices, shards(): got_y.append(lax.ppermute(own, 'y', ring(k)))  8.84 us
  transfers between devices with their start and end apart: 19, of which 7 were waited for; matrix products, arithmetic and copies ran while one was open for 7% of the time, Pallas kernels for 7%

profile of v3, /device:TPU:1, one launch (start us, length us, event | category | flops | bytes accessed | tf_op | source)
XLA Modules:
  0.0 251.9 jit_solution(7299812791291423917)
XLA Ops:
  4.0 20.5 %all_to_all.25 = bf16[8,512,128]{2,1,0:T(8,128)(2,1)S(1)} all-to-all(bf16[8,512,128]{2,1,0:T(8,128)(2,1)S(1)} %shard_map.130), channel_id=1, replica_groups=mesh['x'=4,'y'=4,'core'=2,'vocab'=4] {'x','core'}, dimensions={0} | all-to-all | bytes 2097152 | tf_op jit(solution)/shard_map/all_to_all | solution.py:70
  30.4 8.1 %collective-permute-done.4.refs_0_ = bf16[2048,128]{1,0:T(8,128)(2,1)S(1)} collective-permute-done((bf16[2048,128]{1,0:T(8,128)(2,1)S(1)}, bf16[2048,128]{1,0:T(8,128)(2,1)S(1)}, u32[]{:S(2)}, u32[]{:S(2)}) %collective-permute-start.4) | collective-permute-done | bytes 524320 | tf_op jit(solution)/shard_map/ppermute | solution.py:448
  38.4 2.1 collective-permute-start.5
  40.6 3.9 %fusion.13 = (bf16[512,1152]{1,0:T(8,128)(2,1)}, bf16[512,1152]{1,0:T(8,128)(2,1)}, bf16[512,1152]{1,0:T(8,128)(2,1)}) fusion(bf16[1024,4608]{1,0:T(8,128)(2,1)} %param.15, s32[]{:T(128)S(6)} %select_n.59, s32[]{:T(128)S(6)} %select_n.65, s32[]{:T(128)S(6)} %select_n.61, s32[]{:T(128)S(6)} %select_n.63), kind=kLoop, calls=%fused_computation.39 | loop fusion | bytes 7077904 | tf_op jit(solution)/shard_map/dynamic_slice | solution.py:453
  46.2 3.4 %collective-permute-start.8 = (bf16[512,1152]{1,0:T(8,128)(2,1)}, bf16[512,1152]{1,0:T(8,128)(2,1)}, u32[]{:S(2)}, u32[]{:S(2)}) collective-permute-start(bf16[512,1152]{1,0:T(8,128)(2,1)} %get-tuple-element.16), channel_id=1, source_target_pairs={{0,2},{1,3},{2,0},{3,1},{4,6},{5,7},{6,4},{7,5},{8,10},{9,11},{10,... | collective-permute-start | bytes 3538952 | tf_op jit(solution)/shard_map/ppermute | solution.py:454
  52.8 5.1 %shard_map.131.refs_2_ = f32[4,512,256]{2,1,0:T(8,128)S(1)} custom-call(s32[6]{0:T(128)S(1)} %stack.47.sc_ref, bf16[4,512,128]{2,1,0:T(8,128)(2,1)S(1)} %bitcast.32, bf16[2048,128]{1,0:T(8,128)(2,1)S(1)} %bitcast.39, bf16[2048,128]{1,0:T(8,128)(2,1)} %collective-permute-done.6.b_ref), custom_call_target="tpu_custom_call" | custom-call | flops 5000000000 | bytes 4000000 | tf_op jit(solution)/shard_map/pallas_call | solution.py:246
  57.9 3.8 %collective-permute-start.9 = (bf16[512,1152]{1,0:T(8,128)(2,1)}, bf16[512,1152]{1,0:T(8,128)(2,1)}, u32[]{:S(2)}, u32[]{:S(2)}) collective-permute-start(bf16[512,1152]{1,0:T(8,128)(2,1)} %get-tuple-element.14), channel_id=1, source_target_pairs={{0,3},{1,0},{2,1},{3,2},{4,7},{5,4},{6,5},{7,6},{8,11},{9,8},{10,9... | collective-permute-start | bytes 3538952 | tf_op jit(solution)/shard_map/ppermute | solution.py:454
  61.7 4.3 %shard_map.132.refs_4_ = f32[4,512,256]{2,1,0:T(8,128)S(1)} custom-call(s32[6]{0:T(128)S(1)} %stack.47.sc_ref, bf16[4,512,128]{2,1,0:T(8,128)(2,1)S(1)} %bitcast.33, bf16[2048,128]{1,0:T(8,128)(2,1)S(1)} %collective-permute-done.4.refs_0_, bf16[2048,128]{1,0:T(8,128)(2,1)} %collective-permute-done.5.refs_1_, f32[4,512,256]{2,1,0:T(8,128)S(1)} %shard_map.131.refs_2_), custom_call_target="tpu_custom_call" | custom-call | flops 5000000000 | bytes 4000000 | tf_op jit(solution)/shard_map/pallas_call | solution.py:246
  66.0 7.5 %shard_map.133 = bf16[4,4,512,128]{3,2,1,0:T(8,128)(2,1)} custom-call(s32[6]{0:T(128)S(1)} %stack.47.sc_ref, bf16[4,512,128]{2,1,0:T(8,128)(2,1)S(1)} %bitcast.34, bf16[2048,128]{1,0:T(8,128)(2,1)S(1)} %collective-permute-done.refs_0_, bf16[2048,128]{1,0:T(8,128)(2,1)S(1)} %collective-permute-done.1.refs_1_, ...), custom_call_target="tpu_custom_call" | custom-call | flops 10000000000 | bytes 4000000 | tf_op jit(solution)/shard_map/pallas_call | solution.py:246
  73.6 4.8 %all-to-all-start.1 = ((bf16[32,256,128]{2,1,0:T(8,128)(2,1)}), bf16[32,256,128]{2,1,0:T(8,128)(2,1)}, u32[]{:S(2)}, u32[]{:S(2)}) async-start(bf16[32,256,128]{2,1,0:T(8,128)(2,1)} %bitcast.41), calls=%async_computation.1 | async-start | bytes 4194304 | tf_op jit(solution)/shard_map/all_to_all | solution.py:70
  78.9 39.6 %collective-permute-done.8.a2 = bf16[512,1152]{1,0:T(8,128)(2,1)} collective-permute-done((bf16[512,1152]{1,0:T(8,128)(2,1)}, bf16[512,1152]{1,0:T(8,128)(2,1)}, u32[]{:S(2)}, u32[]{:S(2)}) %collective-permute-start.8) | collective-permute-done | bytes 1179680 | tf_op jit(solution)/shard_map/ppermute | solution.py:454
  121.9 2.3 gather_fusion
  128.9 8.0 %shard_map.134 = (f32[256,1152]{1,0:T(8,128)}, f32[4,24,1152]{2,1,0:T(8,128)}) custom-call(s32[6]{0:T(128)S(1)} %copy-done.5, s32[8]{0:T(128)S(1)} %copy-done.8, bf16[32,256,128]{2,1,0:T(8,128)(2,1)} %all-to-all-done.1.att_ref, bf16[1024,1152]{1,0:T(8,128)(2,1)S(1)} %constant_dynamic-slice_fusion.2.w_ref, bf16[512,1152]{1,0:T(8,128)(2,1)S(1)} %collective-permute-done.7.a1, ...), custom_call_target="tpu_custom_call" | custom-call | tf_op jit(solution)/shard_map/pallas_call | solution.py:299
  136.9 3.5 %all-to-all-start.2 = ((f32[4,24,1152]{2,1,0:T(8,128)}), f32[4,24,1152]{2,1,0:T(8,128)S(1)}, u32[]{:S(2)}, u32[]{:S(2)}) async-start(f32[4,24,1152]{2,1,0:T(8,128)} %get-tuple-element.8), calls=%async_computation.2 | async-start | bytes 884736 | tf_op jit(solution)/shard_map/all_to_all | solution.py:70
  142.0 6.6 %all-to-all-done.2.zr_ref = f32[4,24,1152]{2,1,0:T(8,128)S(1)} async-done(((f32[4,24,1152]{2,1,0:T(8,128)}), f32[4,24,1152]{2,1,0:T(8,128)S(1)}, u32[]{:S(2)}, u32[]{:S(2)}) %all-to-all-start.2) | async-done | bytes 442400 | tf_op jit(solution)/shard_map/all_to_all | solution.py:70
  148.9 31.0 %all_to_all.26 = bf16[16,8,4736]{2,1,0:T(8,128)(2,1)S(1)} all-to-all(bf16[16,8,4736]{2,1,0:T(8,128)(2,1)S(1)} %shard_map.135), channel_id=1, replica_groups=mesh['x'=4,'y'=4,'core'=2,'vocab'=4] {'x','y'}, dimensions={0} | all-to-all | bytes 2424832 | tf_op jit(solution)/shard_map/all_to_all | solution.py:70
  180.0 2.8 %collective-permute-start.13 = (bf16[128,4736]{1,0:T(8,128)(2,1)S(1)}, bf16[128,4736]{1,0:T(8,128)(2,1)S(1)}, u32[]{:S(2)}, u32[]{:S(2)}) collective-permute-start(bf16[128,4736]{1,0:T(8,128)(2,1)S(1)} %bitcast.29), channel_id=1, source_target_pairs={{0,4},{4,0},{1,5},{5,1},{2,6},{6,2},{3,7},{7,3},{8,12},{12,8},{9,1... | collective-permute-start | bytes 3637256 | tf_op jit(solution)/shard_map/ppermute | solution.py:444
  182.7 2.5 %collective-permute-done.13.s_ref = bf16[128,4736]{1,0:T(8,128)(2,1)S(1)} collective-permute-done((bf16[128,4736]{1,0:T(8,128)(2,1)S(1)}, bf16[128,4736]{1,0:T(8,128)(2,1)S(1)}, u32[]{:S(2)}, u32[]{:S(2)}) %collective-permute-start.13) | collective-permute-done | bytes 1212448 | tf_op jit(solution)/shard_map/ppermute | solution.py:444
  185.3 11.9 %shard_map.136 = (bf16[4,128,2432]{2,1,0:T(8,128)(2,1)S(1)}, bf16[4,128,2432]{2,1,0:T(8,128)(2,1)S(1)}) custom-call(s32[6]{0:T(128)S(1)} %copy-done.6, bf16[128,4736]{1,0:T(8,128)(2,1)S(1)} %bitcast.30, bf16[128,4736]{1,0:T(8,128)(2,1)S(1)} %collective-permute-done.13.s_ref, bf16[1024,4608]{1,0:T(8,128)(2,1)} %e_ref.1), custom_call_target="tpu_custom_call" | custom-call | tf_op jit(solution)/shard_map/pallas_call | solution.py:404
  197.6 4.4 %collective-permute-done.14 = bf16[4,128,2432]{2,1,0:T(8,128)(2,1)S(1)} collective-permute-done((bf16[4,128,2432]{2,1,0:T(8,128)(2,1)S(1)}, bf16[4,128,2432]{2,1,0:T(8,128)(2,1)S(1)}, u32[]{:S(2)}, u32[]{:S(2)}) %collective-permute-start.14) | collective-permute-done | bytes 2490400 | tf_op jit(solution)/shard_map/ppermute | solution.py:444
  201.9 2.0 add_convert_fusion
  204.0 5.7 %all-to-all-start.4 = ((bf16[64,8,2432]{2,1,0:T(8,128)(2,1)}), bf16[64,8,2432]{2,1,0:T(8,128)(2,1)}, u32[]{:S(2)}, u32[]{:S(2)}) async-start(bf16[64,8,2432]{2,1,0:T(8,128)(2,1)} %bitcast.40), calls=%async_computation.4 | async-start | bytes 4980736 | tf_op jit(solution)/shard_map/all_to_all | solution.py:70
  211.0 31.5 %all-to-all-done.4 = bf16[64,8,2432]{2,1,0:T(8,128)(2,1)} async-done(((bf16[64,8,2432]{2,1,0:T(8,128)(2,1)}), bf16[64,8,2432]{2,1,0:T(8,128)(2,1)}, u32[]{:S(2)}, u32[]{:S(2)}) %all-to-all-start.4) | async-done | bytes 2490400 | tf_op jit(solution)/shard_map/all_to_all | solution.py:70
  244.7 2.6 %collective-permute-start.15 = (f32[1]{0:T(128)}, f32[1]{0:T(128)}, u32[]{:S(2)}, u32[]{:S(2)}) collective-permute-start(f32[1]{0:T(128)} %bitcast.16), channel_id=1, source_target_pairs={{0,4},{4,0},{1,5},{5,1},{2,6},{6,2},{3,7},{7,3},{8,12},{12,8},{9,1... | collective-permute-start | bytes 20 | tf_op jit(solution)/shard_map/ppermute | solution.py:485
  (83 shorter events, 30.6 us)
Async XLA Ops:
  24.6 13.8 %collective-permute-start.4 = (bf16[2048,128]{1,0:T(8,128)(2,1)S(1)}, bf16[2048,128]{1,0:T(8,128)(2,1)S(1)}, u32[]{:S(2)}, u32[]{:S(2)}) collective-permute-start(bf16[2048,128]{1,0:T(8,128)(2,1)S(1)} %bitcast.35), channel_id=1, source_target_pairs={{0,8},{8,16},{16,24},{24,0},{1,9},{9,17},{17,25},{25,1},{2,10},{10... | collective-permute-start | bytes 1572872 | tf_op jit(solution)/shard_map/ppermute | solution.py:448
  25.9 20.2 %collective-permute-start.6 = (bf16[2048,128]{1,0:T(8,128)(2,1)S(1)}, bf16[2048,128]{1,0:T(8,128)(2,1)}, u32[]{:S(2)}, u32[]{:S(2)}) collective-permute-start(bf16[2048,128]{1,0:T(8,128)(2,1)S(1)} %bitcast.36), channel_id=1, source_target_pairs={{0,4},{4,0},{1,5},{5,1},{2,6},{6,2},{3,7},{7,3},{8,12},{12,8},{9,1... | collective-permute-start | bytes 1572872 | tf_op jit(solution)/shard_map/ppermute | solution.py:444
  27.3 22.3 %collective-permute-start = (bf16[2048,128]{1,0:T(8,128)(2,1)S(1)}, bf16[2048,128]{1,0:T(8,128)(2,1)S(1)}, u32[]{:S(2)}, u32[]{:S(2)}) collective-permute-start(bf16[2048,128]{1,0:T(8,128)(2,1)S(1)} %bitcast.37), channel_id=1, source_target_pairs={{0,24},{8,0},{16,8},{24,16},{1,25},{9,1},{17,9},{25,17},{2,26},{10... | collective-permute-start | bytes 1572872 | tf_op jit(solution)/shard_map/ppermute | solution.py:448
  28.6 22.2 %collective-permute-start.2 = (bf16[2048,128]{1,0:T(8,128)(2,1)S(1)}, bf16[2048,128]{1,0:T(8,128)(2,1)}, u32[]{:S(2)}, u32[]{:S(2)}) collective-permute-start(bf16[2048,128]{1,0:T(8,128)(2,1)S(1)} %bitcast.38), channel_id=1, source_target_pairs={{0,16},{8,24},{16,0},{24,8},{1,17},{9,25},{17,1},{25,9},{2,18},{10... | collective-permute-start | bytes 1572872 | tf_op jit(solution)/shard_map/ppermute | solution.py:448
  38.4 19.4 %collective-permute-start.5 = (bf16[2048,128]{1,0:T(8,128)(2,1)S(1)}, bf16[2048,128]{1,0:T(8,128)(2,1)}, u32[]{:S(2)}, u32[]{:S(2)}) collective-permute-start(bf16[2048,128]{1,0:T(8,128)(2,1)S(1)} %collective-permute-done.4.refs_0_), channel_id=1, source_target_pairs={{0,4},{4,0},{1,5},{5,1},{2,6},{6,2},{3,7},{7,3},{8,12},{12,8},{9,1... | collective-permute-start | bytes 1572872 | tf_op jit(solution)/shard_map/ppermute | solution.py:444
  44.4 34.0 %collective-permute-start.7 = (bf16[512,1152]{1,0:T(8,128)(2,1)}, bf16[512,1152]{1,0:T(8,128)(2,1)S(1)}, u32[]{:S(2)}, u32[]{:S(2)}) collective-permute-start(bf16[512,1152]{1,0:T(8,128)(2,1)} %get-tuple-element.15), channel_id=1, source_target_pairs={{0,1},{1,2},{2,3},{3,0},{4,5},{5,6},{6,7},{7,4},{8,9},{9,10},{10,1... | collective-permute-start | bytes 3538952 | tf_op jit(solution)/shard_map/ppermute | solution.py:454
  46.2 19.8 %copy-start.4 = (s32[6]{0:T(128)}, s32[6]{0:T(128)S(1)}, u32[]{:S(2)}) copy-start(s32[6]{0:T(128)S(1)} %stack.47.sc_ref) | copy-start | bytes 76
  46.2 72.4 %collective-permute-start.8 = (bf16[512,1152]{1,0:T(8,128)(2,1)}, bf16[512,1152]{1,0:T(8,128)(2,1)}, u32[]{:S(2)}, u32[]{:S(2)}) collective-permute-start(bf16[512,1152]{1,0:T(8,128)(2,1)} %get-tuple-element.16), channel_id=1, source_target_pairs={{0,2},{1,3},{2,0},{3,1},{4,6},{5,7},{6,4},{7,5},{8,10},{9,11},{10,... | collective-permute-start | bytes 3538952 | tf_op jit(solution)/shard_map/ppermute | solution.py:454
  49.6 16.4 %collective-permute-start.1 = (bf16[2048,128]{1,0:T(8,128)(2,1)S(1)}, bf16[2048,128]{1,0:T(8,128)(2,1)S(1)}, u32[]{:S(2)}, u32[]{:S(2)}) collective-permute-start(bf16[2048,128]{1,0:T(8,128)(2,1)S(1)} %collective-permute-done.refs_0_), channel_id=1, source_target_pairs={{0,4},{4,0},{1,5},{5,1},{2,6},{6,2},{3,7},{7,3},{8,12},{12,8},{9,1... | collective-permute-start | bytes 1572872 | tf_op jit(solution)/shard_map/ppermute | solution.py:444
  50.9 15.1 %collective-permute-start.3 = (bf16[2048,128]{1,0:T(8,128)(2,1)}, bf16[2048,128]{1,0:T(8,128)(2,1)S(1)}, u32[]{:S(2)}, u32[]{:S(2)}) collective-permute-start(bf16[2048,128]{1,0:T(8,128)(2,1)} %collective-permute-done.2.refs_2_), channel_id=1, source_target_pairs={{0,4},{4,0},{1,5},{5,1},{2,6},{6,2},{3,7},{7,3},{8,12},{12,8},{9,1... | collective-permute-start | bytes 1572872 | tf_op jit(solution)/shard_map/ppermute | solution.py:444
  57.9 62.0 %collective-permute-start.9 = (bf16[512,1152]{1,0:T(8,128)(2,1)}, bf16[512,1152]{1,0:T(8,128)(2,1)}, u32[]{:S(2)}, u32[]{:S(2)}) collective-permute-start(bf16[512,1152]{1,0:T(8,128)(2,1)} %get-tuple-element.14), channel_id=1, source_target_pairs={{0,3},{1,0},{2,1},{3,2},{4,7},{5,4},{6,5},{7,6},{8,11},{9,8},{10,9... | collective-permute-start | bytes 3538952 | tf_op jit(solution)/shard_map/ppermute | solution.py:454
  73.6 46.3 %copy-start.7 = (s32[8]{0:T(128)S(1)}, s32[8]{0:T(128)}, u32[]{:S(2)}) copy-start(s32[8]{0:T(128)} %pick_ref.1) | copy-start | bytes 100
  73.6 46.3 %copy-start.12 = (f32[1152]{0:T(1024)S(1)}, f32[1152]{0:T(1024)}, u32[]{:S(2)}) copy-start(f32[1152]{0:T(1024)} %param.16) | copy-start | bytes 13828
  73.6 46.3 %copy-start.14 = (f32[1152]{0:T(1024)S(1)}, f32[1152]{0:T(1024)}, u32[]{:S(2)}) copy-start(f32[1152]{0:T(1024)} %param.17) | copy-start | bytes 13828
  73.6 53.2 %all-to-all-start.1 = ((bf16[32,256,128]{2,1,0:T(8,128)(2,1)}), bf16[32,256,128]{2,1,0:T(8,128)(2,1)}, u32[]{:S(2)}, u32[]{:S(2)}) async-start(bf16[32,256,128]{2,1,0:T(8,128)(2,1)} %bitcast.41), calls=%async_computation.1 | async-start | bytes 4194304 | tf_op jit(solution)/shard_map/all_to_all | solution.py:70
  78.4 48.4 %collective-permute-start.10 = (bf16[512,1152]{1,0:T(8,128)(2,1)S(1)}, bf16[512,1152]{1,0:T(8,128)(2,1)}, u32[]{:S(2)}, u32[]{:S(2)}) collective-permute-start(bf16[512,1152]{1,0:T(8,128)(2,1)S(1)} %collective-permute-done.7.a1), channel_id=1, source_target_pairs={{0,4},{4,0},{1,5},{5,1},{2,6},{6,2},{3,7},{7,3},{8,12},{12,8},{9,1... | collective-permute-start | bytes 3538952 | tf_op jit(solution)/shard_map/ppermute | solution.py:444
  118.6 8.2 %collective-permute-start.11 = (bf16[512,1152]{1,0:T(8,128)(2,1)}, bf16[512,1152]{1,0:T(8,128)(2,1)}, u32[]{:S(2)}, u32[]{:S(2)}) collective-permute-start(bf16[512,1152]{1,0:T(8,128)(2,1)} %collective-permute-done.8.a2), channel_id=1, source_target_pairs={{0,4},{4,0},{1,5},{5,1},{2,6},{6,2},{3,7},{7,3},{8,12},{12,8},{9,1... | collective-permute-start | bytes 3538952 | tf_op jit(solution)/shard_map/ppermute | solution.py:444
  119.9 6.9 %collective-permute-start.12 = (bf16[512,1152]{1,0:T(8,128)(2,1)}, bf16[512,1152]{1,0:T(8,128)(2,1)}, u32[]{:S(2)}, u32[]{:S(2)}) collective-permute-start(bf16[512,1152]{1,0:T(8,128)(2,1)} %collective-permute-done.9.a3), channel_id=1, source_target_pairs={{0,4},{4,0},{1,5},{5,1},{2,6},{6,2},{3,7},{7,3},{8,12},{12,8},{9,1... | collective-permute-start | bytes 3538952 | tf_op jit(solution)/shard_map/ppermute | solution.py:444
  136.9 11.6 %all-to-all-start.2 = ((f32[4,24,1152]{2,1,0:T(8,128)}), f32[4,24,1152]{2,1,0:T(8,128)S(1)}, u32[]{:S(2)}, u32[]{:S(2)}) async-start(f32[4,24,1152]{2,1,0:T(8,128)} %get-tuple-element.8), calls=%async_computation.2 | async-start | bytes 884736 | tf_op jit(solution)/shard_map/all_to_all | solution.py:70
  140.4 44.8 %copy-start.6 = (s32[6]{0:T(128)S(1)}, s32[6]{0:T(128)}, u32[]{:S(2)}) copy-start(s32[6]{0:T(128)} %copy-done.4) | copy-start | bytes 76
  180.0 5.3 %collective-permute-start.13 = (bf16[128,4736]{1,0:T(8,128)(2,1)S(1)}, bf16[128,4736]{1,0:T(8,128)(2,1)S(1)}, u32[]{:S(2)}, u32[]{:S(2)}) collective-permute-start(bf16[128,4736]{1,0:T(8,128)(2,1)S(1)} %bitcast.29), channel_id=1, source_target_pairs={{0,4},{4,0},{1,5},{5,1},{2,6},{6,2},{3,7},{7,3},{8,12},{12,8},{9,1... | collective-permute-start | bytes 3637256 | tf_op jit(solution)/shard_map/ppermute | solution.py:444
  197.1 4.8 %collective-permute-start.14 = (bf16[4,128,2432]{2,1,0:T(8,128)(2,1)S(1)}, bf16[4,128,2432]{2,1,0:T(8,128)(2,1)S(1)}, u32[]{:S(2)}, u32[]{:S(2)}) collective-permute-start(bf16[4,128,2432]{2,1,0:T(8,128)(2,1)S(1)} %get-tuple-element.10), channel_id=1, source_target_pairs={{0,4},{4,0},{1,5},{5,1},{2,6},{6,2},{3,7},{7,3},{8,12},{12,8},{9,1... | collective-permute-start | bytes 7471112 | tf_op jit(solution)/shard_map/ppermute | solution.py:444
  204.0 38.5 %all-to-all-start.4 = ((bf16[64,8,2432]{2,1,0:T(8,128)(2,1)}), bf16[64,8,2432]{2,1,0:T(8,128)(2,1)}, u32[]{:S(2)}, u32[]{:S(2)}) async-start(bf16[64,8,2432]{2,1,0:T(8,128)(2,1)} %bitcast.40), calls=%async_computation.4 | async-start | bytes 4980736 | tf_op jit(solution)/shard_map/all_to_all | solution.py:70
  244.7 5.4 %collective-permute-start.15 = (f32[1]{0:T(128)}, f32[1]{0:T(128)}, u32[]{:S(2)}, u32[]{:S(2)}) collective-permute-start(f32[1]{0:T(128)} %bitcast.16), channel_id=1, source_target_pairs={{0,4},{4,0},{1,5},{5,1},{2,6},{6,2},{3,7},{7,3},{8,12},{12,8},{9,1... | collective-permute-start | bytes 20 | tf_op jit(solution)/shard_map/ppermute | solution.py:485
  (11 other events, 29.0 us)

commit v4 on v3

--- a/solution.py
+++ b/solution.py
@@ -16,6 +16,7 @@
 BLK = 256
 COLS = 1152
 EXT = 128
+WIDE = 2 * COLS + 2 * EXT
 LOSS_TOKENS = 256
 CTX = ("x", "y", "core")
 
@@ -62,7 +63,6 @@
         grid=(4,),
         in_specs=[pl.BlockSpec((BLK, 2 * HEAD_DIM), lambda i: (0, i)), one, one],
         out_specs=pl.BlockSpec((2, SPAN, HEAD_DIM), lambda i: (i, 0, 0)),
-        compiler_params=params(16),
     )(q, k, v)
 
 
@@ -380,11 +380,15 @@
             row = row_of_sums(sums[part] + both[part])[:1]
             high = row.astype(bf16).astype(f32)
             facts += [high, row - high]
-        none = jnp.zeros((4, 128), f32)
-        mine = jnp.concatenate([r[:, :128] for r in facts] + [none], axis=0)
-        theirs = jnp.concatenate([none] + [r[:, 128:] for r in facts], axis=0)
-        for ref, info in ((own_ref, mine), (sib_ref, theirs)):
-            tall = jnp.concatenate([info] * 16, axis=0).astype(bf16)
+        first = sc_ref[1] == 0
+        half = [jnp.concatenate([r[:, h : h + 128] for r in facts], axis=0) for h in (0, 128)]
+        info = jnp.concatenate(
+            [jnp.where(first, half[0], half[1]), jnp.where(first, half[1], half[0])], axis=0
+        )
+        tall = jnp.concatenate([info] * 16, axis=0)
+        slots = [jnp.where(first, tall, 0.0), jnp.where(first, 0.0, tall)]
+        tall = jnp.concatenate(slots, axis=1).astype(bf16)
+        for ref in (own_ref, sib_ref):
             for z in range(4):
                 ref[z, :, 2 * COLS :] = tall
         for part in range(2):
@@ -404,8 +408,8 @@
     return pl.pallas_call(
         loss_kernel,
         out_shape=(
-            jax.ShapeDtypeStruct((4, 128, 2 * COLS + EXT), bf16),
-            jax.ShapeDtypeStruct((4, 128, 2 * COLS + EXT), bf16),
+            jax.ShapeDtypeStruct((4, 128, WIDE), bf16),
+            jax.ShapeDtypeStruct((4, 128, WIDE), bf16),
         ),
         grid_spec=pltpu.PrefetchScalarGridSpec(
             num_scalar_prefetch=1,
@@ -415,7 +419,7 @@
                 VMEM_SPEC,
                 pl.BlockSpec((BLK, D), lambda i, sc: (i, 0)),
             ],
-            out_specs=(whole(4, 128, 2 * COLS + EXT), whole(4, 128, 2 * COLS + EXT)),
+            out_specs=(whole(4, 128, WIDE), whole(4, 128, WIDE)),
             scratch_shapes=[
                 pltpu.VMEM((LOSS_TOKENS, D + EXT), bf16),
                 pltpu.VMEM((2 * LOSS_TOKENS, D), f32),
@@ -424,6 +428,43 @@
         ),
         compiler_params=params(44),
     )(scalars, in_vmem(g), in_vmem(s), emb)
+
+
+def finish_kernel(sc_ref, back_ref, mask_ref, grad_ref, loss_ref):
+    def add(n, sums):
+        return sums + back_ref[n].astype(f32)
+
+    sums = lax.fori_loop(1, 64, add, back_ref[0].astype(f32), unroll=7)
+    facts = sums[:, 2 * COLS : 2 * COLS + EXT] + sums[:, 2 * COLS + EXT :]
+    totals = [facts[n : n + 1] + facts[n + 1 : n + 2] for n in (0, 4)]
+    hits = [facts[n : n + 1] + facts[n + 1 : n + 2] for n in (2, 6)]
+    masks = [mask_ref[n : n + 1] for n in range(2)]
+    loss = [jnp.sum(m * (jnp.log(t) - h)) for m, t, h in zip(masks, totals, hits)]
+    loss_ref[0, 0] = (loss[0] + loss[1]) / LOSS_TOKENS
+    lane = lax.broadcasted_iota(jnp.int32, (PICK, 128), 1)
+    row = lax.broadcasted_iota(jnp.int32, (PICK, 128), 0)
+    own = lane == row + sc_ref[6]
+
+    def mine(halves):
+        held = jnp.where(sc_ref[1] == 0, halves[0], halves[1])
+        return jnp.sum(jnp.where(own, held, 0.0), axis=1, keepdims=True)
+
+    bent = mine(hits) / logit_cap
+    slope = 1.0 - bent * bent
+    grad_ref[...] = mine(masks) * (sums[:, :COLS] / mine(totals) - slope * sums[:, COLS : 2 * COLS])
+
+
+def finish(scalars, back, masks):
+    return pl.pallas_call(
+        finish_kernel,
+        out_shape=(
+            jax.ShapeDtypeStruct((PICK, COLS), f32),
+            jax.ShapeDtypeStruct((1, 1), f32),
+        ),
+        in_specs=[pl.BlockSpec(memory_space=pltpu.MemorySpace.SMEM), VMEM_SPEC, VMEM_SPEC],
+        out_specs=(VMEM_SPEC, pl.BlockSpec(memory_space=pltpu.MemorySpace.SMEM)),
+        compiler_params=pltpu.CompilerParams(vmem_limit_bytes=16 * 1024 * 1024),
+    )(scalars, in_vmem(back), masks)
 
 
 def shards(
@@ -433,7 +474,7 @@
     xi, yi, ci, zi = (lax.axis_index(a) for a in ("x", "y", "core", "vocab"))
     base = (((xi * 4 + yi) * 2 + ci) * 4 + zi) * embedding.shape[0]
     scalars = jnp.stack(
-        [zi, ci, jnp.where(yi >= 1, 0, 1), jnp.where(yi == 3, 0, 1), jnp.where(yi >= 2, 0, 1), base]
+        [zi, ci, jnp.where(yi >= 1, 0, 1), jnp.where(yi == 3, 0, 1), jnp.where(yi >= 2, 0, 1), base, (xi * 4 + yi) * PICK]
     ).astype(jnp.int32)
 
     packed = pack(query_rows, key_rows, value_rows)
@@ -474,22 +515,14 @@
     ext = jnp.pad(coded, ((0, 0), (0, EXT - 4))).astype(bf16)
     normed = normalise(zr, ext)
     g = exchange(normed, ("x", "y")).reshape(128, D + EXT)
-    own_part, sib_part = loss_parts(scalars, g, swap(g), embedding)
+    sibling = swap(g)
+    own_part, sib_part = loss_parts(scalars, g, sibling, embedding)
     payload = (own_part.astype(f32) + swap(sib_part).astype(f32)).astype(bf16)
-    back = exchange(payload.reshape(64, 8, 2 * COLS + EXT), ("vocab", "x", "y"))
-    facts = jnp.sum(back[:, :, 2 * COLS :].astype(f32), axis=0)
-    totals = facts[0] + facts[1] + facts[4] + facts[5]
-    target_logit = facts[2] + facts[3] + facts[6] + facts[7]
-    masks = g[:, D + 3].astype(f32)
-    loss = jnp.sum(masks * (jnp.log(totals) - target_logit)) / LOSS_TOKENS
-    loss = loss + lax.ppermute(loss[None], "core", SWAP)[0]
-
-    sums = jnp.sum(back[:, :, : 2 * COLS].astype(f32), axis=0)
-    at = (xi * 4 + yi) * PICK
-    my_total = lax.dynamic_slice(totals, (at,), (PICK,))[:, None]
-    my_logit = lax.dynamic_slice(target_logit, (at,), (PICK,))[:, None]
-    slope = 1.0 - (my_logit / logit_cap) ** 2
-    grad = loss_mask.astype(f32)[:, None] * (sums[:, :COLS] / my_total - slope * sums[:, COLS:])
+    back = exchange(payload.reshape(64, 8, WIDE), ("vocab", "x", "y"))
+    held = [g[:, D + 3].astype(f32), sibling[:, D + 3].astype(f32)]
+    masks = jnp.where(ci == 0, jnp.stack(held), jnp.stack(held[::-1]))
+    grad, loss = finish(scalars, back, masks)
+    loss = loss[0, 0]
     return (final_hidden, loss, grad)
 
 

time: 253 us -> 247 us (0.976)
  Pallas kernels: 37.4 us -> 42.1 us
  starting transfers between devices: 40.8 us -> 37.5 us
  local copies, waits for them, and re-layouts: 15.3 us -> 12.5 us
    reduce_sum x3 -> x0, other arithmetic: 3.6 us -> none  [the longest x1 2.02 us: shards(): sums = jnp.sum(back[:, :, :2 * COLS].astype(f32), axis=0)]
    pallas_call x1, Pallas kernels: 0.38 us -> 3.41 us  [pack(): pl.pallas_call(pack_kernel, out_shape=jax.ShapeDtypeStruct((8, SPAN, HEAD...]
    unnamed x32 -> x26, local copies, waits for them, and re-layouts: 5.08 us -> 2.08 us
    ppermute x1 -> x0, starting transfers between devices: 2.59 us -> none  [shards(): loss = loss + lax.ppermute(loss[None], 'core', SWAP)[0]]
    pallas_call x1 -> x2, Pallas kernels: 11.9 us -> 13.5 us  [the longest x1 11.9 us: loss_parts(): pl.pallas_call(loss_kernel, out_shape=(jax.ShapeDtypeStruct((4, 128, WIDE...]
  transfers between devices with their start and end apart: 19 -> 18, of which waited for: 7 -> 7; matrix products, arithmetic and copies ran while one was open for 7% -> 7% of each run, Pallas kernels for 7% -> 7%
where the time goes in v4:
time: 247 us; the launch traced here: 246 us
  waiting for transfers between devices  91.9 us (37%)
  blocking collectives  51.8 us (21%)
  Pallas kernels  42.1 us (17%)
  starting transfers between devices  37.5 us (15%)
  local copies, waits for them, and re-layouts  12.5 us (5%)
  other arithmetic  8.73 us (4%)
    all_to_all x2, blocking collectives, exchange(): return lax.all_to_all(pieces, axes, 0, 0, tiled=True)  51.8 us
    ppermute x3, waiting for transfers between devices, shards(): mine.append(lax.ppermute(part, 'vocab', ring(s)))  39.7 us
    all_to_all x3, waiting for transfers between devices, exchange(): return lax.all_to_all(pieces, axes, 0, 0, tiled=True)  36.4 us
    pallas_call x3, Pallas kernels, attn_call(): pl.pallas_call(kernel, out_shape=out_shape, grid_spec=pltpu.PrefetchScala...  16.9 us
    all_to_all x3, starting transfers between devices, exchange(): return lax.all_to_all(pieces, axes, 0, 0, tiled=True)  13.2 us
    pallas_call x1, Pallas kernels, loss_parts(): pl.pallas_call(loss_kernel, out_shape=(jax.ShapeDtypeStruct((4, 128, WIDE...  11.9 us
    ppermute x9, starting transfers between devices, shards(): swap = lambda a: lax.ppermute(a, 'core', SWAP)  11 us
    ppermute x3, starting transfers between devices, shards(): mine.append(lax.ppermute(part, 'vocab', ring(s)))  8.84 us
  transfers between devices with their start and end apart: 18, of which 7 were waited for; matrix products, arithmetic and copies ran while one was open for 7% of the time, Pallas kernels for 7%

profile of v4, /device:TPU:1, one launch (start us, length us, event | category | flops | bytes accessed | tf_op | source)
XLA Modules:
  0.0 245.7 jit_solution(3624364595358130381)
XLA Ops:
  0.6 3.4 %shard_map.130 = bf16[8,512,128]{2,1,0:T(8,128)(2,1)} custom-call(bf16[256,1024]{1,0:T(8,128)(2,1)} %q_ref.1, bf16[256,512]{1,0:T(8,128)(2,1)} %k_ref.1, bf16[256,512]{1,0:T(8,128)(2,1)} %v_ref.1), custom_call_target="tpu_custom_call" | custom-call | tf_op jit(solution)/shard_map/pallas_call | solution.py:60
  4.0 20.7 %all_to_all.25 = bf16[8,512,128]{2,1,0:T(8,128)(2,1)S(1)} all-to-all(bf16[8,512,128]{2,1,0:T(8,128)(2,1)} %shard_map.130), channel_id=1, replica_groups=mesh['x'=4,'y'=4,'core'=2,'vocab'=4] {'x','core'}, dimensions={0} | all-to-all | bytes 2097152 | tf_op jit(solution)/shard_map/all_to_all | solution.py:70
  30.6 8.1 %collective-permute-done.4.refs_0_ = bf16[2048,128]{1,0:T(8,128)(2,1)S(1)} collective-permute-done((bf16[2048,128]{1,0:T(8,128)(2,1)S(1)}, bf16[2048,128]{1,0:T(8,128)(2,1)S(1)}, u32[]{:S(2)}, u32[]{:S(2)}) %collective-permute-start.4) | collective-permute-done | bytes 524320 | tf_op jit(solution)/shard_map/ppermute | solution.py:489
  40.9 4.0 %fusion.7 = (bf16[512,1152]{1,0:T(8,128)(2,1)}, bf16[512,1152]{1,0:T(8,128)(2,1)}, bf16[512,1152]{1,0:T(8,128)(2,1)}) fusion(bf16[1024,4608]{1,0:T(8,128)(2,1)} %param.15, s32[]{:T(128)S(6)} %select_n.63, s32[]{:T(128)S(6)} %select_n.69, s32[]{:T(128)S(6)} %select_n.65, s32[]{:T(128)S(6)} %select_n.67), kind=kLoop, calls=%fused_computation.25 | loop fusion | bytes 7077904 | tf_op jit(solution)/shard_map/dynamic_slice | solution.py:494
  46.5 3.4 %collective-permute-start.8 = (bf16[512,1152]{1,0:T(8,128)(2,1)}, bf16[512,1152]{1,0:T(8,128)(2,1)}, u32[]{:S(2)}, u32[]{:S(2)}) collective-permute-start(bf16[512,1152]{1,0:T(8,128)(2,1)} %get-tuple-element.17), channel_id=1, source_target_pairs={{0,2},{1,3},{2,0},{3,1},{4,6},{5,7},{6,4},{7,5},{8,10},{9,11},{10,... | collective-permute-start | bytes 3538952 | tf_op jit(solution)/shard_map/ppermute | solution.py:495
  53.1 5.1 %shard_map.131.refs_2_ = f32[4,512,256]{2,1,0:T(8,128)S(1)} custom-call(s32[7]{0:T(128)S(1)} %stack.61.sc_ref, bf16[4,512,128]{2,1,0:T(8,128)(2,1)S(1)} %bitcast.26, bf16[2048,128]{1,0:T(8,128)(2,1)S(1)} %bitcast.33, bf16[2048,128]{1,0:T(8,128)(2,1)} %collective-permute-done.6.b_ref), custom_call_target="tpu_custom_call" | custom-call | flops 5000000000 | bytes 4000000 | tf_op jit(solution)/shard_map/pallas_call | solution.py:246
  58.2 3.8 %collective-permute-start.9 = (bf16[512,1152]{1,0:T(8,128)(2,1)}, bf16[512,1152]{1,0:T(8,128)(2,1)}, u32[]{:S(2)}, u32[]{:S(2)}) collective-permute-start(bf16[512,1152]{1,0:T(8,128)(2,1)} %get-tuple-element.15), channel_id=1, source_target_pairs={{0,3},{1,0},{2,1},{3,2},{4,7},{5,4},{6,5},{7,6},{8,11},{9,8},{10,9... | collective-permute-start | bytes 3538952 | tf_op jit(solution)/shard_map/ppermute | solution.py:495
  62.0 4.3 %shard_map.132.refs_4_ = f32[4,512,256]{2,1,0:T(8,128)S(1)} custom-call(s32[7]{0:T(128)S(1)} %stack.61.sc_ref, bf16[4,512,128]{2,1,0:T(8,128)(2,1)S(1)} %bitcast.27, bf16[2048,128]{1,0:T(8,128)(2,1)S(1)} %collective-permute-done.4.refs_0_, bf16[2048,128]{1,0:T(8,128)(2,1)} %collective-permute-done.5.refs_1_, f32[4,512,256]{2,1,0:T(8,128)S(1)} %shard_map.131.refs_2_), custom_call_target="tpu_custom_call" | custom-call | flops 5000000000 | bytes 4000000 | tf_op jit(solution)/shard_map/pallas_call | solution.py:246
  66.3 7.5 %shard_map.133 = bf16[4,4,512,128]{3,2,1,0:T(8,128)(2,1)} custom-call(s32[7]{0:T(128)S(1)} %stack.61.sc_ref, bf16[4,512,128]{2,1,0:T(8,128)(2,1)S(1)} %bitcast.28, bf16[2048,128]{1,0:T(8,128)(2,1)S(1)} %collective-permute-done.refs_0_, bf16[2048,128]{1,0:T(8,128)(2,1)S(1)} %collective-permute-done.1.refs_1_, ...), custom_call_target="tpu_custom_call" | custom-call | flops 10000000000 | bytes 4000000 | tf_op jit(solution)/shard_map/pallas_call | solution.py:246
  73.9 4.8 %all-to-all-start.1 = ((bf16[32,256,128]{2,1,0:T(8,128)(2,1)}), bf16[32,256,128]{2,1,0:T(8,128)(2,1)}, u32[]{:S(2)}, u32[]{:S(2)}) async-start(bf16[32,256,128]{2,1,0:T(8,128)(2,1)} %bitcast.35), calls=%async_computation.1 | async-start | bytes 4194304 | tf_op jit(solution)/shard_map/all_to_all | solution.py:70
  79.2 39.7 %collective-permute-done.8.a2 = bf16[512,1152]{1,0:T(8,128)(2,1)} collective-permute-done((bf16[512,1152]{1,0:T(8,128)(2,1)}, bf16[512,1152]{1,0:T(8,128)(2,1)}, u32[]{:S(2)}, u32[]{:S(2)}) %collective-permute-start.8) | collective-permute-done | bytes 1179680 | tf_op jit(solution)/shard_map/ppermute | solution.py:495
  122.3 2.3 gather_fusion
  129.3 8.0 %shard_map.134 = (f32[256,1152]{1,0:T(8,128)}, f32[4,24,1152]{2,1,0:T(8,128)}) custom-call(s32[7]{0:T(128)S(1)} %copy-done.4, s32[8]{0:T(128)S(1)} %copy-done.7, bf16[32,256,128]{2,1,0:T(8,128)(2,1)} %all-to-all-done.1.att_ref, bf16[1024,1152]{1,0:T(8,128)(2,1)S(1)} %constant_dynamic-slice_fusion.w_ref, bf16[512,1152]{1,0:T(8,128)(2,1)S(1)} %collective-permute-done.7.a1, ...), custom_call_target="tpu_custom_call" | custom-call | tf_op jit(solution)/shard_map/pallas_call | solution.py:299
  137.3 3.5 %all-to-all-start.2 = ((f32[4,24,1152]{2,1,0:T(8,128)}), f32[4,24,1152]{2,1,0:T(8,128)S(1)}, u32[]{:S(2)}, u32[]{:S(2)}) async-start(f32[4,24,1152]{2,1,0:T(8,128)} %get-tuple-element.10), calls=%async_computation.2 | async-start | bytes 884736 | tf_op jit(solution)/shard_map/all_to_all | solution.py:70
  142.3 6.6 %all-to-all-done.2.zr_ref = f32[4,24,1152]{2,1,0:T(8,128)S(1)} async-done(((f32[4,24,1152]{2,1,0:T(8,128)}), f32[4,24,1152]{2,1,0:T(8,128)S(1)}, u32[]{:S(2)}, u32[]{:S(2)}) %all-to-all-start.2) | async-done | bytes 442400 | tf_op jit(solution)/shard_map/all_to_all | solution.py:70
  149.2 31.1 %all_to_all.26 = bf16[16,8,4736]{2,1,0:T(8,128)(2,1)S(1)} all-to-all(bf16[16,8,4736]{2,1,0:T(8,128)(2,1)S(1)} %shard_map.135), channel_id=1, replica_groups=mesh['x'=4,'y'=4,'core'=2,'vocab'=4] {'x','y'}, dimensions={0} | all-to-all | bytes 2424832 | tf_op jit(solution)/shard_map/all_to_all | solution.py:70
  180.3 2.8 %collective-permute-start.13 = (bf16[128,4736]{1,0:T(8,128)(2,1)S(1)}, bf16[128,4736]{1,0:T(8,128)(2,1)S(1)}, u32[]{:S(2)}, u32[]{:S(2)}) collective-permute-start(bf16[128,4736]{1,0:T(8,128)(2,1)S(1)} %bitcast.23), channel_id=1, source_target_pairs={{0,4},{4,0},{1,5},{5,1},{2,6},{6,2},{3,7},{7,3},{8,12},{12,8},{9,1... | collective-permute-start | bytes 3637256 | tf_op jit(solution)/shard_map/ppermute | solution.py:485
  183.1 2.5 %collective-permute-done.13.s_ref = bf16[128,4736]{1,0:T(8,128)(2,1)S(1)} collective-permute-done((bf16[128,4736]{1,0:T(8,128)(2,1)S(1)}, bf16[128,4736]{1,0:T(8,128)(2,1)S(1)}, u32[]{:S(2)}, u32[]{:S(2)}) %collective-permute-start.13) | collective-permute-done | bytes 1212448 | tf_op jit(solution)/shard_map/ppermute | solution.py:485
  185.6 11.9 %shard_map.136 = (bf16[4,128,2560]{2,1,0:T(8,128)(2,1)S(1)}, bf16[4,128,2560]{2,1,0:T(8,128)(2,1)S(1)}) custom-call(s32[7]{0:T(128)S(1)} %copy-done.5, bf16[128,4736]{1,0:T(8,128)(2,1)S(1)} %bitcast.24, bf16[128,4736]{1,0:T(8,128)(2,1)S(1)} %collective-permute-done.13.s_ref, bf16[1024,4608]{1,0:T(8,128)(2,1)} %e_ref.1), custom_call_target="tpu_custom_call" | custom-call | tf_op jit(solution)/shard_map/pallas_call | solution.py:408
  197.9 4.6 %collective-permute-done.14 = bf16[4,128,2560]{2,1,0:T(8,128)(2,1)S(1)} collective-permute-done((bf16[4,128,2560]{2,1,0:T(8,128)(2,1)S(1)}, bf16[4,128,2560]{2,1,0:T(8,128)(2,1)S(1)}, u32[]{:S(2)}, u32[]{:S(2)}) %collective-permute-start.14) | collective-permute-done | bytes 2621472 | tf_op jit(solution)/shard_map/ppermute | solution.py:485
  202.5 2.2 add_convert_fusion
  204.7 5.0 %all-to-all-start.4 = ((bf16[64,8,2560]{2,1,0:T(8,128)(2,1)}), bf16[64,8,2560]{2,1,0:T(8,128)(2,1)S(1)}, u32[]{:S(2)}, u32[]{:S(2)}) async-start(bf16[64,8,2560]{2,1,0:T(8,128)(2,1)} %bitcast.34), calls=%async_computation.4 | async-start | bytes 5242880 | tf_op jit(solution)/shard_map/all_to_all | solution.py:70
  209.8 2.5 %add_convert_fusion.1 = bf16[256,1152]{1,0:T(8,128)(2,1)} fusion(f32[256,1152]{1,0:T(8,128)} %get-tuple-element.9, bf16[256,1152]{1,0:T(8,128)(2,1)} %param.14, f32[1152]{0:T(1024)S(1)} %copy-done.10, f32[256]{0:T(256)S(1)} %add_rsqrt_fusion), kind=kLoop, calls=%fused_computation.2 | loop fusion | flops 1474560 | bytes 2364928 | tf_op jit(solution)/shard_map/convert_element_type | solution.py:512
  214.1 29.7 %all-to-all-done.4.back_ref = bf16[64,8,2560]{2,1,0:T(8,128)(2,1)S(1)} async-done(((bf16[64,8,2560]{2,1,0:T(8,128)(2,1)}), bf16[64,8,2560]{2,1,0:T(8,128)(2,1)S(1)}, u32[]{:S(2)}, u32[]{:S(2)}) %all-to-all-start.4) | async-done | bytes 2621472 | tf_op jit(solution)/shard_map/all_to_all | solution.py:70
  (73 shorter events, 27.2 us)
Async XLA Ops:
  24.9 13.8 %collective-permute-start.4 = (bf16[2048,128]{1,0:T(8,128)(2,1)S(1)}, bf16[2048,128]{1,0:T(8,128)(2,1)S(1)}, u32[]{:S(2)}, u32[]{:S(2)}) collective-permute-start(bf16[2048,128]{1,0:T(8,128)(2,1)S(1)} %bitcast.29), channel_id=1, source_target_pairs={{0,8},{8,16},{16,24},{24,0},{1,9},{9,17},{17,25},{25,1},{2,10},{10... | collective-permute-start | bytes 1572872 | tf_op jit(solution)/shard_map/ppermute | solution.py:489
  26.2 20.3 %collective-permute-start.6 = (bf16[2048,128]{1,0:T(8,128)(2,1)S(1)}, bf16[2048,128]{1,0:T(8,128)(2,1)}, u32[]{:S(2)}, u32[]{:S(2)}) collective-permute-start(bf16[2048,128]{1,0:T(8,128)(2,1)S(1)} %bitcast.30), channel_id=1, source_target_pairs={{0,4},{4,0},{1,5},{5,1},{2,6},{6,2},{3,7},{7,3},{8,12},{12,8},{9,1... | collective-permute-start | bytes 1572872 | tf_op jit(solution)/shard_map/ppermute | solution.py:485
  27.5 22.4 %collective-permute-start = (bf16[2048,128]{1,0:T(8,128)(2,1)S(1)}, bf16[2048,128]{1,0:T(8,128)(2,1)S(1)}, u32[]{:S(2)}, u32[]{:S(2)}) collective-permute-start(bf16[2048,128]{1,0:T(8,128)(2,1)S(1)} %bitcast.31), channel_id=1, source_target_pairs={{0,24},{8,0},{16,8},{24,16},{1,25},{9,1},{17,9},{25,17},{2,26},{10... | collective-permute-start | bytes 1572872 | tf_op jit(solution)/shard_map/ppermute | solution.py:489
  28.9 22.2 %collective-permute-start.2 = (bf16[2048,128]{1,0:T(8,128)(2,1)S(1)}, bf16[2048,128]{1,0:T(8,128)(2,1)}, u32[]{:S(2)}, u32[]{:S(2)}) collective-permute-start(bf16[2048,128]{1,0:T(8,128)(2,1)S(1)} %bitcast.32), channel_id=1, source_target_pairs={{0,16},{8,24},{16,0},{24,8},{1,17},{9,25},{17,1},{25,9},{2,18},{10... | collective-permute-start | bytes 1572872 | tf_op jit(solution)/shard_map/ppermute | solution.py:489
  38.7 19.4 %collective-permute-start.5 = (bf16[2048,128]{1,0:T(8,128)(2,1)S(1)}, bf16[2048,128]{1,0:T(8,128)(2,1)}, u32[]{:S(2)}, u32[]{:S(2)}) collective-permute-start(bf16[2048,128]{1,0:T(8,128)(2,1)S(1)} %collective-permute-done.4.refs_0_), channel_id=1, source_target_pairs={{0,4},{4,0},{1,5},{5,1},{2,6},{6,2},{3,7},{7,3},{8,12},{12,8},{9,1... | collective-permute-start | bytes 1572872 | tf_op jit(solution)/shard_map/ppermute | solution.py:485
  44.8 33.8 %collective-permute-start.7 = (bf16[512,1152]{1,0:T(8,128)(2,1)}, bf16[512,1152]{1,0:T(8,128)(2,1)S(1)}, u32[]{:S(2)}, u32[]{:S(2)}) collective-permute-start(bf16[512,1152]{1,0:T(8,128)(2,1)} %get-tuple-element.16), channel_id=1, source_target_pairs={{0,1},{1,2},{2,3},{3,0},{4,5},{5,6},{6,7},{7,4},{8,9},{9,10},{10,1... | collective-permute-start | bytes 3538952 | tf_op jit(solution)/shard_map/ppermute | solution.py:495
  46.5 19.8 %copy-start.3 = (s32[7]{0:T(128)}, s32[7]{0:T(128)S(1)}, u32[]{:S(2)}) copy-start(s32[7]{0:T(128)S(1)} %stack.61.sc_ref) | copy-start | bytes 88
  46.5 72.4 %collective-permute-start.8 = (bf16[512,1152]{1,0:T(8,128)(2,1)}, bf16[512,1152]{1,0:T(8,128)(2,1)}, u32[]{:S(2)}, u32[]{:S(2)}) collective-permute-start(bf16[512,1152]{1,0:T(8,128)(2,1)} %get-tuple-element.17), channel_id=1, source_target_pairs={{0,2},{1,3},{2,0},{3,1},{4,6},{5,7},{6,4},{7,5},{8,10},{9,11},{10,... | collective-permute-start | bytes 3538952 | tf_op jit(solution)/shard_map/ppermute | solution.py:495
  49.9 16.3 %collective-permute-start.1 = (bf16[2048,128]{1,0:T(8,128)(2,1)S(1)}, bf16[2048,128]{1,0:T(8,128)(2,1)S(1)}, u32[]{:S(2)}, u32[]{:S(2)}) collective-permute-start(bf16[2048,128]{1,0:T(8,128)(2,1)S(1)} %collective-permute-done.refs_0_), channel_id=1, source_target_pairs={{0,4},{4,0},{1,5},{5,1},{2,6},{6,2},{3,7},{7,3},{8,12},{12,8},{9,1... | collective-permute-start | bytes 1572872 | tf_op jit(solution)/shard_map/ppermute | solution.py:485
  51.2 15.1 %collective-permute-start.3 = (bf16[2048,128]{1,0:T(8,128)(2,1)}, bf16[2048,128]{1,0:T(8,128)(2,1)S(1)}, u32[]{:S(2)}, u32[]{:S(2)}) collective-permute-start(bf16[2048,128]{1,0:T(8,128)(2,1)} %collective-permute-done.2.refs_2_), channel_id=1, source_target_pairs={{0,4},{4,0},{1,5},{5,1},{2,6},{6,2},{3,7},{7,3},{8,12},{12,8},{9,1... | collective-permute-start | bytes 1572872 | tf_op jit(solution)/shard_map/ppermute | solution.py:485
  58.2 62.1 %collective-permute-start.9 = (bf16[512,1152]{1,0:T(8,128)(2,1)}, bf16[512,1152]{1,0:T(8,128)(2,1)}, u32[]{:S(2)}, u32[]{:S(2)}) collective-permute-start(bf16[512,1152]{1,0:T(8,128)(2,1)} %get-tuple-element.15), channel_id=1, source_target_pairs={{0,3},{1,0},{2,1},{3,2},{4,7},{5,4},{6,5},{7,6},{8,11},{9,8},{10,9... | collective-permute-start | bytes 3538952 | tf_op jit(solution)/shard_map/ppermute | solution.py:495
  73.8 46.4 %copy-start.6 = (s32[8]{0:T(128)S(1)}, s32[8]{0:T(128)}, u32[]{:S(2)}) copy-start(s32[8]{0:T(128)} %pick_ref.1) | copy-start | bytes 100
  73.8 46.4 %copy-start.9 = (f32[1152]{0:T(1024)S(1)}, f32[1152]{0:T(1024)}, u32[]{:S(2)}) copy-start(f32[1152]{0:T(1024)} %param.16) | copy-start | bytes 13828
  73.8 46.4 %copy-start.11 = (f32[1152]{0:T(1024)S(1)}, f32[1152]{0:T(1024)}, u32[]{:S(2)}) copy-start(f32[1152]{0:T(1024)} %param.17) | copy-start | bytes 13828
  73.9 53.3 %all-to-all-start.1 = ((bf16[32,256,128]{2,1,0:T(8,128)(2,1)}), bf16[32,256,128]{2,1,0:T(8,128)(2,1)}, u32[]{:S(2)}, u32[]{:S(2)}) async-start(bf16[32,256,128]{2,1,0:T(8,128)(2,1)} %bitcast.35), calls=%async_computation.1 | async-start | bytes 4194304 | tf_op jit(solution)/shard_map/all_to_all | solution.py:70
  78.7 48.5 %collective-permute-start.10 = (bf16[512,1152]{1,0:T(8,128)(2,1)S(1)}, bf16[512,1152]{1,0:T(8,128)(2,1)}, u32[]{:S(2)}, u32[]{:S(2)}) collective-permute-start(bf16[512,1152]{1,0:T(8,128)(2,1)S(1)} %collective-permute-done.7.a1), channel_id=1, source_target_pairs={{0,4},{4,0},{1,5},{5,1},{2,6},{6,2},{3,7},{7,3},{8,12},{12,8},{9,1... | collective-permute-start | bytes 3538952 | tf_op jit(solution)/shard_map/ppermute | solution.py:485
  118.9 8.3 %collective-permute-start.11 = (bf16[512,1152]{1,0:T(8,128)(2,1)}, bf16[512,1152]{1,0:T(8,128)(2,1)}, u32[]{:S(2)}, u32[]{:S(2)}) collective-permute-start(bf16[512,1152]{1,0:T(8,128)(2,1)} %collective-permute-done.8.a2), channel_id=1, source_target_pairs={{0,4},{4,0},{1,5},{5,1},{2,6},{6,2},{3,7},{7,3},{8,12},{12,8},{9,1... | collective-permute-start | bytes 3538952 | tf_op jit(solution)/shard_map/ppermute | solution.py:485
  120.2 7.0 %collective-permute-start.12 = (bf16[512,1152]{1,0:T(8,128)(2,1)}, bf16[512,1152]{1,0:T(8,128)(2,1)}, u32[]{:S(2)}, u32[]{:S(2)}) collective-permute-start(bf16[512,1152]{1,0:T(8,128)(2,1)} %collective-permute-done.9.a3), channel_id=1, source_target_pairs={{0,4},{4,0},{1,5},{5,1},{2,6},{6,2},{3,7},{7,3},{8,12},{12,8},{9,1... | collective-permute-start | bytes 3538952 | tf_op jit(solution)/shard_map/ppermute | solution.py:485
  137.3 11.6 %all-to-all-start.2 = ((f32[4,24,1152]{2,1,0:T(8,128)}), f32[4,24,1152]{2,1,0:T(8,128)S(1)}, u32[]{:S(2)}, u32[]{:S(2)}) async-start(f32[4,24,1152]{2,1,0:T(8,128)} %get-tuple-element.10), calls=%async_computation.2 | async-start | bytes 884736 | tf_op jit(solution)/shard_map/all_to_all | solution.py:70
  149.2 36.4 %copy-start.5 = (s32[7]{0:T(128)S(1)}, s32[7]{0:T(128)}, u32[]{:S(2)}) copy-start(s32[7]{0:T(128)} %copy-done.3) | copy-start | bytes 88
  180.3 17.2 %copy-start = (bf16[16,8,4736]{2,1,0:T(8,128)(2,1)}, bf16[16,8,4736]{2,1,0:T(8,128)(2,1)S(1)}, u32[]{:S(2)}) copy-start(bf16[16,8,4736]{2,1,0:T(8,128)(2,1)S(1)} %all_to_all.26) | copy-start | bytes 3637252
  180.3 5.3 %collective-permute-start.13 = (bf16[128,4736]{1,0:T(8,128)(2,1)S(1)}, bf16[128,4736]{1,0:T(8,128)(2,1)S(1)}, u32[]{:S(2)}, u32[]{:S(2)}) collective-permute-start(bf16[128,4736]{1,0:T(8,128)(2,1)S(1)} %bitcast.23), channel_id=1, source_target_pairs={{0,4},{4,0},{1,5},{5,1},{2,6},{6,2},{3,7},{7,3},{8,12},{12,8},{9,1... | collective-permute-start | bytes 3637256 | tf_op jit(solution)/shard_map/ppermute | solution.py:485
  197.5 5.0 %collective-permute-start.14 = (bf16[4,128,2560]{2,1,0:T(8,128)(2,1)S(1)}, bf16[4,128,2560]{2,1,0:T(8,128)(2,1)S(1)}, u32[]{:S(2)}, u32[]{:S(2)}) collective-permute-start(bf16[4,128,2560]{2,1,0:T(8,128)(2,1)S(1)} %get-tuple-element.12), channel_id=1, source_target_pairs={{0,4},{4,0},{1,5},{5,1},{2,6},{6,2},{3,7},{7,3},{8,12},{12,8},{9,1... | collective-permute-start | bytes 7864328 | tf_op jit(solution)/shard_map/ppermute | solution.py:485
  204.7 39.1 %all-to-all-start.4 = ((bf16[64,8,2560]{2,1,0:T(8,128)(2,1)}), bf16[64,8,2560]{2,1,0:T(8,128)(2,1)S(1)}, u32[]{:S(2)}, u32[]{:S(2)}) async-start(bf16[64,8,2560]{2,1,0:T(8,128)(2,1)} %bitcast.34), calls=%async_computation.4 | async-start | bytes 5242880 | tf_op jit(solution)/shard_map/all_to_all | solution.py:70
  (7 other events, 25.7 us)

commit v5 on v4

--- a/solution.py
+++ b/solution.py
@@ -40,6 +40,10 @@
     return pltpu.with_memory_space_constraint(a, pltpu.MemorySpace.VMEM)
 
 
+def in_hbm(a):
+    return pltpu.with_memory_space_constraint(a, pltpu.MemorySpace.HBM)
+
+
 def params(mib):
     return pltpu.CompilerParams(
         dimension_semantics=("arbitrary",), vmem_limit_bytes=mib * 1024 * 1024
@@ -50,19 +54,20 @@
 
 
 def pack_kernel(q_ref, k_ref, v_ref, out_ref):
-    for h, other in enumerate((k_ref, v_ref)):
+    for h in range(8):
         out_ref[h, :BLK, :] = q_ref[:, h * HEAD_DIM : (h + 1) * HEAD_DIM]
-        out_ref[h, BLK:, :] = other[...]
+        other = (k_ref, v_ref)[h % 2]
+        out_ref[h, BLK:, :] = other[:, h // 2 * HEAD_DIM : (h // 2 + 1) * HEAD_DIM]
 
 
 def pack(q, k, v):
-    one = pl.BlockSpec((BLK, HEAD_DIM), lambda i: (0, i))
+    whole = lambda *dims: pl.BlockSpec(dims, lambda i: (0,) * len(dims))
     return pl.pallas_call(
         pack_kernel,
-        out_shape=jax.ShapeDtypeStruct((8, SPAN, HEAD_DIM), bf16),
-        grid=(4,),
-        in_specs=[pl.BlockSpec((BLK, 2 * HEAD_DIM), lambda i: (0, i)), one, one],
-        out_specs=pl.BlockSpec((2, SPAN, HEAD_DIM), lambda i: (i, 0, 0)),
+        out_shape=pltpu.MemorySpace.HBM((8, SPAN, HEAD_DIM), bf16),
+        grid=(1,),
+        in_specs=[whole(BLK, 8 * HEAD_DIM), whole(BLK, 4 * HEAD_DIM), whole(BLK, 4 * HEAD_DIM)],
+        out_specs=whole(8, SPAN, HEAD_DIM),
     )(q, k, v)
 
 
@@ -219,7 +224,8 @@
         whole = jnp.sum(acc_ref[0, :, HEAD_DIM:], axis=1, keepdims=True)
         done = (acc_ref[0, :, :HEAD_DIM] / whole).astype(bf16)
         for z in range(4):
-            out_ref[z, 0] = done
+            for r in range(2):
+                out_ref[0, r, z] = done[r * BLK : (r + 1) * BLK]
 
 
 def attn_call(scalars, q, keys, acc=None, at=0, last=False):
@@ -240,8 +246,8 @@
             pltpu.SemaphoreType.DMA((chunks, 2)),
         ]
     if last:
-        out_spec = pl.BlockSpec((4, 1, SPAN, HEAD_DIM), lambda i, sc: (0, i, 0, 0))
-        out_shape = pltpu.MemorySpace.HBM((4, 4, SPAN, HEAD_DIM), bf16)
+        out_spec = pl.BlockSpec((1, 2, 4, BLK, HEAD_DIM), lambda i, sc: (i, 0, 0, 0, 0))
+        out_shape = pltpu.MemorySpace.HBM((4, 2, 4, BLK, HEAD_DIM), bf16)
         scratch = scratch + [pltpu.VMEM((1, SPAN, 2 * HEAD_DIM), f32)]
     return pl.pallas_call(
         kernel,
@@ -268,22 +274,33 @@
 
 
 def proj_kernel(
-    sc_ref, pick_ref, att_ref, w_ref, a1, a2, a3, b1, b2, b3, rp_ref, pg_ref, fg_ref,
-    own_ref, zp_ref,
+    sc_ref, pick_ref, att_ref, w_ref, a1, a2, a3, b1, b2, b3, rp_hbm, pg_ref, fg_ref,
+    own_ref, zp_ref, rp_ref, sem, wbuf, wsem,
 ):
     zi, ci = sc_ref[0], sc_ref[1]
     heads = [zi * 2, zi * 2 + 1]
     heads += [((zi - s + 4) % 4) * 2 + ci for s in (1, 2, 3)]
     heads += [((zi - s + 4) % 4) * 2 + 1 - ci for s in (1, 2, 3)]
-    weights = [w_ref.at[:512], w_ref.at[512:], a1, a2, a3, b1, b2, b3]
+    rows_in = pltpu.make_async_copy(rp_hbm, rp_ref, sem)
+    rows_in.start()
+    col = pl.multiple_of(zi * COLS, 128)
+    src = [w_ref.at[pl.ds(0, 512), pl.ds(col, COLS)], w_ref.at[pl.ds(512, 512), pl.ds(col, COLS)]]
+    src += [a1, a2, a3, b1, b2, b3]
+    copies = [pltpu.make_async_copy(src[n], wbuf.at[n], wsem.at[n]) for n in range(8)]
+    copies[0].start()
+    copies[1].start()
     total = None
     for n in range(8):
-        lhs = jnp.concatenate([att_ref[heads[n] * 4 + h] for h in range(4)], axis=1)
-        part = jnp.dot(lhs, weights[n][...], preferred_element_type=f32)
+        copies[n].wait()
+        if n + 2 < 8:
+            copies[n + 2].start()
+        lhs = jnp.concatenate([att_ref[heads[n] % 2 * 16 + h * 4 + heads[n] // 2] for h in range(4)], axis=1)
+        part = jnp.dot(lhs, wbuf[n], preferred_element_type=f32)
         total = part if total is None else total + part
     own_ref[...] = total
     own = own_ref[...]
     squares = row_of_sums(lane_sums(own * own))
+    rows_in.wait()
     for z in range(4):
         for p in range(PICK):
             zp_ref[z, p : p + 1, :] = own_ref[pl.ds(pick_ref[p], 1), :]
@@ -302,15 +319,22 @@
             pltpu.MemorySpace.HBM((BLK, COLS), f32),
             pltpu.MemorySpace.HBM((4, 24, COLS), f32),
         ),
-        grid_spec=pltpu.PrefetchScalarGridSpec(
-            num_scalar_prefetch=2,
-            grid=(1,),
-            in_specs=[VMEM_SPEC] * 8
-            + [whole(PICK, COLS), whole(1, COLS), whole(1, COLS)],
-            out_specs=(whole(BLK, COLS), whole(4, 24, COLS)),
-        ),
+        grid=(1,),
+        in_specs=[pl.BlockSpec(memory_space=pltpu.MemorySpace.SMEM)] * 2
+        + [VMEM_SPEC]
+        + [pl.BlockSpec(memory_space=pltpu.MemorySpace.HBM)] * 8
+        + [whole(1, COLS), whole(1, COLS)],
+        out_specs=(whole(BLK, COLS), whole(4, 24, COLS)),
+        scratch_shapes=[
+            pltpu.VMEM((PICK, COLS), f32),
+            pltpu.SemaphoreType.DMA(()),
+            pltpu.VMEM((8, 512, COLS), bf16),
+            pltpu.SemaphoreType.DMA((8,)),
+        ],
         compiler_params=params(20),
-    )(scalars, pick, in_vmem(att), in_vmem(w), *[in_vmem(p) for p in parts], res_pick, pg, fg)
+    )(
+        scalars, pick, in_vmem(att), *[in_hbm(a) for a in (w, *parts, res_pick)], pg, fg,
+    )
 
 
 def norm_kernel(zr_ref, ext_ref, out_ref):
@@ -498,12 +522,10 @@
     acc = attn_call(scalars, q, own_pair)
     acc = attn_call(scalars, q, [down, swap(down)], acc, at=2)
     out = attn_call(scalars, q, [up, swap(up), far, swap(far)], acc, at=3, last=True)
-    att = exchange(out.reshape(32, BLK, HEAD_DIM), ("vocab", "x", "core"))
-    kept = lax.dynamic_slice(out_weight, (0, zi * COLS), (1024, COLS))
-
+    att = exchange(out.reshape(32, BLK, HEAD_DIM), ("x", "core", "vocab"))
     res_pick = jnp.take(residual, pick_pos, axis=0).astype(f32)
     own_cols, zp = project(
-        scalars, pick_pos, att, kept, mine + theirs,
+        scalars, pick_pos, att, out_weight, mine + theirs,
         res_pick, post_gain[None], final_gain[None],
     )
     zr = exchange(zp, "vocab")

time: 247 us -> 243 us (0.984)
  local copies, waits for them, and re-layouts: 12.5 us -> 6.23 us
  waiting for transfers between devices: 91.9 us -> 97.4 us
  transfers between devices with their start and end apart: 18 -> 18, of which waited for: 7 -> 8; matrix products, arithmetic and copies ran while one was open for 7% -> 5% of each run, Pallas kernels for 7% -> 7%
where the time goes in v5:
time: 243 us; the launch traced here: 241 us
  waiting for transfers between devices  97.4 us (40%)
  blocking collectives  51.8 us (21%)
  Pallas kernels  40.6 us (17%)
  starting transfers between devices  36.6 us (15%)
  other arithmetic  7.4 us (3%)
  local copies, waits for them, and re-layouts  6.23 us (3%)
    all_to_all x2, blocking collectives, exchange(): return lax.all_to_all(pieces, axes, 0, 0, tiled=True)  51.8 us
    ppermute x3, waiting for transfers between devices, shards(): mine.append(lax.ppermute(part, 'vocab', ring(s)))  42.1 us
    all_to_all x3, waiting for transfers between devices, exchange(): return lax.all_to_all(pieces, axes, 0, 0, tiled=True)  37.8 us
    pallas_call x3, Pallas kernels, attn_call(): pl.pallas_call(kernel, out_shape=out_shape, grid_spec=pltpu.PrefetchScala...  15.9 us
    all_to_all x3, starting transfers between devices, exchange(): return lax.all_to_all(pieces, axes, 0, 0, tiled=True)  12.4 us
    pallas_call x1, Pallas kernels, loss_parts(): pl.pallas_call(loss_kernel, out_shape=(jax.ShapeDtypeStruct((4, 128, WIDE...  11.8 us
    ppermute x9, starting transfers between devices, shards(): swap = lambda a: lax.ppermute(a, 'core', SWAP)  10.9 us
    ppermute x3, starting transfers between devices, shards(): mine.append(lax.ppermute(part, 'vocab', ring(s)))  8.83 us
  transfers between devices with their start and end apart: 18, of which 8 were waited for; matrix products, arithmetic and copies ran while one was open for 5% of the time, Pallas kernels for 7%

profile of v5, /device:TPU:1, one launch (start us, length us, event | category | flops | bytes accessed | tf_op | source)
XLA Modules:
  0.0 241.1 jit_solution(16472005913401626938)
XLA Ops:
  0.6 2.4 shard_map.130
  3.0 20.7 %all_to_all.25 = bf16[8,512,128]{2,1,0:T(8,128)(2,1)S(1)} all-to-all(bf16[8,512,128]{2,1,0:T(8,128)(2,1)} %shard_map.130), channel_id=1, replica_groups=mesh['x'=4,'y'=4,'core'=2,'vocab'=4] {'x','core'}, dimensions={0} | all-to-all | bytes 2097152 | tf_op jit(solution)/shard_map/all_to_all | solution.py:75
  29.6 8.1 %collective-permute-done.4.refs_0_ = bf16[2048,128]{1,0:T(8,128)(2,1)S(1)} collective-permute-done((bf16[2048,128]{1,0:T(8,128)(2,1)S(1)}, bf16[2048,128]{1,0:T(8,128)(2,1)S(1)}, u32[]{:S(2)}, u32[]{:S(2)}) %collective-permute-start.4) | collective-permute-done | bytes 524320 | tf_op jit(solution)/shard_map/ppermute | solution.py:513
  37.7 2.1 collective-permute-start.5
  39.8 3.9 %fusion.7 = (bf16[512,1152]{1,0:T(8,128)(2,1)}, bf16[512,1152]{1,0:T(8,128)(2,1)}, bf16[512,1152]{1,0:T(8,128)(2,1)}) fusion(bf16[1024,4608]{1,0:T(8,128)(2,1)} %w_ref.1, s32[]{:T(128)S(6)} %select_n.59, s32[]{:T(128)S(6)} %select_n.65, s32[]{:T(128)S(6)} %select_n.63, s32[]{:T(128)S(6)} %select_n.61), kind=kLoop, calls=%fused_computation.24 | loop fusion | bytes 7077904 | tf_op jit(solution)/shard_map/dynamic_slice | solution.py:518
  45.5 3.4 %collective-permute-start.8 = (bf16[512,1152]{1,0:T(8,128)(2,1)}, bf16[512,1152]{1,0:T(8,128)(2,1)}, u32[]{:S(2)}, u32[]{:S(2)}) collective-permute-start(bf16[512,1152]{1,0:T(8,128)(2,1)} %get-tuple-element.16), channel_id=1, source_target_pairs={{0,2},{1,3},{2,0},{3,1},{4,6},{5,7},{6,4},{7,5},{8,10},{9,11},{10,... | collective-permute-start | bytes 3538952 | tf_op jit(solution)/shard_map/ppermute | solution.py:519
  51.9 5.1 %shard_map.131.refs_2_ = f32[4,512,256]{2,1,0:T(8,128)S(1)} custom-call(s32[7]{0:T(128)S(1)} %stack.61.sc_ref, bf16[4,512,128]{2,1,0:T(8,128)(2,1)S(1)} %bitcast.26, bf16[2048,128]{1,0:T(8,128)(2,1)S(1)} %bitcast.33, bf16[2048,128]{1,0:T(8,128)(2,1)} %collective-permute-done.6.b_ref), custom_call_target="tpu_custom_call" | custom-call | flops 5000000000 | bytes 4000000 | tf_op jit(solution)/shard_map/pallas_call | solution.py:252
  57.0 3.8 %collective-permute-start.9 = (bf16[512,1152]{1,0:T(8,128)(2,1)}, bf16[512,1152]{1,0:T(8,128)(2,1)}, u32[]{:S(2)}, u32[]{:S(2)}) collective-permute-start(bf16[512,1152]{1,0:T(8,128)(2,1)} %get-tuple-element.15), channel_id=1, source_target_pairs={{0,3},{1,0},{2,1},{3,2},{4,7},{5,4},{6,5},{7,6},{8,11},{9,8},{10,9... | collective-permute-start | bytes 3538952 | tf_op jit(solution)/shard_map/ppermute | solution.py:519
  60.8 4.3 %shard_map.132.refs_4_ = f32[4,512,256]{2,1,0:T(8,128)S(1)} custom-call(s32[7]{0:T(128)S(1)} %stack.61.sc_ref, bf16[4,512,128]{2,1,0:T(8,128)(2,1)S(1)} %bitcast.27, bf16[2048,128]{1,0:T(8,128)(2,1)S(1)} %collective-permute-done.4.refs_0_, bf16[2048,128]{1,0:T(8,128)(2,1)} %collective-permute-done.5.refs_1_, f32[4,512,256]{2,1,0:T(8,128)S(1)} %shard_map.131.refs_2_), custom_call_target="tpu_custom_call" | custom-call | flops 5000000000 | bytes 4000000 | tf_op jit(solution)/shard_map/pallas_call | solution.py:252
  65.2 6.5 %shard_map.133 = bf16[4,2,4,256,128]{4,3,2,1,0:T(8,128)(2,1)} custom-call(s32[7]{0:T(128)S(1)} %stack.61.sc_ref, bf16[4,512,128]{2,1,0:T(8,128)(2,1)S(1)} %bitcast.28, bf16[2048,128]{1,0:T(8,128)(2,1)S(1)} %collective-permute-done.refs_0_, bf16[2048,128]{1,0:T(8,128)(2,1)S(1)} %collective-permute-done.1.refs_1_, ...), custom_call_target="tpu_custom_call" | custom-call | flops 10000000000 | bytes 4000000 | tf_op jit(solution)/shard_map/pallas_call | solution.py:252
  71.7 4.1 %all-to-all-start.1 = ((bf16[32,256,128]{2,1,0:T(8,128)(2,1)}), bf16[32,256,128]{2,1,0:T(8,128)(2,1)S(1)}, u32[]{:S(2)}, u32[]{:S(2)}) async-start(bf16[32,256,128]{2,1,0:T(8,128)(2,1)} %bitcast.35), calls=%async_computation.1 | async-start | bytes 4194304 | tf_op jit(solution)/shard_map/all_to_all | solution.py:75
  76.3 42.1 %collective-permute-done.8.a2 = bf16[512,1152]{1,0:T(8,128)(2,1)} collective-permute-done((bf16[512,1152]{1,0:T(8,128)(2,1)}, bf16[512,1152]{1,0:T(8,128)(2,1)}, u32[]{:S(2)}, u32[]{:S(2)}) %collective-permute-start.8) | collective-permute-done | bytes 1179680 | tf_op jit(solution)/shard_map/ppermute | solution.py:519
  124.2 8.5 %shard_map.134 = (f32[256,1152]{1,0:T(8,128)}, f32[4,24,1152]{2,1,0:T(8,128)}) custom-call(s32[7]{0:T(128)S(1)} %stack.61.sc_ref, s32[8]{0:T(128)S(1)} %copy-done.2, bf16[32,256,128]{2,1,0:T(8,128)(2,1)S(1)} %all-to-all-done.1.att_ref, bf16[1024,4608]{1,0:T(8,128)(2,1)} %w_ref.1, bf16[512,1152]{1,0:T(8,128)(2,1)} %collective-permute-done.7.a1, ...), custom_call_target="tpu_custom_call" | custom-call | tf_op jit(solution)/shard_map/pallas_call | solution.py:316
  132.8 3.5 %all-to-all-start.2 = ((f32[4,24,1152]{2,1,0:T(8,128)}), f32[4,24,1152]{2,1,0:T(8,128)S(1)}, u32[]{:S(2)}, u32[]{:S(2)}) async-start(f32[4,24,1152]{2,1,0:T(8,128)} %get-tuple-element.10), calls=%async_computation.2 | async-start | bytes 884736 | tf_op jit(solution)/shard_map/all_to_all | solution.py:75
  136.4 8.1 %all-to-all-done.2.zr_ref = f32[4,24,1152]{2,1,0:T(8,128)S(1)} async-done(((f32[4,24,1152]{2,1,0:T(8,128)}), f32[4,24,1152]{2,1,0:T(8,128)S(1)}, u32[]{:S(2)}, u32[]{:S(2)}) %all-to-all-start.2) | async-done | bytes 442400 | tf_op jit(solution)/shard_map/all_to_all | solution.py:75
  144.8 31.1 %all_to_all.26 = bf16[16,8,4736]{2,1,0:T(8,128)(2,1)S(1)} all-to-all(bf16[16,8,4736]{2,1,0:T(8,128)(2,1)S(1)} %shard_map.135), channel_id=1, replica_groups=mesh['x'=4,'y'=4,'core'=2,'vocab'=4] {'x','y'}, dimensions={0} | all-to-all | bytes 2424832 | tf_op jit(solution)/shard_map/all_to_all | solution.py:75
  176.0 2.8 %collective-permute-start.13 = (bf16[128,4736]{1,0:T(8,128)(2,1)S(1)}, bf16[128,4736]{1,0:T(8,128)(2,1)S(1)}, u32[]{:S(2)}, u32[]{:S(2)}) collective-permute-start(bf16[128,4736]{1,0:T(8,128)(2,1)S(1)} %bitcast.23), channel_id=1, source_target_pairs={{0,4},{4,0},{1,5},{5,1},{2,6},{6,2},{3,7},{7,3},{8,12},{12,8},{9,1... | collective-permute-start | bytes 3637256 | tf_op jit(solution)/shard_map/ppermute | solution.py:509
  178.7 2.5 %collective-permute-done.13.s_ref = bf16[128,4736]{1,0:T(8,128)(2,1)S(1)} collective-permute-done((bf16[128,4736]{1,0:T(8,128)(2,1)S(1)}, bf16[128,4736]{1,0:T(8,128)(2,1)S(1)}, u32[]{:S(2)}, u32[]{:S(2)}) %collective-permute-start.13) | collective-permute-done | bytes 1212448 | tf_op jit(solution)/shard_map/ppermute | solution.py:509
  181.2 11.8 %shard_map.136 = (bf16[4,128,2560]{2,1,0:T(8,128)(2,1)S(1)}, bf16[4,128,2560]{2,1,0:T(8,128)(2,1)S(1)}) custom-call(s32[7]{0:T(128)S(1)} %stack.61.sc_ref, bf16[128,4736]{1,0:T(8,128)(2,1)S(1)} %bitcast.24, bf16[128,4736]{1,0:T(8,128)(2,1)S(1)} %collective-permute-done.13.s_ref, bf16[1024,4608]{1,0:T(8,128)(2,1)} %e_ref.1), custom_call_target="tpu_custom_call" | custom-call | tf_op jit(solution)/shard_map/pallas_call | solution.py:432
  193.6 4.5 %collective-permute-done.14 = bf16[4,128,2560]{2,1,0:T(8,128)(2,1)S(1)} collective-permute-done((bf16[4,128,2560]{2,1,0:T(8,128)(2,1)S(1)}, bf16[4,128,2560]{2,1,0:T(8,128)(2,1)S(1)}, u32[]{:S(2)}, u32[]{:S(2)}) %collective-permute-start.14) | collective-permute-done | bytes 2621472 | tf_op jit(solution)/shard_map/ppermute | solution.py:509
  198.1 2.2 add_convert_fusion
  200.3 4.9 %all-to-all-start.4 = ((bf16[64,8,2560]{2,1,0:T(8,128)(2,1)}), bf16[64,8,2560]{2,1,0:T(8,128)(2,1)S(1)}, u32[]{:S(2)}, u32[]{:S(2)}) async-start(bf16[64,8,2560]{2,1,0:T(8,128)(2,1)} %bitcast.34), calls=%async_computation.4 | async-start | bytes 5242880 | tf_op jit(solution)/shard_map/all_to_all | solution.py:75
  205.2 2.5 %add_convert_fusion.1 = bf16[256,1152]{1,0:T(8,128)(2,1)} fusion(f32[256,1152]{1,0:T(8,128)} %get-tuple-element.9, bf16[256,1152]{1,0:T(8,128)(2,1)} %param.14, f32[1152]{0:T(1024)S(1)} %copy-done.3, f32[256]{0:T(256)S(1)} %add_rsqrt_fusion), kind=kLoop, calls=%fused_computation.2 | loop fusion | flops 1474560 | bytes 2364928 | tf_op jit(solution)/shard_map/convert_element_type | solution.py:534
  209.6 29.7 %all-to-all-done.4.back_ref = bf16[64,8,2560]{2,1,0:T(8,128)(2,1)S(1)} async-done(((bf16[64,8,2560]{2,1,0:T(8,128)(2,1)}), bf16[64,8,2560]{2,1,0:T(8,128)(2,1)S(1)}, u32[]{:S(2)}, u32[]{:S(2)}) %all-to-all-start.4) | async-done | bytes 2621472 | tf_op jit(solution)/shard_map/all_to_all | solution.py:75
  (60 shorter events, 21.5 us)
Async XLA Ops:
  23.8 13.8 %collective-permute-start.4 = (bf16[2048,128]{1,0:T(8,128)(2,1)S(1)}, bf16[2048,128]{1,0:T(8,128)(2,1)S(1)}, u32[]{:S(2)}, u32[]{:S(2)}) collective-permute-start(bf16[2048,128]{1,0:T(8,128)(2,1)S(1)} %bitcast.29), channel_id=1, source_target_pairs={{0,8},{8,16},{16,24},{24,0},{1,9},{9,17},{17,25},{25,1},{2,10},{10... | collective-permute-start | bytes 1572872 | tf_op jit(solution)/shard_map/ppermute | solution.py:513
  25.2 20.3 %collective-permute-start.6 = (bf16[2048,128]{1,0:T(8,128)(2,1)S(1)}, bf16[2048,128]{1,0:T(8,128)(2,1)}, u32[]{:S(2)}, u32[]{:S(2)}) collective-permute-start(bf16[2048,128]{1,0:T(8,128)(2,1)S(1)} %bitcast.30), channel_id=1, source_target_pairs={{0,4},{4,0},{1,5},{5,1},{2,6},{6,2},{3,7},{7,3},{8,12},{12,8},{9,1... | collective-permute-start | bytes 1572872 | tf_op jit(solution)/shard_map/ppermute | solution.py:509
  26.5 22.3 %collective-permute-start = (bf16[2048,128]{1,0:T(8,128)(2,1)S(1)}, bf16[2048,128]{1,0:T(8,128)(2,1)S(1)}, u32[]{:S(2)}, u32[]{:S(2)}) collective-permute-start(bf16[2048,128]{1,0:T(8,128)(2,1)S(1)} %bitcast.31), channel_id=1, source_target_pairs={{0,24},{8,0},{16,8},{24,16},{1,25},{9,1},{17,9},{25,17},{2,26},{10... | collective-permute-start | bytes 1572872 | tf_op jit(solution)/shard_map/ppermute | solution.py:513
  27.9 22.1 %collective-permute-start.2 = (bf16[2048,128]{1,0:T(8,128)(2,1)S(1)}, bf16[2048,128]{1,0:T(8,128)(2,1)S(1)}, u32[]{:S(2)}, u32[]{:S(2)}) collective-permute-start(bf16[2048,128]{1,0:T(8,128)(2,1)S(1)} %bitcast.32), channel_id=1, source_target_pairs={{0,16},{8,24},{16,0},{24,8},{1,17},{9,25},{17,1},{25,9},{2,18},{10... | collective-permute-start | bytes 1572872 | tf_op jit(solution)/shard_map/ppermute | solution.py:513
  37.7 19.3 %collective-permute-start.5 = (bf16[2048,128]{1,0:T(8,128)(2,1)S(1)}, bf16[2048,128]{1,0:T(8,128)(2,1)}, u32[]{:S(2)}, u32[]{:S(2)}) collective-permute-start(bf16[2048,128]{1,0:T(8,128)(2,1)S(1)} %collective-permute-done.4.refs_0_), channel_id=1, source_target_pairs={{0,4},{4,0},{1,5},{5,1},{2,6},{6,2},{3,7},{7,3},{8,12},{12,8},{9,1... | collective-permute-start | bytes 1572872 | tf_op jit(solution)/shard_map/ppermute | solution.py:509
  43.7 32.2 %collective-permute-start.7 = (bf16[512,1152]{1,0:T(8,128)(2,1)}, bf16[512,1152]{1,0:T(8,128)(2,1)}, u32[]{:S(2)}, u32[]{:S(2)}) collective-permute-start(bf16[512,1152]{1,0:T(8,128)(2,1)} %get-tuple-element.17), channel_id=1, source_target_pairs={{0,1},{1,2},{2,3},{3,0},{4,5},{5,6},{6,7},{7,4},{8,9},{9,10},{10,1... | collective-permute-start | bytes 3538952 | tf_op jit(solution)/shard_map/ppermute | solution.py:519
  45.5 73.0 %collective-permute-start.8 = (bf16[512,1152]{1,0:T(8,128)(2,1)}, bf16[512,1152]{1,0:T(8,128)(2,1)}, u32[]{:S(2)}, u32[]{:S(2)}) collective-permute-start(bf16[512,1152]{1,0:T(8,128)(2,1)} %get-tuple-element.16), channel_id=1, source_target_pairs={{0,2},{1,3},{2,0},{3,1},{4,6},{5,7},{6,4},{7,5},{8,10},{9,11},{10,... | collective-permute-start | bytes 3538952 | tf_op jit(solution)/shard_map/ppermute | solution.py:519
  48.8 16.3 %collective-permute-start.1 = (bf16[2048,128]{1,0:T(8,128)(2,1)S(1)}, bf16[2048,128]{1,0:T(8,128)(2,1)S(1)}, u32[]{:S(2)}, u32[]{:S(2)}) collective-permute-start(bf16[2048,128]{1,0:T(8,128)(2,1)S(1)} %collective-permute-done.refs_0_), channel_id=1, source_target_pairs={{0,4},{4,0},{1,5},{5,1},{2,6},{6,2},{3,7},{7,3},{8,12},{12,8},{9,1... | collective-permute-start | bytes 1572872 | tf_op jit(solution)/shard_map/ppermute | solution.py:509
  50.0 15.1 %collective-permute-start.3 = (bf16[2048,128]{1,0:T(8,128)(2,1)S(1)}, bf16[2048,128]{1,0:T(8,128)(2,1)S(1)}, u32[]{:S(2)}, u32[]{:S(2)}) collective-permute-start(bf16[2048,128]{1,0:T(8,128)(2,1)S(1)} %collective-permute-done.2.refs_2_), channel_id=1, source_target_pairs={{0,4},{4,0},{1,5},{5,1},{2,6},{6,2},{3,7},{7,3},{8,12},{12,8},{9,1... | collective-permute-start | bytes 1572872 | tf_op jit(solution)/shard_map/ppermute | solution.py:509
  57.0 62.7 %collective-permute-start.9 = (bf16[512,1152]{1,0:T(8,128)(2,1)}, bf16[512,1152]{1,0:T(8,128)(2,1)}, u32[]{:S(2)}, u32[]{:S(2)}) collective-permute-start(bf16[512,1152]{1,0:T(8,128)(2,1)} %get-tuple-element.15), channel_id=1, source_target_pairs={{0,3},{1,0},{2,1},{3,2},{4,7},{5,4},{6,5},{7,6},{8,11},{9,8},{10,9... | collective-permute-start | bytes 3538952 | tf_op jit(solution)/shard_map/ppermute | solution.py:519
  71.7 4.2 %copy-start.4 = (f32[1152]{0:T(1024)S(1)}, f32[1152]{0:T(1024)}, u32[]{:S(2)}) copy-start(f32[1152]{0:T(1024)} %param.17) | copy-start | bytes 13828
  71.7 48.0 %copy-start.5 = (s32[8]{0:T(128)S(1)}, s32[8]{0:T(128)}, u32[]{:S(2)}) copy-start(s32[8]{0:T(128)} %param.19) | copy-start | bytes 100
  71.7 48.3 %copy-start.2 = (s32[8]{0:T(128)S(1)}, s32[8]{0:T(128)}, u32[]{:S(2)}) copy-start(s32[8]{0:T(128)} %pick_ref.1) | copy-start | bytes 100
  71.7 52.5 %all-to-all-start.1 = ((bf16[32,256,128]{2,1,0:T(8,128)(2,1)}), bf16[32,256,128]{2,1,0:T(8,128)(2,1)S(1)}, u32[]{:S(2)}, u32[]{:S(2)}) async-start(bf16[32,256,128]{2,1,0:T(8,128)(2,1)} %bitcast.35), calls=%async_computation.1 | async-start | bytes 4194304 | tf_op jit(solution)/shard_map/all_to_all | solution.py:75
  75.9 46.6 %collective-permute-start.10 = (bf16[512,1152]{1,0:T(8,128)(2,1)}, bf16[512,1152]{1,0:T(8,128)(2,1)}, u32[]{:S(2)}, u32[]{:S(2)}) collective-permute-start(bf16[512,1152]{1,0:T(8,128)(2,1)} %collective-permute-done.7.a1), channel_id=1, source_target_pairs={{0,4},{4,0},{1,5},{5,1},{2,6},{6,2},{3,7},{7,3},{8,12},{12,8},{9,1... | collective-permute-start | bytes 3538952 | tf_op jit(solution)/shard_map/ppermute | solution.py:509
  118.4 4.1 %collective-permute-start.11 = (bf16[512,1152]{1,0:T(8,128)(2,1)}, bf16[512,1152]{1,0:T(8,128)(2,1)}, u32[]{:S(2)}, u32[]{:S(2)}) collective-permute-start(bf16[512,1152]{1,0:T(8,128)(2,1)} %collective-permute-done.8.a2), channel_id=1, source_target_pairs={{0,4},{4,0},{1,5},{5,1},{2,6},{6,2},{3,7},{7,3},{8,12},{12,8},{9,1... | collective-permute-start | bytes 3538952 | tf_op jit(solution)/shard_map/ppermute | solution.py:509
  119.7 4.5 %collective-permute-start.12 = (bf16[512,1152]{1,0:T(8,128)(2,1)}, bf16[512,1152]{1,0:T(8,128)(2,1)}, u32[]{:S(2)}, u32[]{:S(2)}) collective-permute-start(bf16[512,1152]{1,0:T(8,128)(2,1)} %collective-permute-done.9.a3), channel_id=1, source_target_pairs={{0,4},{4,0},{1,5},{5,1},{2,6},{6,2},{3,7},{7,3},{8,12},{12,8},{9,1... | collective-permute-start | bytes 3538952 | tf_op jit(solution)/shard_map/ppermute | solution.py:509
  122.5 13.7 %copy-start.6 = (s32[8]{0:T(128)S(1)}, s32[8]{0:T(128)}, u32[]{:S(2)}) copy-start(s32[8]{0:T(128)} %param.20) | copy-start | bytes 100
  132.8 11.8 %all-to-all-start.2 = ((f32[4,24,1152]{2,1,0:T(8,128)}), f32[4,24,1152]{2,1,0:T(8,128)S(1)}, u32[]{:S(2)}, u32[]{:S(2)}) async-start(f32[4,24,1152]{2,1,0:T(8,128)} %get-tuple-element.10), calls=%async_computation.2 | async-start | bytes 884736 | tf_op jit(solution)/shard_map/all_to_all | solution.py:75
  175.9 17.1 %copy-start = (bf16[16,8,4736]{2,1,0:T(8,128)(2,1)}, bf16[16,8,4736]{2,1,0:T(8,128)(2,1)S(1)}, u32[]{:S(2)}) copy-start(bf16[16,8,4736]{2,1,0:T(8,128)(2,1)S(1)} %all_to_all.26) | copy-start | bytes 3637252
  176.0 5.3 %collective-permute-start.13 = (bf16[128,4736]{1,0:T(8,128)(2,1)S(1)}, bf16[128,4736]{1,0:T(8,128)(2,1)S(1)}, u32[]{:S(2)}, u32[]{:S(2)}) collective-permute-start(bf16[128,4736]{1,0:T(8,128)(2,1)S(1)} %bitcast.23), channel_id=1, source_target_pairs={{0,4},{4,0},{1,5},{5,1},{2,6},{6,2},{3,7},{7,3},{8,12},{12,8},{9,1... | collective-permute-start | bytes 3637256 | tf_op jit(solution)/shard_map/ppermute | solution.py:509
  181.2 11.9 %copy-start.1 = (bf16[128,4736]{1,0:T(8,128)(2,1)}, bf16[128,4736]{1,0:T(8,128)(2,1)S(1)}, u32[]{:S(2)}) copy-start(bf16[128,4736]{1,0:T(8,128)(2,1)S(1)} %collective-permute-done.13.s_ref) | copy-start | bytes 3637252
  193.1 5.0 %collective-permute-start.14 = (bf16[4,128,2560]{2,1,0:T(8,128)(2,1)S(1)}, bf16[4,128,2560]{2,1,0:T(8,128)(2,1)S(1)}, u32[]{:S(2)}, u32[]{:S(2)}) collective-permute-start(bf16[4,128,2560]{2,1,0:T(8,128)(2,1)S(1)} %get-tuple-element.12), channel_id=1, source_target_pairs={{0,4},{4,0},{1,5},{5,1},{2,6},{6,2},{3,7},{7,3},{8,12},{12,8},{9,1... | collective-permute-start | bytes 7864328 | tf_op jit(solution)/shard_map/ppermute | solution.py:509
  200.3 39.0 %all-to-all-start.4 = ((bf16[64,8,2560]{2,1,0:T(8,128)(2,1)}), bf16[64,8,2560]{2,1,0:T(8,128)(2,1)S(1)}, u32[]{:S(2)}, u32[]{:S(2)}) async-start(bf16[64,8,2560]{2,1,0:T(8,128)(2,1)} %bitcast.34), calls=%async_computation.4 | async-start | bytes 5242880 | tf_op jit(solution)/shard_map/all_to_all | solution.py:75
  (1 other events, 4.2 us)

commit v6 on v5

--- a/solution.py
+++ b/solution.py
@@ -53,22 +53,22 @@
 VMEM_SPEC = pl.BlockSpec(memory_space=pltpu.MemorySpace.VMEM)
 
 
-def pack_kernel(q_ref, k_ref, v_ref, out_ref):
-    for h in range(8):
-        out_ref[h, :BLK, :] = q_ref[:, h * HEAD_DIM : (h + 1) * HEAD_DIM]
-        other = (k_ref, v_ref)[h % 2]
-        out_ref[h, BLK:, :] = other[:, h // 2 * HEAD_DIM : (h // 2 + 1) * HEAD_DIM]
-
-
-def pack(q, k, v):
+def by_head(*blocks):
+    count = sum(b.shape[1] for b in blocks) // HEAD_DIM
+
+    def kernel(*refs):
+        for h in range(count):
+            ref, at = refs[h % len(blocks)], h // len(blocks) * HEAD_DIM
+            refs[-1][h] = ref[:, at : at + HEAD_DIM]
+
     whole = lambda *dims: pl.BlockSpec(dims, lambda i: (0,) * len(dims))
     return pl.pallas_call(
-        pack_kernel,
-        out_shape=pltpu.MemorySpace.HBM((8, SPAN, HEAD_DIM), bf16),
+        kernel,
+        out_shape=pltpu.MemorySpace.HBM((count, BLK, HEAD_DIM), bf16),
         grid=(1,),
-        in_specs=[whole(BLK, 8 * HEAD_DIM), whole(BLK, 4 * HEAD_DIM), whole(BLK, 4 * HEAD_DIM)],
-        out_specs=whole(8, SPAN, HEAD_DIM),
-    )(q, k, v)
+        in_specs=[whole(*b.shape) for b in blocks],
+        out_specs=whole(count, BLK, HEAD_DIM),
+    )(*blocks)
 
 
 def exchange(pieces, axes):
@@ -501,10 +501,10 @@
         [zi, ci, jnp.where(yi >= 1, 0, 1), jnp.where(yi == 3, 0, 1), jnp.where(yi >= 2, 0, 1), base, (xi * 4 + yi) * PICK]
     ).astype(jnp.int32)
 
-    packed = pack(query_rows, key_rows, value_rows)
-    got = exchange(packed, ("x", "core"))
-    q = got[:, :BLK].reshape(4, SPAN, HEAD_DIM)
-    own = got[:, BLK:].reshape(4 * SPAN, HEAD_DIM)
+    packed = by_head(key_rows, value_rows)
+    own = exchange(packed, ("x", "core")).reshape(4 * SPAN, HEAD_DIM)
+    packed = by_head(query_rows)
+    q = exchange(packed, ("x", "core")).reshape(4, SPAN, HEAD_DIM)
 
     swap = lambda a: lax.ppermute(a, "core", SWAP)
     own_pair = [own, swap(own)]

time: 243 us -> 237 us (0.975)
  waiting for transfers between devices: 97.4 us -> 90.4 us
  blocking collectives: 51.8 us -> 46.2 us
  starting transfers between devices: 36.6 us -> 40.5 us
  Pallas kernels: 40.6 us -> 43.1 us
    ppermute x3, waiting for transfers between devices: 8.72 us -> 2.83 us  [shards(): got_y.append(lax.ppermute(own, 'y', ring(k)))]
    all_to_all x2, blocking collectives: 51.8 us -> 46.2 us  [exchange(): return lax.all_to_all(pieces, axes, 0, 0, tiled=True)]
    all_to_all x3 -> x4, starting transfers between devices: 12.4 us -> 16.4 us  [exchange(): return lax.all_to_all(pieces, axes, 0, 0, tiled=True)]
    all_to_all x3 -> x4, waiting for transfers between devices: 37.8 us -> 37.8 us  [exchange(): return lax.all_to_all(pieces, axes, 0, 0, tiled=True)]
  transfers between devices with their start and end apart: 18 -> 19, of which waited for: 8 -> 8; matrix products, arithmetic and copies ran while one was open for 5% -> 5% of each run, Pallas kernels for 7% -> 8%
where the time goes in v6:
time: 237 us; the launch traced here: 235 us
  waiting for transfers between devices  90.4 us (38%)
  blocking collectives  46.2 us (19%)
  Pallas kernels  43.1 us (18%)
  starting transfers between devices  40.5 us (17%)
  other arithmetic  7.39 us (3%)
  local copies, waits for them, and re-layouts  6.14 us (3%)
    all_to_all x2, blocking collectives, exchange(): return lax.all_to_all(pieces, axes, 0, 0, tiled=True)  46.2 us
    ppermute x3, waiting for transfers between devices, shards(): mine.append(lax.ppermute(part, 'vocab', ring(s)))  41 us
    all_to_all x4, waiting for transfers between devices, exchange(): return lax.all_to_all(pieces, axes, 0, 0, tiled=True)  37.8 us
    pallas_call x3, Pallas kernels, attn_call(): pl.pallas_call(kernel, out_shape=out_shape, grid_spec=pltpu.PrefetchScala...  17 us
    all_to_all x4, starting transfers between devices, exchange(): return lax.all_to_all(pieces, axes, 0, 0, tiled=True)  16.4 us
    pallas_call x1, Pallas kernels, loss_parts(): pl.pallas_call(loss_kernel, out_shape=(jax.ShapeDtypeStruct((4, 128, WIDE...  11.8 us
    ppermute x9, starting transfers between devices, shards(): swap = lambda a: lax.ppermute(a, 'core', SWAP)  10.9 us
    ppermute x3, starting transfers between devices, shards(): mine.append(lax.ppermute(part, 'vocab', ring(s)))  8.82 us
  transfers between devices with their start and end apart: 19, of which 8 were waited for; matrix products, arithmetic and copies ran while one was open for 5% of the time, Pallas kernels for 8%

profile of v6, /device:TPU:1, one launch (start us, length us, event | category | flops | bytes accessed | tf_op | source)
XLA Modules:
  0.0 234.8 jit_solution(12228507784438390700)
XLA Ops:
  2.5 15.1 %all_to_all.30 = bf16[8,256,128]{2,1,0:T(8,128)(2,1)S(1)} all-to-all(bf16[8,256,128]{2,1,0:T(8,128)(2,1)} %shard_map.131), channel_id=1, replica_groups=mesh['x'=4,'y'=4,'core'=2,'vocab'=4] {'x','core'}, dimensions={0} | all-to-all | bytes 1048576 | tf_op jit(solution)/shard_map/all_to_all | solution.py:75
  25.3 4.0 %all-to-all-start = ((bf16[8,256,128]{2,1,0:T(8,128)(2,1)}), bf16[8,256,128]{2,1,0:T(8,128)(2,1)S(1)}, u32[]{:S(2)}, u32[]{:S(2)}) async-start(bf16[8,256,128]{2,1,0:T(8,128)(2,1)} %shard_map.130), calls=%async_computation | async-start | bytes 1048576 | tf_op jit(solution)/shard_map/all_to_all | solution.py:75
  29.2 2.2 collective-permute-done.4.refs_0_
  31.4 2.2 collective-permute-start.5
  33.6 3.9 %fusion.7 = (bf16[512,1152]{1,0:T(8,128)(2,1)}, bf16[512,1152]{1,0:T(8,128)(2,1)}, bf16[512,1152]{1,0:T(8,128)(2,1)}) fusion(bf16[1024,4608]{1,0:T(8,128)(2,1)} %w_ref.1, s32[]{:T(128)S(6)} %select_n.59, s32[]{:T(128)S(6)} %select_n.65, s32[]{:T(128)S(6)} %select_n.63, s32[]{:T(128)S(6)} %select_n.61), kind=kLoop, calls=%fused_computation.24 | loop fusion | bytes 7077904 | tf_op jit(solution)/shard_map/dynamic_slice | solution.py:518
  39.2 3.4 %collective-permute-start.8 = (bf16[512,1152]{1,0:T(8,128)(2,1)}, bf16[512,1152]{1,0:T(8,128)(2,1)}, u32[]{:S(2)}, u32[]{:S(2)}) collective-permute-start(bf16[512,1152]{1,0:T(8,128)(2,1)} %get-tuple-element.16), channel_id=1, source_target_pairs={{0,2},{1,3},{2,0},{3,1},{4,6},{5,7},{6,4},{7,5},{8,10},{9,11},{10,... | collective-permute-start | bytes 3538952 | tf_op jit(solution)/shard_map/ppermute | solution.py:519
  45.7 5.1 %shard_map.132.refs_2_ = f32[4,512,256]{2,1,0:T(8,128)S(1)} custom-call(s32[7]{0:T(128)S(1)} %stack.61.sc_ref, bf16[4,512,128]{2,1,0:T(8,128)(2,1)S(1)} %bitcast.26, bf16[2048,128]{1,0:T(8,128)(2,1)S(1)} %bitcast.33, bf16[2048,128]{1,0:T(8,128)(2,1)} %collective-permute-done.6.b_ref), custom_call_target="tpu_custom_call" | custom-call | flops 5000000000 | bytes 4000000 | tf_op jit(solution)/shard_map/pallas_call | solution.py:252
  50.8 3.8 %collective-permute-start.9 = (bf16[512,1152]{1,0:T(8,128)(2,1)}, bf16[512,1152]{1,0:T(8,128)(2,1)}, u32[]{:S(2)}, u32[]{:S(2)}) collective-permute-start(bf16[512,1152]{1,0:T(8,128)(2,1)} %get-tuple-element.15), channel_id=1, source_target_pairs={{0,3},{1,0},{2,1},{3,2},{4,7},{5,4},{6,5},{7,6},{8,11},{9,8},{10,9... | collective-permute-start | bytes 3538952 | tf_op jit(solution)/shard_map/ppermute | solution.py:519
  54.6 4.3 %shard_map.133.refs_4_ = f32[4,512,256]{2,1,0:T(8,128)S(1)} custom-call(s32[7]{0:T(128)S(1)} %stack.61.sc_ref, bf16[4,512,128]{2,1,0:T(8,128)(2,1)S(1)} %bitcast.27, bf16[2048,128]{1,0:T(8,128)(2,1)S(1)} %collective-permute-done.4.refs_0_, bf16[2048,128]{1,0:T(8,128)(2,1)} %collective-permute-done.5.refs_1_, f32[4,512,256]{2,1,0:T(8,128)S(1)} %shard_map.132.refs_2_), custom_call_target="tpu_custom_call" | custom-call | flops 5000000000 | bytes 4000000 | tf_op jit(solution)/shard_map/pallas_call | solution.py:252
  58.9 7.6 %shard_map.134 = bf16[4,2,4,256,128]{4,3,2,1,0:T(8,128)(2,1)} custom-call(s32[7]{0:T(128)S(1)} %stack.61.sc_ref, bf16[4,512,128]{2,1,0:T(8,128)(2,1)S(1)} %bitcast.28, bf16[2048,128]{1,0:T(8,128)(2,1)S(1)} %collective-permute-done.refs_0_, bf16[2048,128]{1,0:T(8,128)(2,1)} %collective-permute-done.1.refs_1_, ...), custom_call_target="tpu_custom_call" | custom-call | flops 10000000000 | bytes 4000000 | tf_op jit(solution)/shard_map/pallas_call | solution.py:252
  66.6 4.1 %all-to-all-start.2 = ((bf16[32,256,128]{2,1,0:T(8,128)(2,1)}), bf16[32,256,128]{2,1,0:T(8,128)(2,1)S(1)}, u32[]{:S(2)}, u32[]{:S(2)}) async-start(bf16[32,256,128]{2,1,0:T(8,128)(2,1)} %bitcast.35), calls=%async_computation.2 | async-start | bytes 4194304 | tf_op jit(solution)/shard_map/all_to_all | solution.py:75
  71.2 41.0 %collective-permute-done.8.a2 = bf16[512,1152]{1,0:T(8,128)(2,1)} collective-permute-done((bf16[512,1152]{1,0:T(8,128)(2,1)}, bf16[512,1152]{1,0:T(8,128)(2,1)}, u32[]{:S(2)}, u32[]{:S(2)}) %collective-permute-start.8) | collective-permute-done | bytes 1179680 | tf_op jit(solution)/shard_map/ppermute | solution.py:519
  118.0 8.5 %shard_map.135 = (f32[256,1152]{1,0:T(8,128)}, f32[4,24,1152]{2,1,0:T(8,128)}) custom-call(s32[7]{0:T(128)S(1)} %stack.61.sc_ref, s32[8]{0:T(128)S(1)} %copy-done.2, bf16[32,256,128]{2,1,0:T(8,128)(2,1)S(1)} %all-to-all-done.2.att_ref, bf16[1024,4608]{1,0:T(8,128)(2,1)} %w_ref.1, bf16[512,1152]{1,0:T(8,128)(2,1)} %collective-permute-done.7.a1, ...), custom_call_target="tpu_custom_call" | custom-call | tf_op jit(solution)/shard_map/pallas_call | solution.py:316
  126.5 3.5 %all-to-all-start.3 = ((f32[4,24,1152]{2,1,0:T(8,128)}), f32[4,24,1152]{2,1,0:T(8,128)S(1)}, u32[]{:S(2)}, u32[]{:S(2)}) async-start(f32[4,24,1152]{2,1,0:T(8,128)} %get-tuple-element.10), calls=%async_computation.3 | async-start | bytes 884736 | tf_op jit(solution)/shard_map/all_to_all | solution.py:75
  130.2 8.1 %all-to-all-done.3.zr_ref = f32[4,24,1152]{2,1,0:T(8,128)S(1)} async-done(((f32[4,24,1152]{2,1,0:T(8,128)}), f32[4,24,1152]{2,1,0:T(8,128)S(1)}, u32[]{:S(2)}, u32[]{:S(2)}) %all-to-all-start.3) | async-done | bytes 442400 | tf_op jit(solution)/shard_map/all_to_all | solution.py:75
  138.6 31.1 %all_to_all.31 = bf16[16,8,4736]{2,1,0:T(8,128)(2,1)S(1)} all-to-all(bf16[16,8,4736]{2,1,0:T(8,128)(2,1)S(1)} %shard_map.136), channel_id=1, replica_groups=mesh['x'=4,'y'=4,'core'=2,'vocab'=4] {'x','y'}, dimensions={0} | all-to-all | bytes 2424832 | tf_op jit(solution)/shard_map/all_to_all | solution.py:75
  169.7 2.8 %collective-permute-start.13 = (bf16[128,4736]{1,0:T(8,128)(2,1)S(1)}, bf16[128,4736]{1,0:T(8,128)(2,1)S(1)}, u32[]{:S(2)}, u32[]{:S(2)}) collective-permute-start(bf16[128,4736]{1,0:T(8,128)(2,1)S(1)} %bitcast.23), channel_id=1, source_target_pairs={{0,4},{4,0},{1,5},{5,1},{2,6},{6,2},{3,7},{7,3},{8,12},{12,8},{9,1... | collective-permute-start | bytes 3637256 | tf_op jit(solution)/shard_map/ppermute | solution.py:509
  172.5 2.5 %collective-permute-done.13.s_ref = bf16[128,4736]{1,0:T(8,128)(2,1)S(1)} collective-permute-done((bf16[128,4736]{1,0:T(8,128)(2,1)S(1)}, bf16[128,4736]{1,0:T(8,128)(2,1)S(1)}, u32[]{:S(2)}, u32[]{:S(2)}) %collective-permute-start.13) | collective-permute-done | bytes 1212448 | tf_op jit(solution)/shard_map/ppermute | solution.py:509
  175.0 11.8 %shard_map.137 = (bf16[4,128,2560]{2,1,0:T(8,128)(2,1)S(1)}, bf16[4,128,2560]{2,1,0:T(8,128)(2,1)S(1)}) custom-call(s32[7]{0:T(128)S(1)} %stack.61.sc_ref, bf16[128,4736]{1,0:T(8,128)(2,1)S(1)} %bitcast.24, bf16[128,4736]{1,0:T(8,128)(2,1)S(1)} %collective-permute-done.13.s_ref, bf16[1024,4608]{1,0:T(8,128)(2,1)} %e_ref.1), custom_call_target="tpu_custom_call" | custom-call | tf_op jit(solution)/shard_map/pallas_call | solution.py:432
  187.3 4.5 %collective-permute-done.14 = bf16[4,128,2560]{2,1,0:T(8,128)(2,1)S(1)} collective-permute-done((bf16[4,128,2560]{2,1,0:T(8,128)(2,1)S(1)}, bf16[4,128,2560]{2,1,0:T(8,128)(2,1)S(1)}, u32[]{:S(2)}, u32[]{:S(2)}) %collective-permute-start.14) | collective-permute-done | bytes 2621472 | tf_op jit(solution)/shard_map/ppermute | solution.py:509
  191.9 2.2 add_convert_fusion
  194.1 4.9 %all-to-all-start.5 = ((bf16[64,8,2560]{2,1,0:T(8,128)(2,1)}), bf16[64,8,2560]{2,1,0:T(8,128)(2,1)S(1)}, u32[]{:S(2)}, u32[]{:S(2)}) async-start(bf16[64,8,2560]{2,1,0:T(8,128)(2,1)} %bitcast.34), calls=%async_computation.5 | async-start | bytes 5242880 | tf_op jit(solution)/shard_map/all_to_all | solution.py:75
  199.0 2.5 %add_convert_fusion.1 = bf16[256,1152]{1,0:T(8,128)(2,1)} fusion(f32[256,1152]{1,0:T(8,128)} %get-tuple-element.9, bf16[256,1152]{1,0:T(8,128)(2,1)} %param.14, f32[1152]{0:T(1024)S(1)} %copy-done.3, f32[256]{0:T(256)S(1)} %add_rsqrt_fusion), kind=kLoop, calls=%fused_computation.2 | loop fusion | flops 1474560 | bytes 2364928 | tf_op jit(solution)/shard_map/convert_element_type | solution.py:534
  203.3 29.7 %all-to-all-done.5.back_ref = bf16[64,8,2560]{2,1,0:T(8,128)(2,1)S(1)} async-done(((bf16[64,8,2560]{2,1,0:T(8,128)(2,1)}), bf16[64,8,2560]{2,1,0:T(8,128)(2,1)S(1)}, u32[]{:S(2)}, u32[]{:S(2)}) %all-to-all-start.5) | async-done | bytes 2621472 | tf_op jit(solution)/shard_map/all_to_all | solution.py:75
  (62 shorter events, 25.2 us)
Async XLA Ops:
  17.6 13.8 %collective-permute-start.4 = (bf16[2048,128]{1,0:T(8,128)(2,1)S(1)}, bf16[2048,128]{1,0:T(8,128)(2,1)S(1)}, u32[]{:S(2)}, u32[]{:S(2)}) collective-permute-start(bf16[2048,128]{1,0:T(8,128)(2,1)S(1)} %bitcast.29), channel_id=1, source_target_pairs={{0,8},{8,16},{16,24},{24,0},{1,9},{9,17},{17,25},{25,1},{2,10},{10... | collective-permute-start | bytes 1572872 | tf_op jit(solution)/shard_map/ppermute | solution.py:513
  18.9 20.3 %collective-permute-start.6 = (bf16[2048,128]{1,0:T(8,128)(2,1)S(1)}, bf16[2048,128]{1,0:T(8,128)(2,1)}, u32[]{:S(2)}, u32[]{:S(2)}) collective-permute-start(bf16[2048,128]{1,0:T(8,128)(2,1)S(1)} %bitcast.30), channel_id=1, source_target_pairs={{0,4},{4,0},{1,5},{5,1},{2,6},{6,2},{3,7},{7,3},{8,12},{12,8},{9,1... | collective-permute-start | bytes 1572872 | tf_op jit(solution)/shard_map/ppermute | solution.py:509
  20.3 22.3 %collective-permute-start = (bf16[2048,128]{1,0:T(8,128)(2,1)S(1)}, bf16[2048,128]{1,0:T(8,128)(2,1)S(1)}, u32[]{:S(2)}, u32[]{:S(2)}) collective-permute-start(bf16[2048,128]{1,0:T(8,128)(2,1)S(1)} %bitcast.31), channel_id=1, source_target_pairs={{0,24},{8,0},{16,8},{24,16},{1,25},{9,1},{17,9},{25,17},{2,26},{10... | collective-permute-start | bytes 1572872 | tf_op jit(solution)/shard_map/ppermute | solution.py:513
  21.6 22.1 %collective-permute-start.2 = (bf16[2048,128]{1,0:T(8,128)(2,1)S(1)}, bf16[2048,128]{1,0:T(8,128)(2,1)S(1)}, u32[]{:S(2)}, u32[]{:S(2)}) collective-permute-start(bf16[2048,128]{1,0:T(8,128)(2,1)S(1)} %bitcast.32), channel_id=1, source_target_pairs={{0,16},{8,24},{16,0},{24,8},{1,17},{9,25},{17,1},{25,9},{2,18},{10... | collective-permute-start | bytes 1572872 | tf_op jit(solution)/shard_map/ppermute | solution.py:513
  25.3 20.4 %all-to-all-start = ((bf16[8,256,128]{2,1,0:T(8,128)(2,1)}), bf16[8,256,128]{2,1,0:T(8,128)(2,1)S(1)}, u32[]{:S(2)}, u32[]{:S(2)}) async-start(bf16[8,256,128]{2,1,0:T(8,128)(2,1)} %shard_map.130), calls=%async_computation | async-start | bytes 1048576 | tf_op jit(solution)/shard_map/all_to_all | solution.py:75
  31.4 19.3 %collective-permute-start.5 = (bf16[2048,128]{1,0:T(8,128)(2,1)S(1)}, bf16[2048,128]{1,0:T(8,128)(2,1)}, u32[]{:S(2)}, u32[]{:S(2)}) collective-permute-start(bf16[2048,128]{1,0:T(8,128)(2,1)S(1)} %collective-permute-done.4.refs_0_), channel_id=1, source_target_pairs={{0,4},{4,0},{1,5},{5,1},{2,6},{6,2},{3,7},{7,3},{8,12},{12,8},{9,1... | collective-permute-start | bytes 1572872 | tf_op jit(solution)/shard_map/ppermute | solution.py:509
  37.5 33.3 %collective-permute-start.7 = (bf16[512,1152]{1,0:T(8,128)(2,1)}, bf16[512,1152]{1,0:T(8,128)(2,1)}, u32[]{:S(2)}, u32[]{:S(2)}) collective-permute-start(bf16[512,1152]{1,0:T(8,128)(2,1)} %get-tuple-element.17), channel_id=1, source_target_pairs={{0,1},{1,2},{2,3},{3,0},{4,5},{5,6},{6,7},{7,4},{8,9},{9,10},{10,1... | collective-permute-start | bytes 3538952 | tf_op jit(solution)/shard_map/ppermute | solution.py:519
  39.2 73.0 %collective-permute-start.8 = (bf16[512,1152]{1,0:T(8,128)(2,1)}, bf16[512,1152]{1,0:T(8,128)(2,1)}, u32[]{:S(2)}, u32[]{:S(2)}) collective-permute-start(bf16[512,1152]{1,0:T(8,128)(2,1)} %get-tuple-element.16), channel_id=1, source_target_pairs={{0,2},{1,3},{2,0},{3,1},{4,6},{5,7},{6,4},{7,5},{8,10},{9,11},{10,... | collective-permute-start | bytes 3538952 | tf_op jit(solution)/shard_map/ppermute | solution.py:519
  42.6 16.3 %collective-permute-start.1 = (bf16[2048,128]{1,0:T(8,128)(2,1)S(1)}, bf16[2048,128]{1,0:T(8,128)(2,1)}, u32[]{:S(2)}, u32[]{:S(2)}) collective-permute-start(bf16[2048,128]{1,0:T(8,128)(2,1)S(1)} %collective-permute-done.refs_0_), channel_id=1, source_target_pairs={{0,4},{4,0},{1,5},{5,1},{2,6},{6,2},{3,7},{7,3},{8,12},{12,8},{9,1... | collective-permute-start | bytes 1572872 | tf_op jit(solution)/shard_map/ppermute | solution.py:509
  43.8 15.1 %collective-permute-start.3 = (bf16[2048,128]{1,0:T(8,128)(2,1)S(1)}, bf16[2048,128]{1,0:T(8,128)(2,1)}, u32[]{:S(2)}, u32[]{:S(2)}) collective-permute-start(bf16[2048,128]{1,0:T(8,128)(2,1)S(1)} %collective-permute-done.2.refs_2_), channel_id=1, source_target_pairs={{0,4},{4,0},{1,5},{5,1},{2,6},{6,2},{3,7},{7,3},{8,12},{12,8},{9,1... | collective-permute-start | bytes 1572872 | tf_op jit(solution)/shard_map/ppermute | solution.py:509
  50.8 62.7 %collective-permute-start.9 = (bf16[512,1152]{1,0:T(8,128)(2,1)}, bf16[512,1152]{1,0:T(8,128)(2,1)}, u32[]{:S(2)}, u32[]{:S(2)}) collective-permute-start(bf16[512,1152]{1,0:T(8,128)(2,1)} %get-tuple-element.15), channel_id=1, source_target_pairs={{0,3},{1,0},{2,1},{3,2},{4,7},{5,4},{6,5},{7,6},{8,11},{9,8},{10,9... | collective-permute-start | bytes 3538952 | tf_op jit(solution)/shard_map/ppermute | solution.py:519
  66.6 46.9 %copy-start.5 = (s32[8]{0:T(128)S(1)}, s32[8]{0:T(128)}, u32[]{:S(2)}) copy-start(s32[8]{0:T(128)} %param.19) | copy-start | bytes 100
  66.6 47.2 %copy-start.2 = (s32[8]{0:T(128)S(1)}, s32[8]{0:T(128)}, u32[]{:S(2)}) copy-start(s32[8]{0:T(128)} %pick_ref.1) | copy-start | bytes 100
  66.6 51.4 %all-to-all-start.2 = ((bf16[32,256,128]{2,1,0:T(8,128)(2,1)}), bf16[32,256,128]{2,1,0:T(8,128)(2,1)S(1)}, u32[]{:S(2)}, u32[]{:S(2)}) async-start(bf16[32,256,128]{2,1,0:T(8,128)(2,1)} %bitcast.35), calls=%async_computation.2 | async-start | bytes 4194304 | tf_op jit(solution)/shard_map/all_to_all | solution.py:75
  70.8 45.5 %collective-permute-start.10 = (bf16[512,1152]{1,0:T(8,128)(2,1)}, bf16[512,1152]{1,0:T(8,128)(2,1)}, u32[]{:S(2)}, u32[]{:S(2)}) collective-permute-start(bf16[512,1152]{1,0:T(8,128)(2,1)} %collective-permute-done.7.a1), channel_id=1, source_target_pairs={{0,4},{4,0},{1,5},{5,1},{2,6},{6,2},{3,7},{7,3},{8,12},{12,8},{9,1... | collective-permute-start | bytes 3538952 | tf_op jit(solution)/shard_map/ppermute | solution.py:509
  112.2 4.1 %collective-permute-start.11 = (bf16[512,1152]{1,0:T(8,128)(2,1)}, bf16[512,1152]{1,0:T(8,128)(2,1)}, u32[]{:S(2)}, u32[]{:S(2)}) collective-permute-start(bf16[512,1152]{1,0:T(8,128)(2,1)} %collective-permute-done.8.a2), channel_id=1, source_target_pairs={{0,4},{4,0},{1,5},{5,1},{2,6},{6,2},{3,7},{7,3},{8,12},{12,8},{9,1... | collective-permute-start | bytes 3538952 | tf_op jit(solution)/shard_map/ppermute | solution.py:509
  113.5 4.5 %collective-permute-start.12 = (bf16[512,1152]{1,0:T(8,128)(2,1)}, bf16[512,1152]{1,0:T(8,128)(2,1)}, u32[]{:S(2)}, u32[]{:S(2)}) collective-permute-start(bf16[512,1152]{1,0:T(8,128)(2,1)} %collective-permute-done.9.a3), channel_id=1, source_target_pairs={{0,4},{4,0},{1,5},{5,1},{2,6},{6,2},{3,7},{7,3},{8,12},{12,8},{9,1... | collective-permute-start | bytes 3538952 | tf_op jit(solution)/shard_map/ppermute | solution.py:509
  116.2 13.7 %copy-start.6 = (s32[8]{0:T(128)S(1)}, s32[8]{0:T(128)}, u32[]{:S(2)}) copy-start(s32[8]{0:T(128)} %param.20) | copy-start | bytes 100
  126.5 11.8 %all-to-all-start.3 = ((f32[4,24,1152]{2,1,0:T(8,128)}), f32[4,24,1152]{2,1,0:T(8,128)S(1)}, u32[]{:S(2)}, u32[]{:S(2)}) async-start(f32[4,24,1152]{2,1,0:T(8,128)} %get-tuple-element.10), calls=%async_computation.3 | async-start | bytes 884736 | tf_op jit(solution)/shard_map/all_to_all | solution.py:75
  169.7 17.1 %copy-start = (bf16[16,8,4736]{2,1,0:T(8,128)(2,1)}, bf16[16,8,4736]{2,1,0:T(8,128)(2,1)S(1)}, u32[]{:S(2)}) copy-start(bf16[16,8,4736]{2,1,0:T(8,128)(2,1)S(1)} %all_to_all.31) | copy-start | bytes 3637252
  169.7 5.3 %collective-permute-start.13 = (bf16[128,4736]{1,0:T(8,128)(2,1)S(1)}, bf16[128,4736]{1,0:T(8,128)(2,1)S(1)}, u32[]{:S(2)}, u32[]{:S(2)}) collective-permute-start(bf16[128,4736]{1,0:T(8,128)(2,1)S(1)} %bitcast.23), channel_id=1, source_target_pairs={{0,4},{4,0},{1,5},{5,1},{2,6},{6,2},{3,7},{7,3},{8,12},{12,8},{9,1... | collective-permute-start | bytes 3637256 | tf_op jit(solution)/shard_map/ppermute | solution.py:509
  175.0 11.9 %copy-start.1 = (bf16[128,4736]{1,0:T(8,128)(2,1)}, bf16[128,4736]{1,0:T(8,128)(2,1)S(1)}, u32[]{:S(2)}) copy-start(bf16[128,4736]{1,0:T(8,128)(2,1)S(1)} %collective-permute-done.13.s_ref) | copy-start | bytes 3637252
  186.9 5.0 %collective-permute-start.14 = (bf16[4,128,2560]{2,1,0:T(8,128)(2,1)S(1)}, bf16[4,128,2560]{2,1,0:T(8,128)(2,1)S(1)}, u32[]{:S(2)}, u32[]{:S(2)}) collective-permute-start(bf16[4,128,2560]{2,1,0:T(8,128)(2,1)S(1)} %get-tuple-element.12), channel_id=1, source_target_pairs={{0,4},{4,0},{1,5},{5,1},{2,6},{6,2},{3,7},{7,3},{8,12},{12,8},{9,1... | collective-permute-start | bytes 7864328 | tf_op jit(solution)/shard_map/ppermute | solution.py:509
  194.1 39.0 %all-to-all-start.5 = ((bf16[64,8,2560]{2,1,0:T(8,128)(2,1)}), bf16[64,8,2560]{2,1,0:T(8,128)(2,1)S(1)}, u32[]{:S(2)}, u32[]{:S(2)}) async-start(bf16[64,8,2560]{2,1,0:T(8,128)(2,1)} %bitcast.34), calls=%async_computation.5 | async-start | bytes 5242880 | tf_op jit(solution)/shard_map/all_to_all | solution.py:75
  (2 other events, 8.4 us)

commit v7 on v6

--- a/solution.py
+++ b/solution.py
@@ -286,16 +286,27 @@
     col = pl.multiple_of(zi * COLS, 128)
     src = [w_ref.at[pl.ds(0, 512), pl.ds(col, COLS)], w_ref.at[pl.ds(512, 512), pl.ds(col, COLS)]]
     src += [a1, a2, a3, b1, b2, b3]
-    copies = [pltpu.make_async_copy(src[n], wbuf.at[n], wsem.at[n]) for n in range(8)]
-    copies[0].start()
-    copies[1].start()
+    copies = [
+        pltpu.make_async_copy(src[n], wbuf.at[pl.ds(n * 512, 512)], wsem.at[n]) for n in range(8)
+    ]
+    for copy in copies[:4]:
+        copy.start()
     total = None
-    for n in range(8):
-        copies[n].wait()
-        if n + 2 < 8:
-            copies[n + 2].start()
-        lhs = jnp.concatenate([att_ref[heads[n] % 2 * 16 + h * 4 + heads[n] // 2] for h in range(4)], axis=1)
-        part = jnp.dot(lhs, wbuf[n], preferred_element_type=f32)
+    for pair in range(4):
+        for n in (2 * pair, 2 * pair + 1):
+            copies[n].wait()
+            if n + 4 < 8:
+                copies[n + 4].start()
+        lhs = jnp.concatenate(
+            [
+                att_ref[heads[n] % 2 * 16 + h * 4 + heads[n] // 2]
+                for n in (2 * pair, 2 * pair + 1)
+                for h in range(4)
+            ],
+            axis=1,
+        )
+        rows = slice(pair * 1024, (pair + 1) * 1024)
+        part = jnp.dot(lhs, wbuf[rows], preferred_element_type=f32)
         total = part if total is None else total + part
     own_ref[...] = total
     own = own_ref[...]
@@ -328,7 +339,7 @@
         scratch_shapes=[
             pltpu.VMEM((PICK, COLS), f32),
             pltpu.SemaphoreType.DMA(()),
-            pltpu.VMEM((8, 512, COLS), bf16),
+            pltpu.VMEM((8 * 512, COLS), bf16),
             pltpu.SemaphoreType.DMA((8,)),
         ],
         compiler_params=params(20),

time: 237 us -> 236 us (level)
  no operation moved by 1% of the time
where the time goes in v7:
time: 236 us; the launch traced here: 234 us
  waiting for transfers between devices  90.4 us (38%)
  blocking collectives  46.2 us (20%)
  Pallas kernels  42.4 us (18%)
  starting transfers between devices  40.5 us (17%)
  other arithmetic  7.39 us (3%)
  local copies, waits for them, and re-layouts  6.14 us (3%)
    all_to_all x2, blocking collectives, exchange(): return lax.all_to_all(pieces, axes, 0, 0, tiled=True)  46.2 us
    ppermute x3, waiting for transfers between devices, shards(): mine.append(lax.ppermute(part, 'vocab', ring(s)))  41 us
    all_to_all x4, waiting for transfers between devices, exchange(): return lax.all_to_all(pieces, axes, 0, 0, tiled=True)  37.8 us
    pallas_call x3, Pallas kernels, attn_call(): pl.pallas_call(kernel, out_shape=out_shape, grid_spec=pltpu.PrefetchScala...  17 us
    all_to_all x4, starting transfers between devices, exchange(): return lax.all_to_all(pieces, axes, 0, 0, tiled=True)  16.4 us
    pallas_call x1, Pallas kernels, loss_parts(): pl.pallas_call(loss_kernel, out_shape=(jax.ShapeDtypeStruct((4, 128, WIDE...  11.8 us
    ppermute x9, starting transfers between devices, shards(): swap = lambda a: lax.ppermute(a, 'core', SWAP)  10.9 us
    ppermute x3, starting transfers between devices, shards(): mine.append(lax.ppermute(part, 'vocab', ring(s)))  8.82 us
  transfers between devices with their start and end apart: 19, of which 8 were waited for; matrix products, arithmetic and copies ran while one was open for 5% of the time, Pallas kernels for 8%

profile of v7, /device:TPU:1, one launch (start us, length us, event | category | flops | bytes accessed | tf_op | source)
XLA Modules:
  0.0 234.1 jit_solution(1293402960551812124)
XLA Ops:
  2.5 15.1 %all_to_all.30 = bf16[8,256,128]{2,1,0:T(8,128)(2,1)S(1)} all-to-all(bf16[8,256,128]{2,1,0:T(8,128)(2,1)} %shard_map.131), channel_id=1, replica_groups=mesh['x'=4,'y'=4,'core'=2,'vocab'=4] {'x','core'}, dimensions={0} | all-to-all | bytes 1048576 | tf_op jit(solution)/shard_map/all_to_all | solution.py:75
  25.3 4.0 %all-to-all-start = ((bf16[8,256,128]{2,1,0:T(8,128)(2,1)}), bf16[8,256,128]{2,1,0:T(8,128)(2,1)S(1)}, u32[]{:S(2)}, u32[]{:S(2)}) async-start(bf16[8,256,128]{2,1,0:T(8,128)(2,1)} %shard_map.130), calls=%async_computation | async-start | bytes 1048576 | tf_op jit(solution)/shard_map/all_to_all | solution.py:75
  29.2 2.2 collective-permute-done.4.refs_0_
  31.4 2.2 collective-permute-start.5
  33.6 3.9 %fusion.7 = (bf16[512,1152]{1,0:T(8,128)(2,1)}, bf16[512,1152]{1,0:T(8,128)(2,1)}, bf16[512,1152]{1,0:T(8,128)(2,1)}) fusion(bf16[1024,4608]{1,0:T(8,128)(2,1)} %w_ref.1, s32[]{:T(128)S(6)} %select_n.59, s32[]{:T(128)S(6)} %select_n.65, s32[]{:T(128)S(6)} %select_n.63, s32[]{:T(128)S(6)} %select_n.61), kind=kLoop, calls=%fused_computation.24 | loop fusion | bytes 7077904 | tf_op jit(solution)/shard_map/dynamic_slice | solution.py:529
  39.2 3.4 %collective-permute-start.8 = (bf16[512,1152]{1,0:T(8,128)(2,1)}, bf16[512,1152]{1,0:T(8,128)(2,1)}, u32[]{:S(2)}, u32[]{:S(2)}) collective-permute-start(bf16[512,1152]{1,0:T(8,128)(2,1)} %get-tuple-element.16), channel_id=1, source_target_pairs={{0,2},{1,3},{2,0},{3,1},{4,6},{5,7},{6,4},{7,5},{8,10},{9,11},{10,... | collective-permute-start | bytes 3538952 | tf_op jit(solution)/shard_map/ppermute | solution.py:530
  45.7 5.1 %shard_map.132.refs_2_ = f32[4,512,256]{2,1,0:T(8,128)S(1)} custom-call(s32[7]{0:T(128)S(1)} %stack.61.sc_ref, bf16[4,512,128]{2,1,0:T(8,128)(2,1)S(1)} %bitcast.26, bf16[2048,128]{1,0:T(8,128)(2,1)S(1)} %bitcast.33, bf16[2048,128]{1,0:T(8,128)(2,1)} %collective-permute-done.6.b_ref), custom_call_target="tpu_custom_call" | custom-call | flops 5000000000 | bytes 4000000 | tf_op jit(solution)/shard_map/pallas_call | solution.py:252
  50.8 3.8 %collective-permute-start.9 = (bf16[512,1152]{1,0:T(8,128)(2,1)}, bf16[512,1152]{1,0:T(8,128)(2,1)}, u32[]{:S(2)}, u32[]{:S(2)}) collective-permute-start(bf16[512,1152]{1,0:T(8,128)(2,1)} %get-tuple-element.15), channel_id=1, source_target_pairs={{0,3},{1,0},{2,1},{3,2},{4,7},{5,4},{6,5},{7,6},{8,11},{9,8},{10,9... | collective-permute-start | bytes 3538952 | tf_op jit(solution)/shard_map/ppermute | solution.py:530
  54.6 4.3 %shard_map.133.refs_4_ = f32[4,512,256]{2,1,0:T(8,128)S(1)} custom-call(s32[7]{0:T(128)S(1)} %stack.61.sc_ref, bf16[4,512,128]{2,1,0:T(8,128)(2,1)S(1)} %bitcast.27, bf16[2048,128]{1,0:T(8,128)(2,1)S(1)} %collective-permute-done.4.refs_0_, bf16[2048,128]{1,0:T(8,128)(2,1)} %collective-permute-done.5.refs_1_, f32[4,512,256]{2,1,0:T(8,128)S(1)} %shard_map.132.refs_2_), custom_call_target="tpu_custom_call" | custom-call | flops 5000000000 | bytes 4000000 | tf_op jit(solution)/shard_map/pallas_call | solution.py:252
  58.9 7.6 %shard_map.134 = bf16[4,2,4,256,128]{4,3,2,1,0:T(8,128)(2,1)} custom-call(s32[7]{0:T(128)S(1)} %stack.61.sc_ref, bf16[4,512,128]{2,1,0:T(8,128)(2,1)S(1)} %bitcast.28, bf16[2048,128]{1,0:T(8,128)(2,1)S(1)} %collective-permute-done.refs_0_, bf16[2048,128]{1,0:T(8,128)(2,1)} %collective-permute-done.1.refs_1_, ...), custom_call_target="tpu_custom_call" | custom-call | flops 10000000000 | bytes 4000000 | tf_op jit(solution)/shard_map/pallas_call | solution.py:252
  66.6 4.1 %all-to-all-start.2 = ((bf16[32,256,128]{2,1,0:T(8,128)(2,1)}), bf16[32,256,128]{2,1,0:T(8,128)(2,1)S(1)}, u32[]{:S(2)}, u32[]{:S(2)}) async-start(bf16[32,256,128]{2,1,0:T(8,128)(2,1)} %bitcast.35), calls=%async_computation.2 | async-start | bytes 4194304 | tf_op jit(solution)/shard_map/all_to_all | solution.py:75
  71.2 41.0 %collective-permute-done.8.a2 = bf16[512,1152]{1,0:T(8,128)(2,1)} collective-permute-done((bf16[512,1152]{1,0:T(8,128)(2,1)}, bf16[512,1152]{1,0:T(8,128)(2,1)}, u32[]{:S(2)}, u32[]{:S(2)}) %collective-permute-start.8) | collective-permute-done | bytes 1179680 | tf_op jit(solution)/shard_map/ppermute | solution.py:530
  118.0 7.8 %shard_map.135 = (f32[256,1152]{1,0:T(8,128)}, f32[4,24,1152]{2,1,0:T(8,128)}) custom-call(s32[7]{0:T(128)S(1)} %stack.61.sc_ref, s32[8]{0:T(128)S(1)} %copy-done.2, bf16[32,256,128]{2,1,0:T(8,128)(2,1)S(1)} %all-to-all-done.2.att_ref, bf16[1024,4608]{1,0:T(8,128)(2,1)} %w_ref.1, bf16[512,1152]{1,0:T(8,128)(2,1)} %collective-permute-done.7.a1, ...), custom_call_target="tpu_custom_call" | custom-call | tf_op jit(solution)/shard_map/pallas_call | solution.py:327
  125.8 3.5 %all-to-all-start.3 = ((f32[4,24,1152]{2,1,0:T(8,128)}), f32[4,24,1152]{2,1,0:T(8,128)S(1)}, u32[]{:S(2)}, u32[]{:S(2)}) async-start(f32[4,24,1152]{2,1,0:T(8,128)} %get-tuple-element.10), calls=%async_computation.3 | async-start | bytes 884736 | tf_op jit(solution)/shard_map/all_to_all | solution.py:75
  129.5 8.1 %all-to-all-done.3.zr_ref = f32[4,24,1152]{2,1,0:T(8,128)S(1)} async-done(((f32[4,24,1152]{2,1,0:T(8,128)}), f32[4,24,1152]{2,1,0:T(8,128)S(1)}, u32[]{:S(2)}, u32[]{:S(2)}) %all-to-all-start.3) | async-done | bytes 442400 | tf_op jit(solution)/shard_map/all_to_all | solution.py:75
  137.9 31.1 %all_to_all.31 = bf16[16,8,4736]{2,1,0:T(8,128)(2,1)S(1)} all-to-all(bf16[16,8,4736]{2,1,0:T(8,128)(2,1)S(1)} %shard_map.136), channel_id=1, replica_groups=mesh['x'=4,'y'=4,'core'=2,'vocab'=4] {'x','y'}, dimensions={0} | all-to-all | bytes 2424832 | tf_op jit(solution)/shard_map/all_to_all | solution.py:75
  169.0 2.8 %collective-permute-start.13 = (bf16[128,4736]{1,0:T(8,128)(2,1)S(1)}, bf16[128,4736]{1,0:T(8,128)(2,1)S(1)}, u32[]{:S(2)}, u32[]{:S(2)}) collective-permute-start(bf16[128,4736]{1,0:T(8,128)(2,1)S(1)} %bitcast.23), channel_id=1, source_target_pairs={{0,4},{4,0},{1,5},{5,1},{2,6},{6,2},{3,7},{7,3},{8,12},{12,8},{9,1... | collective-permute-start | bytes 3637256 | tf_op jit(solution)/shard_map/ppermute | solution.py:520
  171.8 2.5 %collective-permute-done.13.s_ref = bf16[128,4736]{1,0:T(8,128)(2,1)S(1)} collective-permute-done((bf16[128,4736]{1,0:T(8,128)(2,1)S(1)}, bf16[128,4736]{1,0:T(8,128)(2,1)S(1)}, u32[]{:S(2)}, u32[]{:S(2)}) %collective-permute-start.13) | collective-permute-done | bytes 1212448 | tf_op jit(solution)/shard_map/ppermute | solution.py:520
  174.3 11.8 %shard_map.137 = (bf16[4,128,2560]{2,1,0:T(8,128)(2,1)S(1)}, bf16[4,128,2560]{2,1,0:T(8,128)(2,1)S(1)}) custom-call(s32[7]{0:T(128)S(1)} %stack.61.sc_ref, bf16[128,4736]{1,0:T(8,128)(2,1)S(1)} %bitcast.24, bf16[128,4736]{1,0:T(8,128)(2,1)S(1)} %collective-permute-done.13.s_ref, bf16[1024,4608]{1,0:T(8,128)(2,1)} %e_ref.1), custom_call_target="tpu_custom_call" | custom-call | tf_op jit(solution)/shard_map/pallas_call | solution.py:443
  186.6 4.5 %collective-permute-done.14 = bf16[4,128,2560]{2,1,0:T(8,128)(2,1)S(1)} collective-permute-done((bf16[4,128,2560]{2,1,0:T(8,128)(2,1)S(1)}, bf16[4,128,2560]{2,1,0:T(8,128)(2,1)S(1)}, u32[]{:S(2)}, u32[]{:S(2)}) %collective-permute-start.14) | collective-permute-done | bytes 2621472 | tf_op jit(solution)/shard_map/ppermute | solution.py:520
  191.1 2.2 add_convert_fusion
  193.3 4.9 %all-to-all-start.5 = ((bf16[64,8,2560]{2,1,0:T(8,128)(2,1)}), bf16[64,8,2560]{2,1,0:T(8,128)(2,1)S(1)}, u32[]{:S(2)}, u32[]{:S(2)}) async-start(bf16[64,8,2560]{2,1,0:T(8,128)(2,1)} %bitcast.34), calls=%async_computation.5 | async-start | bytes 5242880 | tf_op jit(solution)/shard_map/all_to_all | solution.py:75
  198.3 2.5 %add_convert_fusion.1 = bf16[256,1152]{1,0:T(8,128)(2,1)} fusion(f32[256,1152]{1,0:T(8,128)} %get-tuple-element.9, bf16[256,1152]{1,0:T(8,128)(2,1)} %param.14, f32[1152]{0:T(1024)S(1)} %copy-done.3, f32[256]{0:T(256)S(1)} %add_rsqrt_fusion), kind=kLoop, calls=%fused_computation.2 | loop fusion | flops 1474560 | bytes 2364928 | tf_op jit(solution)/shard_map/convert_element_type | solution.py:545
  202.6 29.7 %all-to-all-done.5.back_ref = bf16[64,8,2560]{2,1,0:T(8,128)(2,1)S(1)} async-done(((bf16[64,8,2560]{2,1,0:T(8,128)(2,1)}), bf16[64,8,2560]{2,1,0:T(8,128)(2,1)S(1)}, u32[]{:S(2)}, u32[]{:S(2)}) %all-to-all-start.5) | async-done | bytes 2621472 | tf_op jit(solution)/shard_map/all_to_all | solution.py:75
  (62 shorter events, 25.1 us)
Async XLA Ops:
  17.6 13.8 %collective-permute-start.4 = (bf16[2048,128]{1,0:T(8,128)(2,1)S(1)}, bf16[2048,128]{1,0:T(8,128)(2,1)S(1)}, u32[]{:S(2)}, u32[]{:S(2)}) collective-permute-start(bf16[2048,128]{1,0:T(8,128)(2,1)S(1)} %bitcast.29), channel_id=1, source_target_pairs={{0,8},{8,16},{16,24},{24,0},{1,9},{9,17},{17,25},{25,1},{2,10},{10... | collective-permute-start | bytes 1572872 | tf_op jit(solution)/shard_map/ppermute | solution.py:524
  18.9 20.3 %collective-permute-start.6 = (bf16[2048,128]{1,0:T(8,128)(2,1)S(1)}, bf16[2048,128]{1,0:T(8,128)(2,1)}, u32[]{:S(2)}, u32[]{:S(2)}) collective-permute-start(bf16[2048,128]{1,0:T(8,128)(2,1)S(1)} %bitcast.30), channel_id=1, source_target_pairs={{0,4},{4,0},{1,5},{5,1},{2,6},{6,2},{3,7},{7,3},{8,12},{12,8},{9,1... | collective-permute-start | bytes 1572872 | tf_op jit(solution)/shard_map/ppermute | solution.py:520
  20.3 22.3 %collective-permute-start = (bf16[2048,128]{1,0:T(8,128)(2,1)S(1)}, bf16[2048,128]{1,0:T(8,128)(2,1)S(1)}, u32[]{:S(2)}, u32[]{:S(2)}) collective-permute-start(bf16[2048,128]{1,0:T(8,128)(2,1)S(1)} %bitcast.31), channel_id=1, source_target_pairs={{0,24},{8,0},{16,8},{24,16},{1,25},{9,1},{17,9},{25,17},{2,26},{10... | collective-permute-start | bytes 1572872 | tf_op jit(solution)/shard_map/ppermute | solution.py:524
  21.6 22.1 %collective-permute-start.2 = (bf16[2048,128]{1,0:T(8,128)(2,1)S(1)}, bf16[2048,128]{1,0:T(8,128)(2,1)S(1)}, u32[]{:S(2)}, u32[]{:S(2)}) collective-permute-start(bf16[2048,128]{1,0:T(8,128)(2,1)S(1)} %bitcast.32), channel_id=1, source_target_pairs={{0,16},{8,24},{16,0},{24,8},{1,17},{9,25},{17,1},{25,9},{2,18},{10... | collective-permute-start | bytes 1572872 | tf_op jit(solution)/shard_map/ppermute | solution.py:524
  25.3 20.4 %all-to-all-start = ((bf16[8,256,128]{2,1,0:T(8,128)(2,1)}), bf16[8,256,128]{2,1,0:T(8,128)(2,1)S(1)}, u32[]{:S(2)}, u32[]{:S(2)}) async-start(bf16[8,256,128]{2,1,0:T(8,128)(2,1)} %shard_map.130), calls=%async_computation | async-start | bytes 1048576 | tf_op jit(solution)/shard_map/all_to_all | solution.py:75
  31.4 19.3 %collective-permute-start.5 = (bf16[2048,128]{1,0:T(8,128)(2,1)S(1)}, bf16[2048,128]{1,0:T(8,128)(2,1)}, u32[]{:S(2)}, u32[]{:S(2)}) collective-permute-start(bf16[2048,128]{1,0:T(8,128)(2,1)S(1)} %collective-permute-done.4.refs_0_), channel_id=1, source_target_pairs={{0,4},{4,0},{1,5},{5,1},{2,6},{6,2},{3,7},{7,3},{8,12},{12,8},{9,1... | collective-permute-start | bytes 1572872 | tf_op jit(solution)/shard_map/ppermute | solution.py:520
  37.5 33.3 %collective-permute-start.7 = (bf16[512,1152]{1,0:T(8,128)(2,1)}, bf16[512,1152]{1,0:T(8,128)(2,1)}, u32[]{:S(2)}, u32[]{:S(2)}) collective-permute-start(bf16[512,1152]{1,0:T(8,128)(2,1)} %get-tuple-element.17), channel_id=1, source_target_pairs={{0,1},{1,2},{2,3},{3,0},{4,5},{5,6},{6,7},{7,4},{8,9},{9,10},{10,1... | collective-permute-start | bytes 3538952 | tf_op jit(solution)/shard_map/ppermute | solution.py:530
  39.2 73.0 %collective-permute-start.8 = (bf16[512,1152]{1,0:T(8,128)(2,1)}, bf16[512,1152]{1,0:T(8,128)(2,1)}, u32[]{:S(2)}, u32[]{:S(2)}) collective-permute-start(bf16[512,1152]{1,0:T(8,128)(2,1)} %get-tuple-element.16), channel_id=1, source_target_pairs={{0,2},{1,3},{2,0},{3,1},{4,6},{5,7},{6,4},{7,5},{8,10},{9,11},{10,... | collective-permute-start | bytes 3538952 | tf_op jit(solution)/shard_map/ppermute | solution.py:530
  42.6 16.3 %collective-permute-start.1 = (bf16[2048,128]{1,0:T(8,128)(2,1)S(1)}, bf16[2048,128]{1,0:T(8,128)(2,1)}, u32[]{:S(2)}, u32[]{:S(2)}) collective-permute-start(bf16[2048,128]{1,0:T(8,128)(2,1)S(1)} %collective-permute-done.refs_0_), channel_id=1, source_target_pairs={{0,4},{4,0},{1,5},{5,1},{2,6},{6,2},{3,7},{7,3},{8,12},{12,8},{9,1... | collective-permute-start | bytes 1572872 | tf_op jit(solution)/shard_map/ppermute | solution.py:520
  43.8 15.1 %collective-permute-start.3 = (bf16[2048,128]{1,0:T(8,128)(2,1)S(1)}, bf16[2048,128]{1,0:T(8,128)(2,1)}, u32[]{:S(2)}, u32[]{:S(2)}) collective-permute-start(bf16[2048,128]{1,0:T(8,128)(2,1)S(1)} %collective-permute-done.2.refs_2_), channel_id=1, source_target_pairs={{0,4},{4,0},{1,5},{5,1},{2,6},{6,2},{3,7},{7,3},{8,12},{12,8},{9,1... | collective-permute-start | bytes 1572872 | tf_op jit(solution)/shard_map/ppermute | solution.py:520
  50.8 62.7 %collective-permute-start.9 = (bf16[512,1152]{1,0:T(8,128)(2,1)}, bf16[512,1152]{1,0:T(8,128)(2,1)}, u32[]{:S(2)}, u32[]{:S(2)}) collective-permute-start(bf16[512,1152]{1,0:T(8,128)(2,1)} %get-tuple-element.15), channel_id=1, source_target_pairs={{0,3},{1,0},{2,1},{3,2},{4,7},{5,4},{6,5},{7,6},{8,11},{9,8},{10,9... | collective-permute-start | bytes 3538952 | tf_op jit(solution)/shard_map/ppermute | solution.py:530
  66.6 46.9 %copy-start.5 = (s32[8]{0:T(128)S(1)}, s32[8]{0:T(128)}, u32[]{:S(2)}) copy-start(s32[8]{0:T(128)} %param.19) | copy-start | bytes 100
  66.6 47.2 %copy-start.2 = (s32[8]{0:T(128)S(1)}, s32[8]{0:T(128)}, u32[]{:S(2)}) copy-start(s32[8]{0:T(128)} %pick_ref.1) | copy-start | bytes 100
  66.6 51.4 %all-to-all-start.2 = ((bf16[32,256,128]{2,1,0:T(8,128)(2,1)}), bf16[32,256,128]{2,1,0:T(8,128)(2,1)S(1)}, u32[]{:S(2)}, u32[]{:S(2)}) async-start(bf16[32,256,128]{2,1,0:T(8,128)(2,1)} %bitcast.35), calls=%async_computation.2 | async-start | bytes 4194304 | tf_op jit(solution)/shard_map/all_to_all | solution.py:75
  70.8 45.5 %collective-permute-start.10 = (bf16[512,1152]{1,0:T(8,128)(2,1)}, bf16[512,1152]{1,0:T(8,128)(2,1)}, u32[]{:S(2)}, u32[]{:S(2)}) collective-permute-start(bf16[512,1152]{1,0:T(8,128)(2,1)} %collective-permute-done.7.a1), channel_id=1, source_target_pairs={{0,4},{4,0},{1,5},{5,1},{2,6},{6,2},{3,7},{7,3},{8,12},{12,8},{9,1... | collective-permute-start | bytes 3538952 | tf_op jit(solution)/shard_map/ppermute | solution.py:520
  112.2 4.1 %collective-permute-start.11 = (bf16[512,1152]{1,0:T(8,128)(2,1)}, bf16[512,1152]{1,0:T(8,128)(2,1)}, u32[]{:S(2)}, u32[]{:S(2)}) collective-permute-start(bf16[512,1152]{1,0:T(8,128)(2,1)} %collective-permute-done.8.a2), channel_id=1, source_target_pairs={{0,4},{4,0},{1,5},{5,1},{2,6},{6,2},{3,7},{7,3},{8,12},{12,8},{9,1... | collective-permute-start | bytes 3538952 | tf_op jit(solution)/shard_map/ppermute | solution.py:520
  113.5 4.5 %collective-permute-start.12 = (bf16[512,1152]{1,0:T(8,128)(2,1)}, bf16[512,1152]{1,0:T(8,128)(2,1)}, u32[]{:S(2)}, u32[]{:S(2)}) collective-permute-start(bf16[512,1152]{1,0:T(8,128)(2,1)} %collective-permute-done.9.a3), channel_id=1, source_target_pairs={{0,4},{4,0},{1,5},{5,1},{2,6},{6,2},{3,7},{7,3},{8,12},{12,8},{9,1... | collective-permute-start | bytes 3538952 | tf_op jit(solution)/shard_map/ppermute | solution.py:520
  116.2 13.0 %copy-start.6 = (s32[8]{0:T(128)S(1)}, s32[8]{0:T(128)}, u32[]{:S(2)}) copy-start(s32[8]{0:T(128)} %param.20) | copy-start | bytes 100
  125.8 11.8 %all-to-all-start.3 = ((f32[4,24,1152]{2,1,0:T(8,128)}), f32[4,24,1152]{2,1,0:T(8,128)S(1)}, u32[]{:S(2)}, u32[]{:S(2)}) async-start(f32[4,24,1152]{2,1,0:T(8,128)} %get-tuple-element.10), calls=%async_computation.3 | async-start | bytes 884736 | tf_op jit(solution)/shard_map/all_to_all | solution.py:75
  169.0 17.1 %copy-start = (bf16[16,8,4736]{2,1,0:T(8,128)(2,1)}, bf16[16,8,4736]{2,1,0:T(8,128)(2,1)S(1)}, u32[]{:S(2)}) copy-start(bf16[16,8,4736]{2,1,0:T(8,128)(2,1)S(1)} %all_to_all.31) | copy-start | bytes 3637252
  169.0 5.3 %collective-permute-start.13 = (bf16[128,4736]{1,0:T(8,128)(2,1)S(1)}, bf16[128,4736]{1,0:T(8,128)(2,1)S(1)}, u32[]{:S(2)}, u32[]{:S(2)}) collective-permute-start(bf16[128,4736]{1,0:T(8,128)(2,1)S(1)} %bitcast.23), channel_id=1, source_target_pairs={{0,4},{4,0},{1,5},{5,1},{2,6},{6,2},{3,7},{7,3},{8,12},{12,8},{9,1... | collective-permute-start | bytes 3637256 | tf_op jit(solution)/shard_map/ppermute | solution.py:520
  174.3 11.9 %copy-start.1 = (bf16[128,4736]{1,0:T(8,128)(2,1)}, bf16[128,4736]{1,0:T(8,128)(2,1)S(1)}, u32[]{:S(2)}) copy-start(bf16[128,4736]{1,0:T(8,128)(2,1)S(1)} %collective-permute-done.13.s_ref) | copy-start | bytes 3637252
  186.1 5.0 %collective-permute-start.14 = (bf16[4,128,2560]{2,1,0:T(8,128)(2,1)S(1)}, bf16[4,128,2560]{2,1,0:T(8,128)(2,1)S(1)}, u32[]{:S(2)}, u32[]{:S(2)}) collective-permute-start(bf16[4,128,2560]{2,1,0:T(8,128)(2,1)S(1)} %get-tuple-element.12), channel_id=1, source_target_pairs={{0,4},{4,0},{1,5},{5,1},{2,6},{6,2},{3,7},{7,3},{8,12},{12,8},{9,1... | collective-permute-start | bytes 7864328 | tf_op jit(solution)/shard_map/ppermute | solution.py:520
  193.3 39.0 %all-to-all-start.5 = ((bf16[64,8,2560]{2,1,0:T(8,128)(2,1)}), bf16[64,8,2560]{2,1,0:T(8,128)(2,1)S(1)}, u32[]{:S(2)}, u32[]{:S(2)}) async-start(bf16[64,8,2560]{2,1,0:T(8,128)(2,1)} %bitcast.34), calls=%async_computation.5 | async-start | bytes 5242880 | tf_op jit(solution)/shard_map/all_to_all | solution.py:75
  (2 other events, 8.4 us)
